TPU v7x, 32 devices: a whole 2x2x4 slice. The times are simulated.
32 devices in a mesh: tp: 8 (over z, y), dp: 4 (over x, core).
Axes of the slice: x: 2, y: 2, z: 4, core: 2. Of those that a mesh axis runs over, the one named last changes fastest.
Arguments:
- tokens: bfloat16 [4, 16, 4096], P('dp', 'tp'), may hold values from -6 to 6
- gate_weight: bfloat16 [4096, 16384], P('dp', 'tp'), may hold values from -0.09375 to 0.09375
- up_weight: bfloat16 [4096, 16384], P('dp', 'tp'), may hold values from -0.09375 to 0.09375
- cotangent: bfloat16 [4, 16, 16384], P('dp', None, 'tp'), may hold values from -6 to 6
Outputs:
- hidden: bfloat16 [4, 16, 16384], P('dp', None, 'tp')
- grad_tokens: bfloat16 [4, 16, 4096], P('dp', 'tp')
- grad_gate: bfloat16 [4096, 16384], P(None, 'tp')
- grad_up: bfloat16 [4096, 16384], P(None, 'tp')
All inputs are finite; a program needn't handle non-finite values.
Results may differ from a plain program's by a relative error of at most 0.009.
Values may be sent and summed in bfloat16 or wider, within the bound.
No kernel may reach another device: no remote copies, remote signals or barrier semaphores. Data moves between devices by JAX's collectives and lax.ppermute only.
A program may use at most 320 MiB of HBM per device.

v0:
```python
import jax
import jax.numpy as jnp
from jax import lax
from jax.sharding import PartitionSpec as P


def swish_parts(gate_pre):
    sigmoid_val = jax.nn.sigmoid(gate_pre)
    return (gate_pre * sigmoid_val, sigmoid_val * (1.0 + gate_pre * (1.0 - sigmoid_val)))


def shards(tokens, gate_weight, up_weight, cotangent):
    gate_full, up_full = (
        lax.all_gather(gate_weight, "dp", axis=0, tiled=True),
        lax.all_gather(up_weight, "dp", axis=0, tiled=True),
    )
    gathered = lax.all_gather(tokens, "tp", axis=1, tiled=True)
    flat_rows = gathered[0]
    gate_pre = jnp.dot(flat_rows, gate_full, preferred_element_type=jnp.float32)
    up_pre = jnp.dot(flat_rows, up_full, preferred_element_type=jnp.float32)
    swish_act, swish_slope = swish_parts(gate_pre)
    hidden = (swish_act * up_pre).astype(jnp.bfloat16)
    back_float = cotangent[0].astype(jnp.float32)
    d_gate = (back_float * up_pre * swish_slope).astype(jnp.bfloat16)
    d_up = (back_float * swish_act).astype(jnp.bfloat16)
    across = (((1,), (1,)), ((), ()))
    down_rows = (((0,), (0,)), ((), ()))
    result = lax.dot_general(d_gate, gate_full, across, preferred_element_type=jnp.float32)
    grad_rows = lax.psum_scatter(
        result + lax.dot_general(d_up, up_full, across, preferred_element_type=jnp.float32),
        "tp",
        scatter_dimension=0,
        tiled=True,
    )
    grad_tokens = grad_rows.astype(jnp.bfloat16)[None]
    inverse_dp = 1.0 / lax.axis_size("dp")
    rows_p = lax.all_gather(gathered, "dp", axis=0, tiled=True)
    gate_p = lax.all_gather(d_gate[None], "dp", axis=0, tiled=True)
    up_p = lax.all_gather(d_up[None], "dp", axis=0, tiled=True)
    acc_gate = jnp.zeros(gate_full.shape, jnp.float32)
    acc_up = jnp.zeros(up_full.shape, jnp.float32)
    for replica in range(rows_p.shape[0]):
        term_gate = lax.dot_general(
            rows_p[replica], gate_p[replica], down_rows, preferred_element_type=jnp.float32
        )
        term_up = lax.dot_general(
            rows_p[replica], up_p[replica], down_rows, preferred_element_type=jnp.float32
        )
        acc_gate = acc_gate + lax.optimization_barrier(term_gate.astype(jnp.bfloat16)).astype(
            jnp.float32
        )
        acc_up = acc_up + lax.optimization_barrier(term_up.astype(jnp.bfloat16)).astype(jnp.float32)
    grad_gate = (acc_gate * inverse_dp).astype(jnp.bfloat16)
    grad_up = (acc_up * inverse_dp).astype(jnp.bfloat16)
    return (hidden[None], grad_tokens, grad_gate, grad_up)


def solution(mesh):
    in_specs = (P("dp", "tp", None), P("dp", "tp"), P("dp", "tp"), P("dp", None, "tp"))
    out_specs = (P("dp", None, "tp"), P("dp", "tp", None), P(None, "tp"), P(None, "tp"))
    return jax.shard_map(shards, mesh=mesh, in_specs=in_specs, out_specs=out_specs, check_vma=False)
```

profile of v0, /device:TPU:0, one launch (start us, length us, event | category | flops | bytes accessed | tf_op | source)
XLA Modules:
  0.0 485.2 jit_solution(3672661935274794439)
XLA Ops:
  7.2 0.0 copy-start
  7.2 0.0 all-gather.7.cloned.1.call-start
  7.2 0.7 all-gather.7.cloned.1.call-update
  7.9 0.0 all-gather.5.cloned.1.call-start
  8.0 0.7 all-gather.5.cloned.1.call-update
  8.7 0.7 copy.14
  9.4 32.6 %all_gather.18 = bf16[1,16,4096]{2,0,1:T(2,128)(2,1)S(1)} all-gather(bf16[1,2,4096]{2,0,1:T(2,128)(2,1)S(1)} %copy.14), channel_id=1, replica_groups=mesh['tp'=8,'dp'=4] {'tp'}, dimensions={1}, use_global_device_ids=true | all-gather | bytes 147456 | tf_op jit(solution)/shard_map/all_gather | solution.py:17
  42.0 0.1 copy.18
  42.1 1.2 dynamic-slice
  44.0 10.5 %all_gather.22 = bf16[4,16,4096]{2,1,0:T(8,128)(2,1)S(1)} all-gather(bf16[1,16,4096]{2,1,0:T(8,128)(2,1)S(1)} %copy.18), channel_id=1, replica_groups=mesh['tp'=8,'dp'=4] {'dp'}, dimensions={0}, use_global_device_ids=true | all-gather | bytes 655360 | tf_op jit(solution)/shard_map/all_gather | solution.py:37
  54.5 66.5 %all-gather.7.cloned.1.call-done = bf16[4096,2048]{1,0:T(8,128)(2,1)} async-done(((bf16[1024,2048]{1,0:T(8,128)(2,1)}), bf16[4096,2048]{1,0:T(8,128)(2,1)}) %all-gather.7.cloned.1.call-update) | async-done | bytes 16777232 | tf_op jit(solution)/shard_map/all_gather | solution.py:15
  121.0 8.0 %fusion.3 = f32[16,2048]{1,0:T(8,128)S(1)} fusion(bf16[4096,2048]{1,0:T(8,128)(2,1)} %all-gather.7.cloned.1.call-done, bf16[1,16,4096]{2,1,0:T(8,128)(2,1)S(1)} %copy.18), kind=kOutput, calls=%fused_computation.20 | convolution fusion | flops 268435456 | bytes 17039360 | tf_op jit(solution)/shard_map/dot_general | solution.py:20
  129.0 99.4 %all-gather.5.cloned.1.call-done = bf16[4096,2048]{1,0:T(8,128)(2,1)} async-done(((bf16[1024,2048]{1,0:T(8,128)(2,1)}), bf16[4096,2048]{1,0:T(8,128)(2,1)}) %all-gather.5.cloned.1.call-update) | async-done | bytes 16777232 | tf_op jit(solution)/shard_map/all_gather | solution.py:14
  228.5 8.7 %fusion.1 = (bf16[16,2048]{1,0:T(8,128)(2,1)S(1)}, bf16[1,16,2048]{2,1,0:T(8,128)(2,1)}, bf16[16,2048]{1,0:T(8,128)(2,1)S(1)}) fusion(f32[16,2048]{1,0:T(8,128)S(1)} %fusion.3, bf16[1,16,2048]{2,1,0:T(8,128)(2,1)S(1)} %copy-done, bf16[4096,2048]{1,0:T(8,128)(2,1)} %all-gather.5.cloned.1.call-done, bf16[1,16,4096]{2,1,0:T(8,128)(2,1)S(1)} %copy.18), kind=kOutput, calls=%fused_computation.14 | convolution fusion | flops 268959744 | bytes 17301504 | tf_op jit(solution)/shard_map/dot_general | solution.py:19
  237.2 5.9 %all-gather.1 = bf16[64,2048]{1,0:T(8,128)(2,1)S(1)} all-gather(bf16[16,2048]{1,0:T(8,128)(2,1)S(1)} %get-tuple-element.18), channel_id=3, replica_groups=mesh['tp'=8,'dp'=4] {'dp'}, dimensions={0}, use_global_device_ids=true | all-gather | bytes 327680 | tf_op jit(solution)/shard_map/all_gather | solution.py:39
  243.1 8.5 %convert_bitcast_fusion = bf16[4096,2048]{0,1:T(8,128)(2,1)} fusion(bf16[4,16,4096]{2,1,0:T(8,128)(2,1)S(1)} %all_gather.22, bf16[64,2048]{1,0:T(8,128)(2,1)S(1)} %all-gather.1), kind=kOutput, calls=%fused_computation.2 | convolution fusion | flops 276824064 | bytes 16973824 | tf_op jit(solution)/shard_map/dot_general | solution.py:46
  251.7 8.1 %convert_bitcast_fusion.1 = bf16[4096,2048]{0,1:T(8,128)(2,1)} fusion(bf16[4,16,4096]{2,1,0:T(8,128)(2,1)S(1)} %all_gather.22, bf16[64,2048]{1,0:T(8,128)(2,1)S(1)} %all-gather.1), kind=kOutput, calls=%fused_computation.3 | convolution fusion | flops 276824064 | bytes 16973824 | tf_op jit(solution)/shard_map/dot_general | solution.py:46
  259.7 8.0 %convert_bitcast_fusion.2 = bf16[4096,2048]{0,1:T(8,128)(2,1)} fusion(bf16[4,16,4096]{2,1,0:T(8,128)(2,1)S(1)} %all_gather.22, bf16[64,2048]{1,0:T(8,128)(2,1)S(1)} %all-gather.1), kind=kOutput, calls=%fused_computation.4 | convolution fusion | flops 276824064 | bytes 16973824 | tf_op jit(solution)/shard_map/dot_general | solution.py:46
  267.8 8.0 %convert_bitcast_fusion.3 = bf16[4096,2048]{0,1:T(8,128)(2,1)} fusion(bf16[4,16,4096]{2,1,0:T(8,128)(2,1)S(1)} %all_gather.22, bf16[64,2048]{1,0:T(8,128)(2,1)S(1)} %all-gather.1), kind=kOutput, calls=%fused_computation.5 | convolution fusion | flops 276824064 | bytes 16973824 | tf_op jit(solution)/shard_map/dot_general | solution.py:46
  275.8 6.0 %all-gather = bf16[64,2048]{1,0:T(8,128)(2,1)S(1)} all-gather(bf16[16,2048]{1,0:T(8,128)(2,1)S(1)} %get-tuple-element.16), channel_id=2, replica_groups=mesh['tp'=8,'dp'=4] {'dp'}, dimensions={0}, use_global_device_ids=true | all-gather | bytes 327680 | tf_op jit(solution)/shard_map/all_gather | solution.py:38
  281.9 8.5 %convert_bitcast_fusion.4 = bf16[4096,2048]{0,1:T(8,128)(2,1)} fusion(bf16[4,16,4096]{2,1,0:T(8,128)(2,1)S(1)} %all_gather.22, bf16[64,2048]{1,0:T(8,128)(2,1)S(1)} %all-gather), kind=kOutput, calls=%fused_computation.6 | convolution fusion | flops 276824064 | bytes 16973824 | tf_op jit(solution)/shard_map/dot_general | solution.py:43
  290.4 8.1 %convert_bitcast_fusion.5 = bf16[4096,2048]{0,1:T(8,128)(2,1)} fusion(bf16[4,16,4096]{2,1,0:T(8,128)(2,1)S(1)} %all_gather.22, bf16[64,2048]{1,0:T(8,128)(2,1)S(1)} %all-gather), kind=kOutput, calls=%fused_computation.7 | convolution fusion | flops 276824064 | bytes 16973824 | tf_op jit(solution)/shard_map/dot_general | solution.py:43
  298.5 8.1 %convert_bitcast_fusion.6 = bf16[4096,2048]{0,1:T(8,128)(2,1)} fusion(bf16[4,16,4096]{2,1,0:T(8,128)(2,1)S(1)} %all_gather.22, bf16[64,2048]{1,0:T(8,128)(2,1)S(1)} %all-gather), kind=kOutput, calls=%fused_computation.8 | convolution fusion | flops 276824064 | bytes 16973824 | tf_op jit(solution)/shard_map/dot_general | solution.py:43
  306.5 8.1 %convert_bitcast_fusion.7 = bf16[4096,2048]{0,1:T(8,128)(2,1)} fusion(bf16[4,16,4096]{2,1,0:T(8,128)(2,1)S(1)} %all_gather.22, bf16[64,2048]{1,0:T(8,128)(2,1)S(1)} %all-gather), kind=kOutput, calls=%fused_computation.9 | convolution fusion | flops 276824064 | bytes 16973824 | tf_op jit(solution)/shard_map/dot_general | solution.py:43
  314.6 10.2 %fusion.20 = f32[16,4096]{1,0:T(8,128)S(1)} fusion(bf16[16,2048]{1,0:T(8,128)(2,1)S(1)} %get-tuple-element.16, bf16[4096,2048]{1,0:T(8,128)(2,1)} %all-gather.5.cloned.1.call-done), kind=kOutput, calls=%fused_computation.38 | convolution fusion | flops 268435456 | bytes 17104896 | tf_op jit(solution)/shard_map/dot_general | solution.py:28
  324.8 10.2 %convolution_add_fusion = f32[16,4096]{1,0:T(8,128)S(1)} fusion(f32[16,4096]{1,0:T(8,128)S(1)} %fusion.20, bf16[16,2048]{1,0:T(8,128)(2,1)S(1)} %get-tuple-element.18, bf16[4096,2048]{1,0:T(8,128)(2,1)} %all-gather.7.cloned.1.call-done), kind=kOutput, calls=%fused_computation.10 | convolution fusion | flops 268500992 | bytes 17367040 | tf_op jit(solution)/shard_map/dot_general | solution.py:30
  335.0 40.4 %all-reduce.2 = bf16[16,4096]{1,0:T(8,128)(2,1)S(1)} all-reduce(f32[16,4096]{1,0:T(8,128)S(1)} %convolution_add_fusion), channel_id=4, replica_groups=mesh['tp'=8,'dp'=4] {'tp'}, use_global_device_ids=true, to_apply=%region_0.0.clone | all-reduce | flops 65536 | bytes 393216
  375.4 28.7 %multiply_convert_fusion = bf16[4096,2048]{0,1:T(8,128)(2,1)} fusion(bf16[4096,2048]{0,1:T(8,128)(2,1)} %convert_bitcast_fusion, bf16[4096,2048]{0,1:T(8,128)(2,1)} %convert_bitcast_fusion.1, bf16[4096,2048]{0,1:T(8,128)(2,1)} %convert_bitcast_fusion.2, bf16[4096,2048]{0,1:T(8,128)(2,1)} %convert_bitcast_fusion.3), kind=kLoop, calls=%fused_computation | loop fusion | flops 75497472 | bytes 83886080 | tf_op jit(solution)/shard_map/convert_element_type | solution.py:54
  404.2 22.4 %copy.17 = bf16[4096,2048]{1,0:T(8,128)(2,1)} copy(bf16[4096,2048]{0,1:T(8,128)(2,1)} %multiply_convert_fusion) | data formatting | bytes 33554432
  426.6 28.8 %multiply_convert_fusion.1 = bf16[4096,2048]{0,1:T(8,128)(2,1)} fusion(bf16[4096,2048]{0,1:T(8,128)(2,1)} %convert_bitcast_fusion.4, bf16[4096,2048]{0,1:T(8,128)(2,1)} %convert_bitcast_fusion.5, bf16[4096,2048]{0,1:T(8,128)(2,1)} %convert_bitcast_fusion.6, bf16[4096,2048]{0,1:T(8,128)(2,1)} %convert_bitcast_fusion.7), kind=kLoop, calls=%fused_computation.1 | loop fusion | flops 75497472 | bytes 83886080 | tf_op jit(solution)/shard_map/convert_element_type | solution.py:53
  455.3 22.4 %copy.16 = bf16[4096,2048]{1,0:T(8,128)(2,1)} copy(bf16[4096,2048]{0,1:T(8,128)(2,1)} %multiply_convert_fusion.1) | data formatting | bytes 33554432
  477.8 0.6 fusion.17
  (1 shorter events, 0.0 us)
Async XLA Ops:
  7.2 221.3 %copy-start = (bf16[1,16,2048]{2,1,0:T(8,128)(2,1)S(1)}, bf16[1,16,2048]{2,1,0:T(8,128)(2,1)}, u32[]{:S(2)}) copy-start(bf16[1,16,2048]{2,1,0:T(8,128)(2,1)} %param.7) | copy-start | bytes 196612
  7.2 113.8 %all-gather.7.cloned.1.call-start = ((), (), s32[]{:S(2)}) async-start(), calls=%async_computation.1 | async-start | bytes 20971520 | tf_op jit(solution)/shard_map/all_gather | solution.py:15
  7.9 220.6 %all-gather.5.cloned.1.call-start = ((), (), s32[]{:S(2)}) async-start(), calls=%async_computation | async-start | bytes 20971520 | tf_op jit(solution)/shard_map/all_gather | solution.py:14
Sparse Core Ops, SparseCore 0:
  9.5 111.4 all-gather.6
  122.6 105.8 all-gather.4
where the time goes:
time: 487 us; the launch traced here: 485 us
  waiting for transfers between devices  167 us (34%)
  matrix products  103 us (21%)
  blocking collectives  95.5 us (20%)
  other arithmetic  57.5 us (12%)
  local copies, waits for them, and re-layouts  47.6 us (10%)
  between operations  14.7 us (3%)
    all_gather x1, waiting for transfers between devices, shards(): lax.all_gather(gate_weight, 'dp', axis=0, tiled=True)  99.4 us
    all_gather x1, waiting for transfers between devices, shards(): lax.all_gather(up_weight, 'dp', axis=0, tiled=True)  66.5 us
    unnamed x7, local copies, waits for them, and re-layouts  47 us
    unnamed x1, blocking collectives  40.4 us
    dot_general x4, matrix products, shards(): lax.dot_general(rows_p[replica], gate_p[replica], down_rows, preferred_el...  32.7 us
    dot_general x4, matrix products, shards(): lax.dot_general(rows_p[replica], up_p[replica], down_rows, preferred_elem...  32.7 us
    all_gather x1, blocking collectives, shards(): gathered = lax.all_gather(tokens, 'tp', axis=1, tiled=True)  32.6 us
    convert_element_type x1, other arithmetic, shards(): grad_gate = (acc_gate * inverse_dp).astype(jnp.bfloat16)  28.8 us
  transfers between devices with their start and end apart: 2, of which 2 were waited for; matrix products, arithmetic and copies ran while one was open for 2% of the time, Pallas kernels for 0%

commit v1 on v0

v1 whole, which is shorter than its diff:
```python
import jax
import jax.numpy as jnp
from jax import lax
from jax.sharding import PartitionSpec as P

F32 = jnp.float32
BF16 = jnp.bfloat16


def swap(value, axis, bit):
    return lax.ppermute(value, axis, [(i, i ^ bit) for i in range(lax.axis_size(axis))])


def bits_of(size):
    assert size & (size - 1) == 0
    return [1 << k for k in reversed(range(size.bit_length() - 1))]


def swish_parts(gate_pre):
    s = jax.nn.sigmoid(gate_pre)
    return gate_pre * s, s * (1.0 + gate_pre * (1.0 - s))


def shards(tokens, gate_weight, up_weight, cotangent):
    n_tp, n_dp = lax.axis_size("tp"), lax.axis_size("dp")
    assert n_dp == 4
    t, r = lax.axis_index("tp"), lax.axis_index("dp")
    _, rt, d_model = tokens.shape
    depth, width = gate_weight.shape
    rows = rt * n_tp
    rel = [0]
    for bit in bits_of(n_tp):
        rel = rel + [v ^ bit for v in rel]
    rel = jnp.array(rel)

    own = tokens[0].reshape(rt, n_dp, depth)
    own = jnp.take(own, r ^ jnp.arange(n_dp), axis=1).transpose(1, 0, 2).reshape(2, 2, rt, depth)
    part = jnp.stack([own[0], swap(own[1], "dp", 2)], axis=1)
    part = jnp.stack([part[0], swap(part[1], "dp", 1)])
    part = part[:, :, None]
    for bit in bits_of(n_tp):
        part = jnp.concatenate([part, swap(part, "tp", bit)], axis=2)
    feats = part.reshape(4 * rows, depth)

    cot = cotangent[0].reshape(n_tp, rt, width)
    cot = jnp.take(cot, t ^ rel, axis=0).reshape(rows, width)
    cot = jnp.concatenate([cot, swap(cot, "dp", 2)])

    def across(v):
        return v.reshape((-1, 2) + v.shape[1:])[:, ::-1].reshape(v.shape)

    def pre(weight):
        out = jnp.dot(feats, weight, preferred_element_type=F32)
        half = (out[: 2 * rows] + swap(out[2 * rows :], "dp", 1)).astype(BF16)
        other = swap(half, "dp", 2)
        other = jnp.concatenate([other[rows:], other[:rows]])
        return half.astype(F32) + other.astype(F32)

    gate_pre, up_pre = pre(gate_weight), pre(up_weight)
    act, slope = swish_parts(gate_pre)
    hidden = (act * up_pre)[:rows].astype(BF16).reshape(n_tp, rt, width)
    place = jnp.argsort(rel)
    hidden = jnp.take(hidden, place[t ^ jnp.arange(n_tp)], axis=0).reshape(1, rows, width)
    back = cot.astype(F32)
    d_gate = (back * up_pre * slope).astype(BF16)
    d_up = (back * act).astype(BF16)
    d_gate = jnp.concatenate([d_gate, swap(d_gate, "dp", 1)])
    d_up = jnp.concatenate([d_up, swap(d_up, "dp", 1)])

    feats4 = feats.reshape(2, 2, rows, depth)
    feats4 = jnp.stack([feats4, swap(feats4, "dp", 2)[:, ::-1]])
    feats4 = jnp.stack([feats4, swap(feats4, "dp", 1)[:, ::-1]])
    feats4 = feats4.transpose(1, 0, 2, 3, 4, 5).reshape(n_dp, 4 * rows, depth)
    whole = jnp.take(feats4, r ^ jnp.arange(n_dp), axis=0).transpose(1, 0, 2).reshape(4 * rows, d_model)

    cols = (((1,), (1,)), ((), ()))
    total = lax.dot_general(d_gate, gate_weight, cols, preferred_element_type=F32)
    total = total + lax.dot_general(d_up, up_weight, cols, preferred_element_type=F32)
    total = total.reshape(2, 2, n_tp, rt, depth)
    for bit in reversed(bits_of(n_tp)):
        mid = total.shape[2] // 2
        total = total[:, :, :mid] + swap(total[:, :, mid:], "tp", bit)
    total = total[:, :, 0]
    total = jnp.stack([total[:, 0], swap(total[:, 1], "dp", 2)], axis=1)
    total = jnp.stack([total[0], swap(total[1], "dp", 1)])
    total = total.transpose(1, 0, 2, 3).reshape(n_dp, rt, depth)
    total = jnp.take(total, r ^ jnp.arange(n_dp), axis=0).transpose(1, 0, 2)
    grad_tokens = total.reshape(1, rt, d_model).astype(BF16)

    down = (((0,), (0,)), ((), ()))
    inverse = 1.0 / n_dp
    grad_gate = (lax.dot_general(whole, d_gate, down, preferred_element_type=F32) * inverse).astype(BF16)
    grad_up = (lax.dot_general(whole, d_up, down, preferred_element_type=F32) * inverse).astype(BF16)
    return hidden, grad_tokens, grad_gate, grad_up


def solution(mesh):
    in_specs = (P("dp", "tp", None), P("dp", "tp"), P("dp", "tp"), P("dp", None, "tp"))
    out_specs = (P("dp", None, "tp"), P("dp", "tp", None), P(None, "tp"), P(None, "tp"))
    return jax.shard_map(shards, mesh=mesh, in_specs=in_specs, out_specs=out_specs, check_vma=False)
```

time: 487 us -> 81.3 us (0.17)
  waiting for transfers between devices: 167 us -> 18.8 us
  blocking collectives: 95.5 us -> 0 us
  matrix products: 103 us -> 26.1 us
  other arithmetic: 57.5 us -> 4.2 us
  local copies, waits for them, and re-layouts: 47.6 us -> 8.41 us
  starting transfers between devices: 0.08 us -> 22.4 us
  between operations: 14.7 us -> 1.07 us
    all_gather x2 -> x0, waiting for transfers between devices: 166 us -> none  [the longest x1 99.4 us: shards(): lax.all_gather(gate_weight, 'dp', axis=0, tiled=True)]
    dot_general x12 -> x6, matrix products: 103 us -> 26.1 us  [the longest x1 8.55 us: shards(): lax.dot_general(whole, d_up, down, preferred_element_type=F32) * inverse]
    convert_element_type x2 -> x4, other arithmetic: 57.5 us -> 0.93 us  [the longest x1 0.69 us: shards(): grad_tokens = total.reshape(1, rt, d_model).astype(BF16)]
    all_gather x4 -> x0, blocking collectives: 55.1 us -> none  [the longest x1 32.6 us: shards(): gathered = lax.all_gather(tokens, 'tp', axis=1, tiled=True)]
    unnamed x7, local copies, waits for them, and re-layouts: 47 us -> 0.69 us
    unnamed x1 -> x0, blocking collectives: 40.4 us -> none
    ppermute x0 -> x19, starting transfers between devices: none -> 22.4 us  [swap(): lax.ppermute(value, axis, [(i, i ^ bit) for i in range(lax.axis_size(axis...]
    ppermute x0 -> x19, waiting for transfers between devices: none -> 18.8 us  [swap(): lax.ppermute(value, axis, [(i, i ^ bit) for i in range(lax.axis_size(axis...]
  transfers between devices with their start and end apart: 2 -> 19, of which waited for: 2 -> 8; matrix products, arithmetic and copies ran while one was open for 2% -> 44% of each run, Pallas kernels for 0% -> 0%
where the time goes in v1:
time: 81.3 us; the launch traced here: 81 us
  matrix products  26.1 us (32%)
  starting transfers between devices  22.4 us (28%)
  waiting for transfers between devices  18.8 us (23%)
  local copies, waits for them, and re-layouts  8.41 us (10%)
  other arithmetic  4.2 us (5%)
  between operations  1.07 us (1%)
    ppermute x19, starting transfers between devices, swap(): lax.ppermute(value, axis, [(i, i ^ bit) for i in range(lax.axis_size(axis...  22.4 us
    ppermute x19, waiting for transfers between devices, swap(): lax.ppermute(value, axis, [(i, i ^ bit) for i in range(lax.axis_size(axis...  18.8 us
    dot_general x1, matrix products, shards(): lax.dot_general(whole, d_up, down, preferred_element_type=F32) * inverse  8.55 us
    dot_general x1, matrix products, shards(): lax.dot_general(whole, d_gate, down, preferred_element_type=F32) * inverse  8.53 us
    dot_general x2, matrix products, pre(): out = jnp.dot(feats, weight, preferred_element_type=F32)  3.86 us
    dot_general x1, matrix products, shards(): lax.dot_general(d_up, up_weight, cols, preferred_element_type=F32)  3.73 us
  transfers between devices with their start and end apart: 19, of which 8 were waited for; matrix products, arithmetic and copies ran while one was open for 44% of the time, Pallas kernels for 0%

profile of v1, /device:TPU:0, one launch (start us, length us, event | category | flops | bytes accessed | tf_op | source)
XLA Modules:
  0.0 81.0 jit_solution(11063471344165335839)
XLA Ops:
  2.1 3.0 %collective-permute-start = (bf16[2,2,1024]{2,1,0:T(2,128)(2,1)S(1)}, bf16[2,2,1024]{2,1,0:T(2,128)(2,1)S(1)}, u32[]{:S(2)}, u32[]{:S(2)}) collective-permute-start(bf16[2,2,1024]{2,1,0:T(2,128)(2,1)S(1)} %get-tuple-element.25), channel_id=1, source_target_pairs={{0,2},{1,3},{2,0},{3,1},{4,6},{5,7},{6,4},{7,5},{8,10},{9,11},{10,... | collective-permute-start | bytes 24584 | tf_op jit(solution)/shard_map/ppermute | solution.py:11
  5.1 0.7 compare_and_fusion
  5.8 0.9 %reshape_squeeze.7 = bf16[8,2,2048]{2,1,0:T(2,128)(2,1)S(1)} reshape(bf16[1,16,2048]{2,1,0:T(8,128)(2,1)} %param.10) | data formatting | bytes 131072 | tf_op jit(solution)/shard_map/reshape;squeeze | solution.py:45
  6.7 0.7 gather_fusion.5
  7.7 1.3 %gather_fusion.1 = s32[8]{0:T(128)S(1)} fusion(s32[8]{0:T(128)} %constant.69.clone, s32[1024]{0:T(1024)S(1)} %pad_clamp_fusion.3), kind=kCustom, calls=%fused_computation.3 | custom fusion | bytes 96 | tf_op jit(solution)/shard_map/gather | solution.py:63
  9.1 3.2 %collective-permute-start.2 = (bf16[2,2,1,2,1024]{4,3,0,1,2:T(2,128)(2,1)S(1)}, bf16[2,2,1,2,1024]{4,3,0,1,2:T(2,128)(2,1)S(1)}, u32[]{:S(2)}, u32[]{:S(2)}) collective-permute-start(bf16[2,2,1,2,1024]{4,3,0,1,2:T(2,128)(2,1)S(1)} %maximum_bitcast_fusion.1), channel_id=1, source_target_pairs={{0,16},{4,20},{8,24},{12,28},{16,0},{20,4},{24,8},{28,12},{1,17},{... | collective-permute-start | bytes 49160 | tf_op jit(solution)/shard_map/ppermute | solution.py:11
  12.2 1.7 %collective-permute-done.2 = bf16[2,2,1,2,1024]{4,3,0,1,2:T(2,128)(2,1)S(1)} collective-permute-done((bf16[2,2,1,2,1024]{4,3,0,1,2:T(2,128)(2,1)S(1)}, bf16[2,2,1,2,1024]{4,3,0,1,2:T(2,128)(2,1)S(1)}, u32[]{:S(2)}, u32[]{:S(2)}) %collective-permute-start.2) | collective-permute-done | bytes 16416 | tf_op jit(solution)/shard_map/ppermute | solution.py:11
  14.0 2.0 %collective-permute-start.3 = (bf16[2,2,2,2,1024]{4,3,0,1,2:T(2,128)(2,1)S(1)}, bf16[2,2,2,2,1024]{4,3,0,1,2:T(2,128)(2,1)S(1)}, u32[]{:S(2)}, u32[]{:S(2)}) collective-permute-start(bf16[2,2,2,2,1024]{4,3,0,1,2:T(2,128)(2,1)S(1)} %pad_maximum_fusion.11), channel_id=1, source_target_pairs={{0,8},{4,12},{8,0},{12,4},{16,24},{20,28},{24,16},{28,20},{1,9},{5... | collective-permute-start | bytes 98312 | tf_op jit(solution)/shard_map/ppermute | solution.py:11
  16.0 2.0 %collective-permute-done.3 = bf16[2,2,2,2,1024]{4,3,0,1,2:T(2,128)(2,1)S(1)} collective-permute-done((bf16[2,2,2,2,1024]{4,3,0,1,2:T(2,128)(2,1)S(1)}, bf16[2,2,2,2,1024]{4,3,0,1,2:T(2,128)(2,1)S(1)}, u32[]{:S(2)}, u32[]{:S(2)}) %collective-permute-start.3) | collective-permute-done | bytes 32800 | tf_op jit(solution)/shard_map/ppermute | solution.py:11
  18.1 1.9 %collective-permute-start.4 = (bf16[2,2,4,2,1024]{4,3,0,1,2:T(2,128)(2,1)S(1)}, bf16[2,2,4,2,1024]{4,3,0,1,2:T(2,128)(2,1)S(1)}, u32[]{:S(2)}, u32[]{:S(2)}) collective-permute-start(bf16[2,2,4,2,1024]{4,3,0,1,2:T(2,128)(2,1)S(1)} %pad_maximum_fusion.10), channel_id=1, source_target_pairs={{0,4},{4,0},{8,12},{12,8},{16,20},{20,16},{24,28},{28,24},{1,5},{5... | collective-permute-start | bytes 196616 | tf_op jit(solution)/shard_map/ppermute | solution.py:11
  20.0 2.4 %collective-permute-done.4 = bf16[2,2,4,2,1024]{4,3,0,1,2:T(2,128)(2,1)S(1)} collective-permute-done((bf16[2,2,4,2,1024]{4,3,0,1,2:T(2,128)(2,1)S(1)}, bf16[2,2,4,2,1024]{4,3,0,1,2:T(2,128)(2,1)S(1)}, u32[]{:S(2)}, u32[]{:S(2)}) %collective-permute-start.4) | collective-permute-done | bytes 65568 | tf_op jit(solution)/shard_map/ppermute | solution.py:11
  22.9 1.9 %collective-permute-start.17 = (bf16[2,2,16,1024]{3,1,2,0:T(2,128)(2,1)S(1)}, bf16[2,2,16,1024]{3,1,2,0:T(2,128)(2,1)S(1)}, u32[]{:S(2)}, u32[]{:S(2)}) collective-permute-start(bf16[2,2,16,1024]{3,1,2,0:T(2,128)(2,1)S(1)} %bitcast.57), channel_id=1, source_target_pairs={{0,2},{1,3},{2,0},{3,1},{4,6},{5,7},{6,4},{7,5},{8,10},{9,11},{10,... | collective-permute-start | bytes 393224 | tf_op jit(solution)/shard_map/ppermute | solution.py:11
  24.8 3.0 %fusion.25 = f32[64,2048]{1,0:T(8,128)S(1)} fusion(bf16[64,1024]{1,0:T(8,128)(2,1)S(1)} %reshape.93, bf16[1024,2048]{1,0:T(8,128)(2,1)} %param.9), kind=kOutput, calls=%fused_computation.82 | convolution fusion | flops 268435456 | bytes 4849664 | tf_op jit(solution)/shard_map/dot_general | solution.py:53
  27.9 0.8 %fusion.24 = f32[64,2048]{1,0:T(8,128)S(1)} fusion(bf16[64,1024]{1,0:T(8,128)(2,1)S(1)} %reshape.93, bf16[1024,2048]{1,0:T(8,128)(2,1)S(1)} %copy-done.1), kind=kOutput, calls=%fused_computation.81 | convolution fusion | flops 268435456 | bytes 4849664 | tf_op jit(solution)/shard_map/dot_general | solution.py:53
  29.4 0.8 rev.6
  31.7 1.7 %collective-permute-start.6 = (bf16[32,2048]{1,0:T(8,128)(2,1)S(1)}, bf16[32,2048]{1,0:T(8,128)(2,1)S(1)}, u32[]{:S(2)}, u32[]{:S(2)}) collective-permute-start(bf16[32,2048]{1,0:T(8,128)(2,1)S(1)} %fusion.4), channel_id=1, source_target_pairs={{0,2},{1,3},{2,0},{3,1},{4,6},{5,7},{6,4},{7,5},{8,10},{9,11},{10,... | collective-permute-start | bytes 393224 | tf_op jit(solution)/shard_map/ppermute | solution.py:11
  33.4 4.2 %collective-permute-done.8 = bf16[32,2048]{1,0:T(8,128)(2,1)S(1)} collective-permute-done((bf16[32,2048]{1,0:T(8,128)(2,1)S(1)}, bf16[32,2048]{1,0:T(8,128)(2,1)S(1)}, u32[]{:S(2)}, u32[]{:S(2)}) %collective-permute-start.8) | collective-permute-done | bytes 131104 | tf_op jit(solution)/shard_map/ppermute | solution.py:11
  37.7 2.1 %collective-permute-done.6 = bf16[32,2048]{1,0:T(8,128)(2,1)S(1)} collective-permute-done((bf16[32,2048]{1,0:T(8,128)(2,1)S(1)}, bf16[32,2048]{1,0:T(8,128)(2,1)S(1)}, u32[]{:S(2)}, u32[]{:S(2)}) %collective-permute-start.6) | collective-permute-done | bytes 131104 | tf_op jit(solution)/shard_map/ppermute | solution.py:11
  40.8 0.7 gather_fusion.4
  41.5 3.7 %fusion.6 = f32[64,1024]{1,0:T(8,128)S(1)} fusion(bf16[1024,2048]{1,0:T(8,128)(2,1)} %param.9, bf16[32,2048]{1,0:T(8,128)(2,1)S(1)} %collective-permute-done.11, bf16[32,2048]{1,0:T(8,128)(2,1)S(1)} %get-tuple-element.7), kind=kOutput, calls=%fused_computation.28 | convolution fusion | flops 268959744 | bytes 4718592 | tf_op jit(solution)/shard_map/dot_general | solution.py:78
  45.2 1.4 %convolution_add_fusion = f32[64,1024]{1,0:T(8,128)S(1)} fusion(f32[64,1024]{1,0:T(8,128)S(1)} %fusion.6, bf16[1024,2048]{1,0:T(8,128)(2,1)S(1)} %copy-done.2, bf16[32,2048]{1,0:T(8,128)(2,1)S(1)} %collective-permute-done.10, bf16[32,2048]{1,0:T(8,128)(2,1)S(1)} %get-tuple-element.11), kind=kOutput, calls=%fused_computation.8 | convolution fusion | flops 269025280 | bytes 4980736 | tf_op jit(solution)/shard_map/dot_general | solution.py:77
  46.8 1.6 %collective-permute-start.12 = (f32[2,2,4,2,1024]{4,3,0,1,2:T(2,128)S(1)}, f32[2,2,4,2,1024]{4,3,0,1,2:T(2,128)S(1)}, u32[]{:S(2)}, u32[]{:S(2)}) collective-permute-start(f32[2,2,4,2,1024]{4,3,0,1,2:T(2,128)S(1)} %copy.22), channel_id=1, source_target_pairs={{0,4},{4,0},{8,12},{12,8},{16,20},{20,16},{24,28},{28,24},{1,5},{5... | collective-permute-start | bytes 393224 | tf_op jit(solution)/shard_map/ppermute | solution.py:11
  48.7 3.7 %collective-permute-done.12 = f32[2,2,4,2,1024]{4,3,0,1,2:T(2,128)S(1)} collective-permute-done((f32[2,2,4,2,1024]{4,3,0,1,2:T(2,128)S(1)}, f32[2,2,4,2,1024]{4,3,0,1,2:T(2,128)S(1)}, u32[]{:S(2)}, u32[]{:S(2)}) %collective-permute-start.12) | collective-permute-done | bytes 131104 | tf_op jit(solution)/shard_map/ppermute | solution.py:11
  52.5 1.6 %collective-permute-start.13 = (f32[2,2,2,2,1024]{4,3,0,1,2:T(2,128)S(1)}, f32[2,2,2,2,1024]{4,3,0,1,2:T(2,128)S(1)}, u32[]{:S(2)}, u32[]{:S(2)}) collective-permute-start(f32[2,2,2,2,1024]{4,3,0,1,2:T(2,128)S(1)} %slice.124), channel_id=1, source_target_pairs={{0,8},{4,12},{8,0},{12,4},{16,24},{20,28},{24,16},{28,20},{1,9},{5... | collective-permute-start | bytes 196616 | tf_op jit(solution)/shard_map/ppermute | solution.py:11
  54.1 0.7 maximum_bitcast_fusion
  55.6 1.2 %collective-permute-done.13 = f32[2,2,2,2,1024]{4,3,0,1,2:T(2,128)S(1)} collective-permute-done((f32[2,2,2,2,1024]{4,3,0,1,2:T(2,128)S(1)}, f32[2,2,2,2,1024]{4,3,0,1,2:T(2,128)S(1)}, u32[]{:S(2)}, u32[]{:S(2)}) %collective-permute-start.13) | collective-permute-done | bytes 65568 | tf_op jit(solution)/shard_map/ppermute | solution.py:11
  56.9 2.7 %collective-permute-start.14 = (f32[2,2,1,2,1024]{4,3,0,1,2:T(2,128)S(1)}, f32[2,2,1,2,1024]{4,3,0,1,2:T(2,128)S(1)}, u32[]{:S(2)}, u32[]{:S(2)}) collective-permute-start(f32[2,2,1,2,1024]{4,3,0,1,2:T(2,128)S(1)} %slice.126), channel_id=1, source_target_pairs={{0,16},{4,20},{8,24},{12,28},{16,0},{20,4},{24,8},{28,12},{1,17},{... | collective-permute-start | bytes 98312 | tf_op jit(solution)/shard_map/ppermute | solution.py:11
  60.4 1.4 %collective-permute-done.14 = f32[2,2,1,2,1024]{4,3,0,1,2:T(2,128)S(1)} collective-permute-done((f32[2,2,1,2,1024]{4,3,0,1,2:T(2,128)S(1)}, f32[2,2,1,2,1024]{4,3,0,1,2:T(2,128)S(1)}, u32[]{:S(2)}, u32[]{:S(2)}) %collective-permute-start.14) | collective-permute-done | bytes 32800 | tf_op jit(solution)/shard_map/ppermute | solution.py:11
  61.8 0.7 collective-permute-start.15
  62.5 8.5 %multiply_convert_fusion.1 = bf16[4096,2048]{1,0:T(8,128)(2,1)} fusion(bf16[64,4096]{1,0:T(8,128)(2,1)S(1)} %bitcast.54, bf16[32,2048]{1,0:T(8,128)(2,1)S(1)} %collective-permute-done.10, bf16[32,2048]{1,0:T(8,128)(2,1)S(1)} %get-tuple-element.11), kind=kOutput, calls=%fused_computation.7 | convolution fusion | flops 1091043328 | bytes 17563648 | tf_op jit(solution)/shard_map/dot_general | solution.py:92
  71.1 8.6 %multiply_convert_fusion = bf16[4096,2048]{1,0:T(8,128)(2,1)} fusion(bf16[64,4096]{1,0:T(8,128)(2,1)S(1)} %bitcast.55, bf16[32,2048]{1,0:T(8,128)(2,1)S(1)} %collective-permute-done.11, bf16[32,2048]{1,0:T(8,128)(2,1)S(1)} %get-tuple-element.7), kind=kOutput, calls=%fused_computation.6 | convolution fusion | flops 1091043328 | bytes 17563648 | tf_op jit(solution)/shard_map/dot_general | solution.py:93
  80.3 0.7 select_convert_fusion
  (79 shorter events, 8.4 us)
Async XLA Ops:
  0.6 0.7 copy-start
  2.1 5.6 %collective-permute-start = (bf16[2,2,1024]{2,1,0:T(2,128)(2,1)S(1)}, bf16[2,2,1024]{2,1,0:T(2,128)(2,1)S(1)}, u32[]{:S(2)}, u32[]{:S(2)}) collective-permute-start(bf16[2,2,1024]{2,1,0:T(2,128)(2,1)S(1)} %get-tuple-element.25), channel_id=1, source_target_pairs={{0,2},{1,3},{2,0},{3,1},{4,6},{5,7},{6,4},{7,5},{8,10},{9,11},{10,... | collective-permute-start | bytes 24584 | tf_op jit(solution)/shard_map/ppermute | solution.py:11
  7.5 32.3 %collective-permute-start.9 = (bf16[16,2048]{1,0:T(8,128)(2,1)S(1)}, bf16[16,2048]{1,0:T(8,128)(2,1)S(1)}, u32[]{:S(2)}, u32[]{:S(2)}) collective-permute-start(bf16[16,2048]{1,0:T(8,128)(2,1)S(1)} %reshape.96), channel_id=1, source_target_pairs={{0,2},{1,3},{2,0},{3,1},{4,6},{5,7},{6,4},{7,5},{8,10},{9,11},{10,... | collective-permute-start | bytes 196616 | tf_op jit(solution)/shard_map/ppermute | solution.py:11
  7.6 1.4 %collective-permute-start.1 = (bf16[2,2,1024]{2,1,0:T(2,128)(2,1)S(1)}, bf16[2,2,1024]{2,1,0:T(2,128)(2,1)S(1)}, u32[]{:S(2)}, u32[]{:S(2)}) collective-permute-start(bf16[2,2,1024]{2,1,0:T(2,128)(2,1)S(1)} %get-tuple-element.23), channel_id=1, source_target_pairs={{0,1},{1,0},{2,3},{3,2},{4,5},{5,4},{6,7},{7,6},{8,9},{9,8},{10,11... | collective-permute-start | bytes 24584 | tf_op jit(solution)/shard_map/ppermute | solution.py:11
  9.1 4.9 %collective-permute-start.2 = (bf16[2,2,1,2,1024]{4,3,0,1,2:T(2,128)(2,1)S(1)}, bf16[2,2,1,2,1024]{4,3,0,1,2:T(2,128)(2,1)S(1)}, u32[]{:S(2)}, u32[]{:S(2)}) collective-permute-start(bf16[2,2,1,2,1024]{4,3,0,1,2:T(2,128)(2,1)S(1)} %maximum_bitcast_fusion.1), channel_id=1, source_target_pairs={{0,16},{4,20},{8,24},{12,28},{16,0},{20,4},{24,8},{28,12},{1,17},{... | collective-permute-start | bytes 49160 | tf_op jit(solution)/shard_map/ppermute | solution.py:11
  14.0 4.0 %collective-permute-start.3 = (bf16[2,2,2,2,1024]{4,3,0,1,2:T(2,128)(2,1)S(1)}, bf16[2,2,2,2,1024]{4,3,0,1,2:T(2,128)(2,1)S(1)}, u32[]{:S(2)}, u32[]{:S(2)}) collective-permute-start(bf16[2,2,2,2,1024]{4,3,0,1,2:T(2,128)(2,1)S(1)} %pad_maximum_fusion.11), channel_id=1, source_target_pairs={{0,8},{4,12},{8,0},{12,4},{16,24},{20,28},{24,16},{28,20},{1,9},{5... | collective-permute-start | bytes 98312 | tf_op jit(solution)/shard_map/ppermute | solution.py:11
  18.1 4.3 %collective-permute-start.4 = (bf16[2,2,4,2,1024]{4,3,0,1,2:T(2,128)(2,1)S(1)}, bf16[2,2,4,2,1024]{4,3,0,1,2:T(2,128)(2,1)S(1)}, u32[]{:S(2)}, u32[]{:S(2)}) collective-permute-start(bf16[2,2,4,2,1024]{4,3,0,1,2:T(2,128)(2,1)S(1)} %pad_maximum_fusion.10), channel_id=1, source_target_pairs={{0,4},{4,0},{8,12},{12,8},{16,20},{20,16},{24,28},{28,24},{1,5},{5... | collective-permute-start | bytes 196616 | tf_op jit(solution)/shard_map/ppermute | solution.py:11
  22.9 5.0 %copy-start.1 = (bf16[1024,2048]{1,0:T(8,128)(2,1)S(1)}, bf16[1024,2048]{1,0:T(8,128)(2,1)}, u32[]{:S(2)}) copy-start(bf16[1024,2048]{1,0:T(8,128)(2,1)} %param.8) | copy-start | bytes 12582916
  22.9 6.5 %collective-permute-start.17 = (bf16[2,2,16,1024]{3,1,2,0:T(2,128)(2,1)S(1)}, bf16[2,2,16,1024]{3,1,2,0:T(2,128)(2,1)S(1)}, u32[]{:S(2)}, u32[]{:S(2)}) collective-permute-start(bf16[2,2,16,1024]{3,1,2,0:T(2,128)(2,1)S(1)} %bitcast.57), channel_id=1, source_target_pairs={{0,2},{1,3},{2,0},{3,1},{4,6},{5,7},{6,4},{7,5},{8,10},{9,11},{10,... | collective-permute-start | bytes 393224 | tf_op jit(solution)/shard_map/ppermute | solution.py:11
  27.8 3.4 %collective-permute-start.7 = (f32[32,2048]{1,0:T(8,128)S(1)}, f32[32,2048]{1,0:T(8,128)S(1)}, u32[]{:S(2)}, u32[]{:S(2)}) collective-permute-start(f32[32,2048]{1,0:T(8,128)S(1)} %slice.116), channel_id=1, source_target_pairs={{0,1},{1,0},{2,3},{3,2},{4,5},{5,4},{6,7},{7,6},{8,9},{9,8},{10,11... | collective-permute-start | bytes 786440 | tf_op jit(solution)/shard_map/ppermute | solution.py:11
  28.8 2.9 %collective-permute-start.5 = (f32[32,2048]{1,0:T(8,128)S(1)}, f32[32,2048]{1,0:T(8,128)S(1)}, u32[]{:S(2)}, u32[]{:S(2)}) collective-permute-start(f32[32,2048]{1,0:T(8,128)S(1)} %slice.112), channel_id=1, source_target_pairs={{0,1},{1,0},{2,3},{3,2},{4,5},{5,4},{6,7},{7,6},{8,9},{9,8},{10,11... | collective-permute-start | bytes 786440 | tf_op jit(solution)/shard_map/ppermute | solution.py:11
  30.5 18.0 %collective-permute-start.18 = (bf16[2,2,2,16,1024]{4,2,3,1,0:T(2,128)(2,1)S(1)}, bf16[2,2,2,16,1024]{4,2,3,1,0:T(2,128)(2,1)S(1)}, u32[]{:S(2)}, u32[]{:S(2)}) collective-permute-start(bf16[2,2,2,16,1024]{4,2,3,1,0:T(2,128)(2,1)S(1)} %pad_maximum_fusion.2), channel_id=1, source_target_pairs={{0,1},{1,0},{2,3},{3,2},{4,5},{5,4},{6,7},{7,6},{8,9},{9,8},{10,11... | collective-permute-start | bytes 786440 | tf_op jit(solution)/shard_map/ppermute | solution.py:11
  31.2 6.4 %collective-permute-start.8 = (bf16[32,2048]{1,0:T(8,128)(2,1)S(1)}, bf16[32,2048]{1,0:T(8,128)(2,1)S(1)}, u32[]{:S(2)}, u32[]{:S(2)}) collective-permute-start(bf16[32,2048]{1,0:T(8,128)(2,1)S(1)} %fusion.3), channel_id=1, source_target_pairs={{0,2},{1,3},{2,0},{3,1},{4,6},{5,7},{6,4},{7,5},{8,10},{9,11},{10,... | collective-permute-start | bytes 393224 | tf_op jit(solution)/shard_map/ppermute | solution.py:11
  31.7 8.1 %collective-permute-start.6 = (bf16[32,2048]{1,0:T(8,128)(2,1)S(1)}, bf16[32,2048]{1,0:T(8,128)(2,1)S(1)}, u32[]{:S(2)}, u32[]{:S(2)}) collective-permute-start(bf16[32,2048]{1,0:T(8,128)(2,1)S(1)} %fusion.4), channel_id=1, source_target_pairs={{0,2},{1,3},{2,0},{3,1},{4,6},{5,7},{6,4},{7,5},{8,10},{9,11},{10,... | collective-permute-start | bytes 393224 | tf_op jit(solution)/shard_map/ppermute | solution.py:11
  40.0 1.4 %collective-permute-start.11 = (bf16[32,2048]{1,0:T(8,128)(2,1)S(1)}, bf16[32,2048]{1,0:T(8,128)(2,1)S(1)}, u32[]{:S(2)}, u32[]{:S(2)}) collective-permute-start(bf16[32,2048]{1,0:T(8,128)(2,1)S(1)} %get-tuple-element.7), channel_id=1, source_target_pairs={{0,1},{1,0},{2,3},{3,2},{4,5},{5,4},{6,7},{7,6},{8,9},{9,8},{10,11... | collective-permute-start | bytes 393224 | tf_op jit(solution)/shard_map/ppermute | solution.py:11
  40.2 5.0 %collective-permute-start.10 = (bf16[32,2048]{1,0:T(8,128)(2,1)S(1)}, bf16[32,2048]{1,0:T(8,128)(2,1)S(1)}, u32[]{:S(2)}, u32[]{:S(2)}) collective-permute-start(bf16[32,2048]{1,0:T(8,128)(2,1)S(1)} %get-tuple-element.11), channel_id=1, source_target_pairs={{0,1},{1,0},{2,3},{3,2},{4,5},{5,4},{6,7},{7,6},{8,9},{9,8},{10,11... | collective-permute-start | bytes 393224 | tf_op jit(solution)/shard_map/ppermute | solution.py:11
  41.4 3.8 %copy-start.2 = (bf16[1024,2048]{1,0:T(8,128)(2,1)S(1)}, bf16[1024,2048]{1,0:T(8,128)(2,1)}, u32[]{:S(2)}) copy-start(bf16[1024,2048]{1,0:T(8,128)(2,1)} %param.8) | copy-start | bytes 12582916
  46.8 5.6 %collective-permute-start.12 = (f32[2,2,4,2,1024]{4,3,0,1,2:T(2,128)S(1)}, f32[2,2,4,2,1024]{4,3,0,1,2:T(2,128)S(1)}, u32[]{:S(2)}, u32[]{:S(2)}) collective-permute-start(f32[2,2,4,2,1024]{4,3,0,1,2:T(2,128)S(1)} %copy.22), channel_id=1, source_target_pairs={{0,4},{4,0},{8,12},{12,8},{16,20},{20,16},{24,28},{28,24},{1,5},{5... | collective-permute-start | bytes 393224 | tf_op jit(solution)/shard_map/ppermute | solution.py:11
  52.5 4.3 %collective-permute-start.13 = (f32[2,2,2,2,1024]{4,3,0,1,2:T(2,128)S(1)}, f32[2,2,2,2,1024]{4,3,0,1,2:T(2,128)S(1)}, u32[]{:S(2)}, u32[]{:S(2)}) collective-permute-start(f32[2,2,2,2,1024]{4,3,0,1,2:T(2,128)S(1)} %slice.124), channel_id=1, source_target_pairs={{0,8},{4,12},{8,0},{12,4},{16,24},{20,28},{24,16},{28,20},{1,9},{5... | collective-permute-start | bytes 196616 | tf_op jit(solution)/shard_map/ppermute | solution.py:11
  56.9 4.9 %collective-permute-start.14 = (f32[2,2,1,2,1024]{4,3,0,1,2:T(2,128)S(1)}, f32[2,2,1,2,1024]{4,3,0,1,2:T(2,128)S(1)}, u32[]{:S(2)}, u32[]{:S(2)}) collective-permute-start(f32[2,2,1,2,1024]{4,3,0,1,2:T(2,128)S(1)} %slice.126), channel_id=1, source_target_pairs={{0,16},{4,20},{8,24},{12,28},{16,0},{20,4},{24,8},{28,12},{1,17},{... | collective-permute-start | bytes 98312 | tf_op jit(solution)/shard_map/ppermute | solution.py:11
  61.8 9.2 %collective-permute-start.15 = (bf16[2,2,1024]{2,1,0:T(2,128)(2,1)S(1)}, bf16[2,2,1024]{2,1,0:T(2,128)(2,1)S(1)}, u32[]{:S(2)}, u32[]{:S(2)}) collective-permute-start(bf16[2,2,1024]{2,1,0:T(2,128)(2,1)S(1)} %get-tuple-element.21), channel_id=1, source_target_pairs={{0,2},{1,3},{2,0},{3,1},{4,6},{5,7},{6,4},{7,5},{8,10},{9,11},{10,... | collective-permute-start | bytes 24584 | tf_op jit(solution)/shard_map/ppermute | solution.py:11
  71.1 8.6 %collective-permute-start.16 = (bf16[2,2,1024]{2,1,0:T(2,128)(2,1)S(1)}, bf16[2,2,1024]{2,1,0:T(2,128)(2,1)S(1)}, u32[]{:S(2)}, u32[]{:S(2)}) collective-permute-start(bf16[2,2,1024]{2,1,0:T(2,128)(2,1)S(1)} %get-tuple-element.19), channel_id=1, source_target_pairs={{0,1},{1,0},{2,3},{3,2},{4,5},{5,4},{6,7},{7,6},{8,9},{9,8},{10,11... | collective-permute-start | bytes 24584 | tf_op jit(solution)/shard_map/ppermute | solution.py:11

commit v2 on v1

v2 whole, which is shorter than its diff:
```python
import functools

import jax
import jax.numpy as jnp
from jax import lax
from jax.experimental import pallas as pl
from jax.experimental.pallas import tpu as pltpu
from jax.sharding import PartitionSpec as P


F32 = jnp.float32
BF16 = jnp.bfloat16
VMEM = pl.BlockSpec(memory_space=pltpu.VMEM)
ANY = pl.BlockSpec(memory_space=pl.ANY)


def swap(value, tp_mask, dp_mask):
    n_tp, n_dp = lax.axis_size("tp"), lax.axis_size("dp")
    pairs = [(t * n_dp + r, (t ^ tp_mask) * n_dp + (r ^ dp_mask)) for t in range(n_tp) for r in range(n_dp)]
    return lax.ppermute(value, ("tp", "dp"), pairs)


def bits_of(size):
    assert size & (size - 1) == 0
    return [1 << k for k in reversed(range(size.bit_length() - 1))]


def swish_parts(gate_pre):
    s = jax.nn.sigmoid(gate_pre)
    return gate_pre * s, s * (1.0 + gate_pre * (1.0 - s))


def load_kernel(w_ref, o_ref, sem):
    copy = pltpu.make_async_copy(w_ref, o_ref, sem)
    copy.start()
    copy.wait()


def load(weight):
    return pl.pallas_call(
        load_kernel,
        in_specs=[ANY],
        out_specs=VMEM,
        out_shape=pltpu.VMEM(weight.shape, weight.dtype),
        scratch_shapes=[pltpu.SemaphoreType.DMA],
        compiler_params=pltpu.CompilerParams(vmem_limit_bytes=1 << 20),
        cost_estimate=pl.CostEstimate(flops=0, bytes_accessed=2 * weight.size, transcendentals=0),
    )(weight)


def outer_kernel(rows_ref, grad_ref, *rest, base, steps, scale):
    out_ref, buf, sem = rest[-3:]
    slots, tall, wide = buf.shape
    across = grad_ref.shape[1] // wide
    depth = slots // across

    def copy(step, col):
        slot = lax.rem(step, depth) * across + col
        top = pl.multiple_of((base + step) * tall, tall)
        return pltpu.make_async_copy(
            buf.at[slot], out_ref.at[pl.ds(top, tall), pl.ds(col * wide, wide)], sem.at[slot]
        )

    def body(step, carry):
        top = pl.multiple_of((base + step) * tall, tall)
        left = rows_ref[:, pl.ds(top, tall)]
        for col in range(across):

            @pl.when(step >= depth)
            def _():
                copy(step - depth, col).wait()

            acc = lax.dot_general(
                left, grad_ref[:, col * wide : (col + 1) * wide], (((0,), (0,)), ((), ())), preferred_element_type=F32
            )
            buf[lax.rem(step, depth) * across + col] = (acc * scale).astype(BF16)
            copy(step, col).start()
        return carry

    lax.fori_loop(0, steps, body, 0)
    for step in range(max(0, steps - depth), steps):
        for col in range(across):
            copy(step, col).wait()


def outer(rows, grad, scale, begin, share, whole=None):
    count, d_model = rows.shape
    width = grad.shape[1]
    tall, wide = min(512, d_model // share), min(1024, width)
    steps = d_model // share // tall
    slots = 2 * (width // wide)
    kernel = functools.partial(outer_kernel, base=begin * steps, steps=steps, scale=scale)
    args = (rows, grad) if whole is None else (rows, grad, whole)
    return pl.pallas_call(
        kernel,
        in_specs=[VMEM, VMEM] + [ANY] * (len(args) - 2),
        out_specs=ANY,
        out_shape=jax.ShapeDtypeStruct((d_model, width), BF16),
        input_output_aliases={2: 0} if whole is not None else {},
        scratch_shapes=[pltpu.VMEM((slots, tall, wide), BF16), pltpu.SemaphoreType.DMA((slots,))],
        compiler_params=pltpu.CompilerParams(vmem_limit_bytes=24 << 20),
        cost_estimate=pl.CostEstimate(
            flops=2 * count * d_model * width // share,
            bytes_accessed=2 * d_model * width // share + 2 * count * (d_model + width),
            transcendentals=0,
        ),
    )(*args)


def shards(tokens, gate_weight, up_weight, cotangent):
    n_tp, n_dp = lax.axis_size("tp"), lax.axis_size("dp")
    assert n_dp == 4
    t, r = lax.axis_index("tp"), lax.axis_index("dp")
    _, rt, d_model = tokens.shape
    depth, width = gate_weight.shape
    rows = rt * n_tp
    rel = [0]
    for bit in bits_of(n_tp):
        rel = rel + [v ^ bit for v in rel]
    odd = jnp.array([v.bit_count() % 2 == 1 for v in rel])[None, :, None, None]
    place = [rel.index(v) for v in range(n_tp)]
    rel, place = jnp.array(rel), jnp.array(place)

    cot = swap(cotangent[0], 0, 3)
    cot = jnp.stack([cotangent[0], cot]).reshape(2, n_tp, rt, width)
    cot = jnp.take(cot, t ^ rel, axis=1).reshape(2 * rows, width)

    part = tokens
    for bit in bits_of(n_tp):
        part = jnp.concatenate([part, swap(part, bit, 1)])
    part = jnp.stack([part, swap(part, 0, 3)])
    far = swap(part, 0, 1)
    feats = jnp.stack([jnp.where(odd, far, part), jnp.where(odd, part, far)])
    feats = feats.reshape(4 * rows, d_model)
    own = lax.dynamic_slice(feats, (0, r * depth), (4 * rows, depth))
    gate_weight = load(gate_weight)
    up_weight = load(up_weight)

    def pre(weight):
        out = jnp.dot(own, weight, preferred_element_type=F32)
        half = (out[: 2 * rows] + swap(out[2 * rows :], 0, 1)).astype(BF16)
        other = swap(half, 0, 3)
        other = jnp.concatenate([other[rows:], other[:rows]])
        return half.astype(F32) + other.astype(F32)

    gate_pre, up_pre = pre(gate_weight), pre(up_weight)
    act, slope = swish_parts(gate_pre)
    hidden = (act * up_pre)[:rows].astype(BF16).reshape(n_tp, rt, width)
    hidden = jnp.take(hidden, place[t ^ jnp.arange(n_tp)], axis=0).reshape(1, rows, width)
    back = cot.astype(F32)
    d_gate = (back * up_pre * slope).astype(BF16)
    d_up = (back * act).astype(BF16)
    d_gate = jnp.concatenate([d_gate, swap(d_gate, 0, 1)])
    d_up = jnp.concatenate([d_up, swap(d_up, 0, 1)])

    cols = (((1,), (1,)), ((), ()))
    total = lax.dot_general(d_gate, gate_weight, cols, preferred_element_type=F32)
    total = total + lax.dot_general(d_up, up_weight, cols, preferred_element_type=F32)
    total = total.reshape(2, 2, n_tp, rt, depth)
    for bit in reversed(bits_of(n_tp)):
        mid = total.shape[2] // 2
        total = total[:, :, :mid] + swap(total[:, :, mid:], bit, 0)
    total = total[:, :, 0]
    total = jnp.stack([total[:, 0], swap(total[:, 1], 0, 3)], axis=1)
    total = jnp.stack([total[0], swap(total[1], 0, 1)])
    total = total.reshape(n_dp, rt, depth)
    at = jnp.array([0, 2, 3, 1])
    total = jnp.take(total, at[r ^ jnp.arange(n_dp)], axis=0).transpose(1, 0, 2)
    grad_tokens = total.reshape(1, rt, d_model).astype(BF16)

    inverse = 1.0 / n_dp
    grad_gate = outer(feats, d_gate, inverse, 0, 2)
    grad_gate = outer(feats, d_gate, inverse, 1, 2, grad_gate)
    grad_up = outer(feats, d_up, inverse, 0, 2)
    grad_up = outer(feats, d_up, inverse, 1, 2, grad_up)
    return hidden, grad_tokens, grad_gate, grad_up


def solution(mesh):
    in_specs = (P("dp", "tp", None), P("dp", "tp"), P("dp", "tp"), P("dp", None, "tp"))
    out_specs = (P("dp", None, "tp"), P("dp", "tp", None), P(None, "tp"), P(None, "tp"))

    return jax.shard_map(shards, mesh=mesh, in_specs=in_specs, out_specs=out_specs, check_vma=False)
```

time: 81.3 us -> 87.5 us (1.076)
  Pallas kernels: 0 us -> 18.6 us
  matrix products: 26.1 us -> 8.99 us
  starting transfers between devices: 22.4 us -> 14.8 us
  local copies, waits for them, and re-layouts: 8.41 us -> 15.1 us
  waiting for transfers between devices: 18.8 us -> 22.3 us
  other arithmetic: 4.2 us -> 6.17 us
    pallas_call x0 -> x6, Pallas kernels: none -> 18.6 us  [the longest x4 18 us: outer(): pl.pallas_call(kernel, in_specs=[VMEM, VMEM] + [ANY] * (len(args) - 2), o...]
    dot_general x4 -> x2, matrix products: 20.9 us -> 4.02 us  [pre(): out = jnp.dot(own, weight, preferred_element_type=F32)]
    unnamed x7 -> x18, local copies, waits for them, and re-layouts: 0.69 us -> 8.42 us
    ppermute x19 -> x17, starting transfers between devices: 22.4 us -> 14.8 us  [swap(): return lax.ppermute(value, ('tp', 'dp'), pairs)]
    ppermute x19 -> x17, waiting for transfers between devices: 18.8 us -> 22.3 us  [swap(): return lax.ppermute(value, ('tp', 'dp'), pairs)]
    concatenate x3 -> x4, other arithmetic: 0.33 us -> 1.61 us  [the longest x2 1.58 us: shards(): part = jnp.concatenate([part, swap(part, bit, 1)])]
    another operation x5 -> x6, other arithmetic: 0.81 us -> 1.99 us  [the longest x2 1.39 us: shards(): feats = jnp.stack([jnp.where(odd, far, part), jnp.where(odd, part, far)])]
    gather x4 -> x5, local copies, waits for them, and re-layouts: 2.44 us -> 2.84 us  [the longest x2 1.89 us: shards(): total = jnp.take(total, at[r ^ jnp.arange(n_dp)], axis=0).transpose(1, 0, 2)]
  transfers between devices with their start and end apart: 19 -> 17, of which waited for: 8 -> 10; matrix products, arithmetic and copies ran while one was open for 44% -> 16% of each run, Pallas kernels for 0% -> 21%
where the time goes in v2:
time: 87.5 us; the launch traced here: 87 us
  waiting for transfers between devices  22.3 us (25%)
  Pallas kernels  18.6 us (21%)
  local copies, waits for them, and re-layouts  15.1 us (17%)
  starting transfers between devices  14.8 us (17%)
  matrix products  8.99 us (10%)
  other arithmetic  6.17 us (7%)
  between operations  1.06 us (1%)
    ppermute x17, waiting for transfers between devices, swap(): return lax.ppermute(value, ('tp', 'dp'), pairs)  22.3 us
    pallas_call x4, Pallas kernels, outer(): pl.pallas_call(kernel, in_specs=[VMEM, VMEM] + [ANY] * (len(args) - 2), o...  18 us
    ppermute x17, starting transfers between devices, swap(): return lax.ppermute(value, ('tp', 'dp'), pairs)  14.8 us
    unnamed x18, local copies, waits for them, and re-layouts  8.42 us
    dot_general x2, matrix products, pre(): out = jnp.dot(own, weight, preferred_element_type=F32)  4.02 us
    dot_general x1, matrix products, shards(): lax.dot_general(d_up, up_weight, cols, preferred_element_type=F32)  3.58 us
    gather x2, local copies, waits for them, and re-layouts, shards(): total = jnp.take(total, at[r ^ jnp.arange(n_dp)], axis=0).transpose(1, 0, 2)  1.89 us
  transfers between devices with their start and end apart: 17, of which 10 were waited for; matrix products, arithmetic and copies ran while one was open for 16% of the time, Pallas kernels for 21%

profile of v2, /device:TPU:0, one launch (start us, length us, event | category | flops | bytes accessed | tf_op | source)
XLA Modules:
  0.0 87.0 jit_solution(5323132969271789025)
XLA Ops:
  0.6 3.6 %collective-permute-start = (bf16[1,2,4096]{2,1,0:T(2,128)(2,1)}, bf16[1,2,4096]{2,1,0:T(2,128)(2,1)S(1)}, u32[]{:S(2)}, u32[]{:S(2)}) collective-permute-start(bf16[1,2,4096]{2,1,0:T(2,128)(2,1)} %param.8), channel_id=1, source_target_pairs={{0,17},{1,16},{2,19},{3,18},{4,21},{5,20},{6,23},{7,22},{8,25},{9,... | collective-permute-start | bytes 49160 | tf_op jit(solution)/shard_map/ppermute | solution.py:20
  4.2 1.8 %collective-permute-start.9 = (bf16[16,2048]{1,0:T(8,128)(2,1)}, bf16[16,2048]{1,0:T(8,128)(2,1)S(1)}, u32[]{:S(2)}, u32[]{:S(2)}) collective-permute-start(bf16[16,2048]{1,0:T(8,128)(2,1)} %bitcast.45), channel_id=1, source_target_pairs={{0,3},{1,2},{2,1},{3,0},{4,7},{5,6},{6,5},{7,4},{8,11},{9,10},{10,... | collective-permute-start | bytes 196616 | tf_op jit(solution)/shard_map/ppermute | solution.py:20
  6.6 1.3 %gather_fusion = s32[8]{0:T(128)S(1)} fusion(s32[8]{0:T(128)} %constant.70.clone, s32[1024]{0:T(1024)S(1)} %pad_clamp_fusion.4), kind=kCustom, calls=%fused_computation | custom fusion | bytes 96 | tf_op jit(solution)/shard_map/gather | solution.py:149
  8.0 0.7 constant_dynamic-update-slice_fusion.3
  8.7 1.3 %gather_fusion.2 = s32[4]{0:T(128)S(1)} fusion(s32[4]{0:T(128)} %constant.71.clone, s32[1024]{0:T(1024)S(1)} %pad_clamp_fusion.2), kind=kCustom, calls=%fused_computation.2 | custom fusion | bytes 48 | tf_op jit(solution)/shard_map/gather | solution.py:168
  10.0 0.8 pad_maximum_fusion.7
  10.8 1.1 %collective-permute-start.1 = (bf16[2,2,4096]{2,1,0:T(2,128)(2,1)S(1)}, bf16[2,2,4096]{2,1,0:T(2,128)(2,1)S(1)}, u32[]{:S(2)}, u32[]{:S(2)}) collective-permute-start(bf16[2,2,4096]{2,1,0:T(2,128)(2,1)S(1)} %pad_maximum_fusion.7), channel_id=1, source_target_pairs={{0,9},{1,8},{2,11},{3,10},{4,13},{5,12},{6,15},{7,14},{8,1},{9,0},... | collective-permute-start | bytes 98312 | tf_op jit(solution)/shard_map/ppermute | solution.py:20
  11.9 2.5 %collective-permute-done.1 = bf16[2,2,4096]{2,1,0:T(2,128)(2,1)S(1)} collective-permute-done((bf16[2,2,4096]{2,1,0:T(2,128)(2,1)S(1)}, bf16[2,2,4096]{2,1,0:T(2,128)(2,1)S(1)}, u32[]{:S(2)}, u32[]{:S(2)}) %collective-permute-start.1) | collective-permute-done | bytes 32800 | tf_op jit(solution)/shard_map/ppermute | solution.py:20
  14.4 0.8 pad_maximum_fusion.6
  15.3 1.3 %collective-permute-start.2 = (bf16[4,2,4096]{2,1,0:T(2,128)(2,1)S(1)}, bf16[4,2,4096]{2,1,0:T(2,128)(2,1)S(1)}, u32[]{:S(2)}, u32[]{:S(2)}) collective-permute-start(bf16[4,2,4096]{2,1,0:T(2,128)(2,1)S(1)} %pad_maximum_fusion.6), channel_id=1, source_target_pairs={{0,5},{1,4},{2,7},{3,6},{4,1},{5,0},{6,3},{7,2},{8,13},{9,12},{10,... | collective-permute-start | bytes 196616 | tf_op jit(solution)/shard_map/ppermute | solution.py:20
  16.6 2.8 %collective-permute-done.2 = bf16[4,2,4096]{2,1,0:T(2,128)(2,1)S(1)} collective-permute-done((bf16[4,2,4096]{2,1,0:T(2,128)(2,1)S(1)}, bf16[4,2,4096]{2,1,0:T(2,128)(2,1)S(1)}, u32[]{:S(2)}, u32[]{:S(2)}) %collective-permute-start.2) | collective-permute-done | bytes 65568 | tf_op jit(solution)/shard_map/ppermute | solution.py:20
  19.8 5.2 %collective-permute-done.3 = bf16[8,2,4096]{2,1,0:T(2,128)(2,1)S(1)} collective-permute-done((bf16[8,2,4096]{2,1,0:T(2,128)(2,1)S(1)}, bf16[8,2,4096]{2,1,0:T(2,128)(2,1)S(1)}, u32[]{:S(2)}, u32[]{:S(2)}) %collective-permute-start.3) | collective-permute-done | bytes 131104 | tf_op jit(solution)/shard_map/ppermute | solution.py:20
  25.6 0.9 %stack.44 = bf16[1,8,2,2048]{3,2,1,0:T(2,128)(2,1)S(1)} reshape(bf16[1,16,2048]{2,1,0:T(8,128)(2,1)} %param.11) | data formatting | bytes 131072 | tf_op jit(solution)/shard_map/stack | solution.py:125
  26.8 2.2 %copy-done.4 = bf16[1024,2048]{1,0:T(8,128)(2,1)S(1)} copy-done((bf16[1024,2048]{1,0:T(8,128)(2,1)S(1)}, bf16[1024,2048]{1,0:T(8,128)(2,1)}, u32[]{:S(2)}) %copy-start.4) | copy-done | bytes 4194328
  29.3 2.1 %copy-done = bf16[1024,2048]{1,0:T(8,128)(2,1)} copy-done((bf16[1024,2048]{1,0:T(8,128)(2,1)}, bf16[1024,2048]{1,0:T(8,128)(2,1)S(1)}, u32[]{:S(2)}) %copy-start) | copy-done | bytes 4194328
  31.5 1.3 %copy-done.5 = bf16[1024,2048]{1,0:T(8,128)(2,1)S(1)} copy-done((bf16[1024,2048]{1,0:T(8,128)(2,1)S(1)}, bf16[1024,2048]{1,0:T(8,128)(2,1)}, u32[]{:S(2)}) %copy-start.5) | copy-done | bytes 4194328
  33.0 2.0 %copy-done.3 = bf16[1024,2048]{1,0:T(8,128)(2,1)} copy-done((bf16[1024,2048]{1,0:T(8,128)(2,1)}, bf16[1024,2048]{1,0:T(8,128)(2,1)S(1)}, u32[]{:S(2)}) %copy-start.3) | copy-done | bytes 4194328
  35.3 0.8 gather_fusion.3
  37.0 0.7 pad_maximum_fusion
  37.9 3.2 %fusion.9 = f32[64,2048]{1,0:T(8,128)S(1)} fusion(bf16[1024,2048]{1,0:T(8,128)(2,1)} %copy-done.3, bf16[64,4096]{1,0:T(8,128)(2,1)S(1)} %reshape.148.rows_ref, s32[]{:T(128)S(6)} %select_n.92), kind=kOutput, calls=%fused_computation.33 | convolution fusion | flops 268435456 | bytes 4849668 | tf_op jit(solution)/shard_map/dot_general | solution.py:140
  41.6 0.8 fusion.11
  44.7 3.4 %collective-permute-done.8 = bf16[32,2048]{1,0:T(8,128)(2,1)S(1)} collective-permute-done((bf16[32,2048]{1,0:T(8,128)(2,1)S(1)}, bf16[32,2048]{1,0:T(8,128)(2,1)S(1)}, u32[]{:S(2)}, u32[]{:S(2)}) %collective-permute-start.8) | collective-permute-done | bytes 131104 | tf_op jit(solution)/shard_map/ppermute | solution.py:20
  48.2 2.8 %collective-permute-done.6 = bf16[32,2048]{1,0:T(8,128)(2,1)S(1)} collective-permute-done((bf16[32,2048]{1,0:T(8,128)(2,1)S(1)}, bf16[32,2048]{1,0:T(8,128)(2,1)S(1)}, u32[]{:S(2)}, u32[]{:S(2)}) %collective-permute-start.6) | collective-permute-done | bytes 131104 | tf_op jit(solution)/shard_map/ppermute | solution.py:20
  53.4 3.6 %fusion.23 = f32[64,1024]{1,0:T(8,128)S(1)} fusion(bf16[1024,2048]{1,0:T(8,128)(2,1)} %copy-done.3, bf16[32,2048]{1,0:T(8,128)(2,1)S(1)} %collective-permute-done.11, bf16[32,2048]{1,0:T(8,128)(2,1)S(1)} %get-tuple-element.4), kind=kOutput, calls=%fused_computation.78 | convolution fusion | flops 268959744 | bytes 4718592 | tf_op jit(solution)/shard_map/dot_general | solution.py:158
  57.0 1.4 %convolution_add_fusion = f32[64,1024]{1,0:T(8,128)S(1)} fusion(f32[64,1024]{1,0:T(8,128)S(1)} %fusion.23, bf16[1024,2048]{1,0:T(8,128)(2,1)S(1)} %copy-done.2, bf16[32,2048]{1,0:T(8,128)(2,1)S(1)} %collective-permute-done.10, bf16[32,2048]{1,0:T(8,128)(2,1)S(1)} %get-tuple-element.10), kind=kOutput, calls=%fused_computation.5 | convolution fusion | flops 269025280 | bytes 4980736 | tf_op jit(solution)/shard_map/dot_general | solution.py:157
  58.5 1.6 %collective-permute-start.12 = (f32[2,2,4,2,1024]{4,3,2,1,0:T(2,128)S(1)}, f32[2,2,4,2,1024]{4,3,2,1,0:T(2,128)S(1)}, u32[]{:S(2)}, u32[]{:S(2)}) collective-permute-start(f32[2,2,4,2,1024]{4,3,2,1,0:T(2,128)S(1)} %slice.98), channel_id=1, source_target_pairs={{0,4},{1,5},{2,6},{3,7},{4,0},{5,1},{6,2},{7,3},{8,12},{9,13},{10,... | collective-permute-start | bytes 393224 | tf_op jit(solution)/shard_map/ppermute | solution.py:20
  60.1 4.2 %collective-permute-done.12 = f32[2,2,4,2,1024]{4,3,2,1,0:T(2,128)S(1)} collective-permute-done((f32[2,2,4,2,1024]{4,3,2,1,0:T(2,128)S(1)}, f32[2,2,4,2,1024]{4,3,2,1,0:T(2,128)S(1)}, u32[]{:S(2)}, u32[]{:S(2)}) %collective-permute-start.12) | collective-permute-done | bytes 131104 | tf_op jit(solution)/shard_map/ppermute | solution.py:20
  64.5 1.8 %collective-permute-start.13 = (f32[2,2,2,2,1024]{4,3,2,1,0:T(2,128)S(1)}, f32[2,2,2,2,1024]{4,3,2,1,0:T(2,128)S(1)}, u32[]{:S(2)}, u32[]{:S(2)}) collective-permute-start(f32[2,2,2,2,1024]{4,3,2,1,0:T(2,128)S(1)} %slice.100), channel_id=1, source_target_pairs={{0,8},{1,9},{2,10},{3,11},{4,12},{5,13},{6,14},{7,15},{8,0},{9,1},... | collective-permute-start | bytes 196616 | tf_op jit(solution)/shard_map/ppermute | solution.py:20
  66.2 4.5 %shard_map.113.rest_0_ = bf16[4096,2048]{1,0:T(8,128)(2,1)} custom-call(bf16[64,4096]{1,0:T(8,128)(2,1)S(1)} %reshape.148.rows_ref, bf16[64,2048]{1,0:T(8,128)(2,1)S(1)} %pad_maximum_fusion.2.grad_ref), custom_call_target="tpu_custom_call" | custom-call | flops 536870912 | bytes 9175040 | tf_op jit(solution)/shard_map/pallas_call | solution.py:94
  70.9 4.5 %shard_map.114 = bf16[4096,2048]{1,0:T(8,128)(2,1)} custom-call(bf16[64,4096]{1,0:T(8,128)(2,1)S(1)} %reshape.148.rows_ref, bf16[64,2048]{1,0:T(8,128)(2,1)S(1)} %pad_maximum_fusion.2.grad_ref, bf16[4096,2048]{1,0:T(8,128)(2,1)} %shard_map.113.rest_0_), custom_call_target="tpu_custom_call", output_to_operand_aliasing={{}: (2, {})} | custom-call | flops 536870912 | bytes 9175040 | tf_op jit(solution)/shard_map/pallas_call | solution.py:94
  76.0 4.5 %shard_map.115.rest_0_ = bf16[4096,2048]{1,0:T(8,128)(2,1)} custom-call(bf16[64,4096]{1,0:T(8,128)(2,1)S(1)} %reshape.148.rows_ref, bf16[64,2048]{1,0:T(8,128)(2,1)S(1)} %pad_maximum_fusion.3.grad_ref), custom_call_target="tpu_custom_call" | custom-call | flops 536870912 | bytes 9175040 | tf_op jit(solution)/shard_map/pallas_call | solution.py:94
  81.2 4.5 %shard_map.116 = bf16[4096,2048]{1,0:T(8,128)(2,1)} custom-call(bf16[64,4096]{1,0:T(8,128)(2,1)S(1)} %reshape.148.rows_ref, bf16[64,2048]{1,0:T(8,128)(2,1)S(1)} %pad_maximum_fusion.3.grad_ref, bf16[4096,2048]{1,0:T(8,128)(2,1)} %shard_map.115.rest_0_), custom_call_target="tpu_custom_call", output_to_operand_aliasing={{}: (2, {})} | custom-call | flops 536870912 | bytes 9175040 | tf_op jit(solution)/shard_map/pallas_call | solution.py:94
  (86 shorter events, 12.0 us)
Async XLA Ops:
  0.6 9.4 %collective-permute-start = (bf16[1,2,4096]{2,1,0:T(2,128)(2,1)}, bf16[1,2,4096]{2,1,0:T(2,128)(2,1)S(1)}, u32[]{:S(2)}, u32[]{:S(2)}) collective-permute-start(bf16[1,2,4096]{2,1,0:T(2,128)(2,1)} %param.8), channel_id=1, source_target_pairs={{0,17},{1,16},{2,19},{3,18},{4,21},{5,20},{6,23},{7,22},{8,25},{9,... | collective-permute-start | bytes 49160 | tf_op jit(solution)/shard_map/ppermute | solution.py:20
  4.2 30.9 %collective-permute-start.9 = (bf16[16,2048]{1,0:T(8,128)(2,1)}, bf16[16,2048]{1,0:T(8,128)(2,1)S(1)}, u32[]{:S(2)}, u32[]{:S(2)}) collective-permute-start(bf16[16,2048]{1,0:T(8,128)(2,1)} %bitcast.45), channel_id=1, source_target_pairs={{0,3},{1,2},{2,1},{3,0},{4,7},{5,6},{6,5},{7,4},{8,11},{9,10},{10,... | collective-permute-start | bytes 196616 | tf_op jit(solution)/shard_map/ppermute | solution.py:20
  10.8 3.6 %collective-permute-start.1 = (bf16[2,2,4096]{2,1,0:T(2,128)(2,1)S(1)}, bf16[2,2,4096]{2,1,0:T(2,128)(2,1)S(1)}, u32[]{:S(2)}, u32[]{:S(2)}) collective-permute-start(bf16[2,2,4096]{2,1,0:T(2,128)(2,1)S(1)} %pad_maximum_fusion.7), channel_id=1, source_target_pairs={{0,9},{1,8},{2,11},{3,10},{4,13},{5,12},{6,15},{7,14},{8,1},{9,0},... | collective-permute-start | bytes 98312 | tf_op jit(solution)/shard_map/ppermute | solution.py:20
  15.3 4.2 %collective-permute-start.2 = (bf16[4,2,4096]{2,1,0:T(2,128)(2,1)S(1)}, bf16[4,2,4096]{2,1,0:T(2,128)(2,1)S(1)}, u32[]{:S(2)}, u32[]{:S(2)}) collective-permute-start(bf16[4,2,4096]{2,1,0:T(2,128)(2,1)S(1)} %pad_maximum_fusion.6), channel_id=1, source_target_pairs={{0,5},{1,4},{2,7},{3,6},{4,1},{5,0},{6,3},{7,2},{8,13},{9,12},{10,... | collective-permute-start | bytes 196616 | tf_op jit(solution)/shard_map/ppermute | solution.py:20
  19.5 5.6 %collective-permute-start.3 = (bf16[8,2,4096]{2,1,0:T(2,128)(2,1)S(1)}, bf16[8,2,4096]{2,1,0:T(2,128)(2,1)S(1)}, u32[]{:S(2)}, u32[]{:S(2)}) collective-permute-start(bf16[8,2,4096]{2,1,0:T(2,128)(2,1)S(1)} %constant_dynamic-update-slice_fusion), channel_id=1, source_target_pairs={{0,3},{1,2},{2,1},{3,0},{4,7},{5,6},{6,5},{7,4},{8,11},{9,10},{10,... | collective-permute-start | bytes 393224 | tf_op jit(solution)/shard_map/ppermute | solution.py:20
  25.4 10.9 %collective-permute-start.4 = (bf16[2,8,2,4096]{3,2,1,0:T(2,128)(2,1)S(1)}, bf16[2,8,2,4096]{3,2,1,0:T(2,128)(2,1)S(1)}, u32[]{:S(2)}, u32[]{:S(2)}) collective-permute-start(bf16[2,8,2,4096]{3,2,1,0:T(2,128)(2,1)S(1)} %pad_maximum_fusion.1), channel_id=1, source_target_pairs={{0,1},{1,0},{2,3},{3,2},{4,5},{5,4},{6,7},{7,6},{8,9},{9,8},{10,11... | collective-permute-start | bytes 786440 | tf_op jit(solution)/shard_map/ppermute | solution.py:20
  26.8 2.2 %copy-start.4 = (bf16[1024,2048]{1,0:T(8,128)(2,1)S(1)}, bf16[1024,2048]{1,0:T(8,128)(2,1)}, u32[]{:S(2)}) copy-start(bf16[1024,2048]{1,0:T(8,128)(2,1)} %w_ref.2) | copy-start | bytes 12582916
  29.0 3.7 %copy-start.5 = (bf16[1024,2048]{1,0:T(8,128)(2,1)S(1)}, bf16[1024,2048]{1,0:T(8,128)(2,1)}, u32[]{:S(2)}) copy-start(bf16[1024,2048]{1,0:T(8,128)(2,1)} %w_ref.3) | copy-start | bytes 12582916
  29.3 2.1 %copy-start = (bf16[1024,2048]{1,0:T(8,128)(2,1)}, bf16[1024,2048]{1,0:T(8,128)(2,1)S(1)}, u32[]{:S(2)}) copy-start(bf16[1024,2048]{1,0:T(8,128)(2,1)S(1)} %shard_map.111) | copy-start | bytes 12582916
  32.7 3.6 %copy-start.6 = (pred[8]{0:T(512)(128)(4,1)S(1)}, pred[8]{0:T(512)(128)(4,1)}, u32[]{:S(2)}) copy-start(pred[8]{0:T(512)(128)(4,1)} %constant.69.clone) | copy-start | bytes 28
  33.0 2.0 %copy-start.3 = (bf16[1024,2048]{1,0:T(8,128)(2,1)}, bf16[1024,2048]{1,0:T(8,128)(2,1)S(1)}, u32[]{:S(2)}) copy-start(bf16[1024,2048]{1,0:T(8,128)(2,1)S(1)} %shard_map.112) | copy-start | bytes 12582916
  37.9 3.7 %copy-start.1 = (bf16[1024,2048]{1,0:T(8,128)(2,1)S(1)}, bf16[1024,2048]{1,0:T(8,128)(2,1)}, u32[]{:S(2)}) copy-start(bf16[1024,2048]{1,0:T(8,128)(2,1)} %copy-done) | copy-start | bytes 12582916
  41.1 1.6 %collective-permute-start.7 = (f32[32,2048]{1,0:T(8,128)S(1)}, f32[32,2048]{1,0:T(8,128)S(1)}, u32[]{:S(2)}, u32[]{:S(2)}) collective-permute-start(f32[32,2048]{1,0:T(8,128)S(1)} %slice.92), channel_id=1, source_target_pairs={{0,1},{1,0},{2,3},{3,2},{4,5},{5,4},{6,7},{7,6},{8,9},{9,8},{10,11... | collective-permute-start | bytes 786440 | tf_op jit(solution)/shard_map/ppermute | solution.py:20
  42.5 1.6 %collective-permute-start.5 = (f32[32,2048]{1,0:T(8,128)S(1)}, f32[32,2048]{1,0:T(8,128)S(1)}, u32[]{:S(2)}, u32[]{:S(2)}) collective-permute-start(f32[32,2048]{1,0:T(8,128)S(1)} %slice.88), channel_id=1, source_target_pairs={{0,1},{1,0},{2,3},{3,2},{4,5},{5,4},{6,7},{7,6},{8,9},{9,8},{10,11... | collective-permute-start | bytes 786440 | tf_op jit(solution)/shard_map/ppermute | solution.py:20
  42.8 5.3 %collective-permute-start.8 = (bf16[32,2048]{1,0:T(8,128)(2,1)S(1)}, bf16[32,2048]{1,0:T(8,128)(2,1)S(1)}, u32[]{:S(2)}, u32[]{:S(2)}) collective-permute-start(bf16[32,2048]{1,0:T(8,128)(2,1)S(1)} %fusion.3), channel_id=1, source_target_pairs={{0,3},{1,2},{2,1},{3,0},{4,7},{5,6},{6,5},{7,4},{8,11},{9,10},{10,... | collective-permute-start | bytes 393224 | tf_op jit(solution)/shard_map/ppermute | solution.py:20
  44.1 6.8 %collective-permute-start.6 = (bf16[32,2048]{1,0:T(8,128)(2,1)S(1)}, bf16[32,2048]{1,0:T(8,128)(2,1)S(1)}, u32[]{:S(2)}, u32[]{:S(2)}) collective-permute-start(bf16[32,2048]{1,0:T(8,128)(2,1)S(1)} %fusion.4), channel_id=1, source_target_pairs={{0,3},{1,2},{2,1},{3,0},{4,7},{5,6},{6,5},{7,4},{8,11},{9,10},{10,... | collective-permute-start | bytes 393224 | tf_op jit(solution)/shard_map/ppermute | solution.py:20
  51.9 5.0 %copy-start.2 = (bf16[1024,2048]{1,0:T(8,128)(2,1)S(1)}, bf16[1024,2048]{1,0:T(8,128)(2,1)}, u32[]{:S(2)}) copy-start(bf16[1024,2048]{1,0:T(8,128)(2,1)} %copy-done) | copy-start | bytes 12582916
  51.9 1.4 %collective-permute-start.11 = (bf16[32,2048]{1,0:T(8,128)(2,1)S(1)}, bf16[32,2048]{1,0:T(8,128)(2,1)S(1)}, u32[]{:S(2)}, u32[]{:S(2)}) collective-permute-start(bf16[32,2048]{1,0:T(8,128)(2,1)S(1)} %get-tuple-element.4), channel_id=1, source_target_pairs={{0,1},{1,0},{2,3},{3,2},{4,5},{5,4},{6,7},{7,6},{8,9},{9,8},{10,11... | collective-permute-start | bytes 393224 | tf_op jit(solution)/shard_map/ppermute | solution.py:20
  52.4 4.6 %collective-permute-start.10 = (bf16[32,2048]{1,0:T(8,128)(2,1)S(1)}, bf16[32,2048]{1,0:T(8,128)(2,1)S(1)}, u32[]{:S(2)}, u32[]{:S(2)}) collective-permute-start(bf16[32,2048]{1,0:T(8,128)(2,1)S(1)} %get-tuple-element.10), channel_id=1, source_target_pairs={{0,1},{1,0},{2,3},{3,2},{4,5},{5,4},{6,7},{7,6},{8,9},{9,8},{10,11... | collective-permute-start | bytes 393224 | tf_op jit(solution)/shard_map/ppermute | solution.py:20
  58.5 5.8 %collective-permute-start.12 = (f32[2,2,4,2,1024]{4,3,2,1,0:T(2,128)S(1)}, f32[2,2,4,2,1024]{4,3,2,1,0:T(2,128)S(1)}, u32[]{:S(2)}, u32[]{:S(2)}) collective-permute-start(f32[2,2,4,2,1024]{4,3,2,1,0:T(2,128)S(1)} %slice.98), channel_id=1, source_target_pairs={{0,4},{1,5},{2,6},{3,7},{4,0},{5,1},{6,2},{7,3},{8,12},{9,13},{10,... | collective-permute-start | bytes 393224 | tf_op jit(solution)/shard_map/ppermute | solution.py:20
  64.5 6.3 %collective-permute-start.13 = (f32[2,2,2,2,1024]{4,3,2,1,0:T(2,128)S(1)}, f32[2,2,2,2,1024]{4,3,2,1,0:T(2,128)S(1)}, u32[]{:S(2)}, u32[]{:S(2)}) collective-permute-start(f32[2,2,2,2,1024]{4,3,2,1,0:T(2,128)S(1)} %slice.100), channel_id=1, source_target_pairs={{0,8},{1,9},{2,10},{3,11},{4,12},{5,13},{6,14},{7,15},{8,0},{9,1},... | collective-permute-start | bytes 196616 | tf_op jit(solution)/shard_map/ppermute | solution.py:20
  70.8 5.0 %collective-permute-start.14 = (f32[2,2,1,2,1024]{4,3,2,1,0:T(2,128)S(1)}, f32[2,2,1,2,1024]{4,3,2,1,0:T(2,128)S(1)}, u32[]{:S(2)}, u32[]{:S(2)}) collective-permute-start(f32[2,2,1,2,1024]{4,3,2,1,0:T(2,128)S(1)} %slice.102), channel_id=1, source_target_pairs={{0,16},{1,17},{2,18},{3,19},{4,20},{5,21},{6,22},{7,23},{8,24},{9,... | collective-permute-start | bytes 98312 | tf_op jit(solution)/shard_map/ppermute | solution.py:20
  75.9 4.6 %collective-permute-start.15 = (bf16[2,2,1024]{2,1,0:T(2,128)(2,1)S(1)}, bf16[2,2,1024]{2,1,0:T(2,128)(2,1)S(1)}, u32[]{:S(2)}, u32[]{:S(2)}) collective-permute-start(bf16[2,2,1024]{2,1,0:T(2,128)(2,1)S(1)} %get-tuple-element.18), channel_id=1, source_target_pairs={{0,3},{1,2},{2,1},{3,0},{4,7},{5,6},{6,5},{7,4},{8,11},{9,10},{10,... | collective-permute-start | bytes 24584 | tf_op jit(solution)/shard_map/ppermute | solution.py:20
  80.5 5.2 %collective-permute-start.16 = (bf16[2,2,1024]{2,1,0:T(2,128)(2,1)S(1)}, bf16[2,2,1024]{2,1,0:T(2,128)(2,1)S(1)}, u32[]{:S(2)}, u32[]{:S(2)}) collective-permute-start(bf16[2,2,1024]{2,1,0:T(2,128)(2,1)S(1)} %get-tuple-element.16), channel_id=1, source_target_pairs={{0,1},{1,0},{2,3},{3,2},{4,5},{5,4},{6,7},{7,6},{8,9},{9,8},{10,11... | collective-permute-start | bytes 24584 | tf_op jit(solution)/shard_map/ppermute | solution.py:20

commit v3 on v2

v3 whole, which is shorter than its diff:
```python
import functools

import jax
import jax.numpy as jnp
from jax import lax
from jax.experimental import pallas as pl
from jax.experimental.pallas import tpu as pltpu
from jax.sharding import PartitionSpec as P


F32 = jnp.float32
BF16 = jnp.bfloat16
VMEM = pl.BlockSpec(memory_space=pltpu.VMEM)
HBM = pl.BlockSpec(memory_space=pltpu.HBM)


def swap(value, tp_mask, dp_mask):
    n_tp, n_dp = lax.axis_size("tp"), lax.axis_size("dp")
    pairs = [(t * n_dp + r, (t ^ tp_mask) * n_dp + (r ^ dp_mask)) for t in range(n_tp) for r in range(n_dp)]
    return lax.ppermute(value, ("tp", "dp"), pairs)


def bits_of(size):
    assert size & (size - 1) == 0
    return [1 << k for k in reversed(range(size.bit_length() - 1))]


def swish_parts(gate_pre):
    s = jax.nn.sigmoid(gate_pre)
    return gate_pre * s, s * (1.0 + gate_pre * (1.0 - s))


def outer_kernel(rows_ref, grad_ref, *rest, base, steps, scale):
    out_ref, buf, sem = rest[-3:]
    depth, tall, width = buf.shape
    wide = min(512, width)

    def copy(step):
        top = pl.multiple_of((base + step) * tall, tall)
        slot = lax.rem(step, depth)
        return pltpu.make_async_copy(buf.at[slot], out_ref.at[pl.ds(top, tall), :], sem.at[slot])

    def body(step, carry):
        top = pl.multiple_of((base + step) * tall, tall)
        left = rows_ref[:, pl.ds(top, tall)]

        @pl.when(step >= depth)
        def _():
            copy(step - depth).wait()

        for at in range(0, width, wide):
            acc = lax.dot_general(
                left, grad_ref[:, at : at + wide], (((0,), (0,)), ((), ())), preferred_element_type=F32
            )
            buf[lax.rem(step, depth), :, at : at + wide] = (acc * scale).astype(BF16)
        copy(step).start()
        return carry

    lax.fori_loop(0, steps, body, 0)
    for step in range(max(0, steps - depth), steps):
        copy(step).wait()


def outer(rows, grad, scale, begin, share, whole=None):
    count, d_model = rows.shape
    width = grad.shape[1]
    tall = min(1024, d_model // share)
    steps = d_model // share // tall
    kernel = functools.partial(outer_kernel, base=begin * steps, steps=steps, scale=scale)
    args = (rows, grad) if whole is None else (rows, grad, whole)
    return pl.pallas_call(
        kernel,
        in_specs=[VMEM, VMEM] + [HBM] * (len(args) - 2),
        out_specs=HBM,
        out_shape=jax.ShapeDtypeStruct((d_model, width), BF16),
        input_output_aliases={2: 0} if whole is not None else {},
        scratch_shapes=[pltpu.VMEM((2, tall, width), BF16), pltpu.SemaphoreType.DMA((2,))],
        compiler_params=pltpu.CompilerParams(vmem_limit_bytes=20 << 20),
        cost_estimate=pl.CostEstimate(
            flops=2 * count * d_model * width // share,
            bytes_accessed=2 * d_model * width // share + 2 * count * (d_model + width),
            transcendentals=0,
        ),
    )(*args)


def shards(tokens, gate_weight, up_weight, cotangent):
    n_tp, n_dp = lax.axis_size("tp"), lax.axis_size("dp")
    assert n_dp == 4
    t, r = lax.axis_index("tp"), lax.axis_index("dp")
    _, rt, d_model = tokens.shape
    depth, width = gate_weight.shape
    rows = rt * n_tp
    rel = [0]
    for bit in bits_of(n_tp):
        rel = rel + [v ^ bit for v in rel]
    odd = jnp.array([v.bit_count() % 2 == 1 for v in rel])[None, :, None, None]
    place = [rel.index(v) for v in range(n_tp)]
    rel, place = jnp.array(rel), jnp.array(place)

    part = tokens
    for bit in bits_of(n_tp):
        part = jnp.concatenate([part, swap(part, bit, 1)])
    part = jnp.stack([part, swap(part, 0, 3)])
    far = swap(part, 0, 1)
    feats = jnp.stack([jnp.where(odd, far, part), jnp.where(odd, part, far)])
    feats = feats.reshape(4 * rows, d_model)
    own = lax.dynamic_slice(feats, (0, r * depth), (4 * rows, depth))

    def partial(weight):
        out = jnp.dot(own, weight, preferred_element_type=F32)
        return (out[: 2 * rows] + swap(out[2 * rows :], 0, 1)).astype(BF16)

    def summed(half):
        other = swap(half, 0, 3)
        other = jnp.concatenate([other[rows:], other[:rows]])
        return half.astype(F32) + other.astype(F32)

    half_gate, half_up = partial(gate_weight), partial(up_weight)
    gate_pre, up_pre = summed(half_gate), summed(half_up)

    cot = swap(cotangent[0], 0, 3)
    near, cot, _ = lax.optimization_barrier((cotangent[0], cot, half_up))
    cot = jnp.stack([near, cot]).reshape(2, n_tp, rt, width)
    cot = jnp.take(cot, t ^ rel, axis=1).reshape(2 * rows, width)

    act, slope = swish_parts(gate_pre)
    hidden = (act * up_pre)[:rows].astype(BF16).reshape(n_tp, rt, width)
    hidden = jnp.take(hidden, place[t ^ jnp.arange(n_tp)], axis=0).reshape(1, rows, width)
    grad_hidden = cot.astype(F32)
    d_gate = (grad_hidden * up_pre * slope).astype(BF16)
    d_up = (grad_hidden * act).astype(BF16)
    d_gate = jnp.concatenate([d_gate, swap(d_gate, 0, 1)])
    d_up = jnp.concatenate([d_up, swap(d_up, 0, 1)])

    cols = (((1,), (1,)), ((), ()))
    total = lax.dot_general(d_gate, gate_weight, cols, preferred_element_type=F32)
    total = total + lax.dot_general(d_up, up_weight, cols, preferred_element_type=F32)
    total = total.reshape(2, 2, n_tp, rt, depth)
    for bit in reversed(bits_of(n_tp)):
        mid = total.shape[2] // 2
        total = total[:, :, :mid] + swap(total[:, :, mid:], bit, 0)
    total = total[:, :, 0]
    total = jnp.stack([total[:, 0], swap(total[:, 1], 0, 3)], axis=1)
    total = jnp.stack([total[0], swap(total[1], 0, 1)])
    total = [total[0, 0], total[1, 0], total[1, 1], total[0, 1]]
    for bit in (1, 2):
        total = [jnp.where(r & bit != 0, total[m ^ bit], total[m]) for m in range(n_dp)]
    grad_tokens = jnp.concatenate([v.astype(BF16) for v in total], axis=1)[None]

    inverse = 1.0 / n_dp
    grad_gate = outer(feats, d_gate, inverse, 0, 2)
    grad_gate = outer(feats, d_gate, inverse, 1, 2, grad_gate)
    grad_up = outer(feats, d_up, inverse, 0, 2)
    grad_up = outer(feats, d_up, inverse, 1, 2, grad_up)
    return hidden, grad_tokens, grad_gate, grad_up


def solution(mesh):
    in_specs = (P("dp", "tp", None), P("dp", "tp"), P("dp", "tp"), P("dp", None, "tp"))
    out_specs = (P("dp", None, "tp"), P("dp", "tp", None), P(None, "tp"), P(None, "tp"))

    return jax.shard_map(shards, mesh=mesh, in_specs=in_specs, out_specs=out_specs, check_vma=False)
```

time: 87.5 us -> 78.9 us (0.902)
  local copies, waits for them, and re-layouts: 15.1 us -> 4.79 us
  starting transfers between devices: 14.8 us -> 16.2 us
    unnamed x18 -> x10, local copies, waits for them, and re-layouts: 8.42 us -> 0.82 us
    gather x2 -> x0, local copies, waits for them, and re-layouts: 1.89 us -> none  [shards(): total = jnp.take(total, at[r ^ jnp.arange(n_dp)], axis=0).transpose(1, 0, 2)]
    ppermute x17, starting transfers between devices: 14.8 us -> 16.2 us  [swap(): return lax.ppermute(value, ('tp', 'dp'), pairs)]
    pallas_call x6 -> x4, Pallas kernels: 18.6 us -> 19 us  [outer(): pl.pallas_call(kernel, in_specs=[VMEM, VMEM] + [HBM] * (len(args) - 2), o...]
  transfers between devices with their start and end apart: 17 -> 17, of which waited for: 10 -> 10; matrix products, arithmetic and copies ran while one was open for 16% -> 22% of each run, Pallas kernels for 21% -> 24%
where the time goes in v3:
time: 78.9 us; the launch traced here: 78.4 us
  waiting for transfers between devices  21.7 us (28%)
  Pallas kernels  19 us (24%)
  starting transfers between devices  16.2 us (21%)
  matrix products  8.99 us (11%)
  other arithmetic  6.74 us (9%)
  local copies, waits for them, and re-layouts  4.79 us (6%)
  between operations  1.01 us (1%)
    ppermute x17, waiting for transfers between devices, swap(): return lax.ppermute(value, ('tp', 'dp'), pairs)  21.7 us
    pallas_call x4, Pallas kernels, outer(): pl.pallas_call(kernel, in_specs=[VMEM, VMEM] + [HBM] * (len(args) - 2), o...  19 us
    ppermute x17, starting transfers between devices, swap(): return lax.ppermute(value, ('tp', 'dp'), pairs)  16.2 us
    dot_general x2, matrix products, partial(): out = jnp.dot(own, weight, preferred_element_type=F32)  4.02 us
    dot_general x1, matrix products, shards(): lax.dot_general(d_up, up_weight, cols, preferred_element_type=F32)  3.58 us
    another operation x2, other arithmetic, shards(): feats = jnp.stack([jnp.where(odd, far, part), jnp.where(odd, part, far)])  2.05 us
    concatenate x2, other arithmetic, shards(): part = jnp.concatenate([part, swap(part, bit, 1)])  1.58 us
  transfers between devices with their start and end apart: 17, of which 10 were waited for; matrix products, arithmetic and copies ran while one was open for 22% of the time, Pallas kernels for 24%

profile of v3, /device:TPU:0, one launch (start us, length us, event | category | flops | bytes accessed | tf_op | source)
XLA Modules:
  0.0 78.4 jit_solution(589139766720224899)
XLA Ops:
  0.6 3.6 %collective-permute-start = (bf16[1,2,4096]{2,1,0:T(2,128)(2,1)}, bf16[1,2,4096]{2,1,0:T(2,128)(2,1)S(1)}, u32[]{:S(2)}, u32[]{:S(2)}) collective-permute-start(bf16[1,2,4096]{2,1,0:T(2,128)(2,1)} %param.7), channel_id=1, source_target_pairs={{0,17},{1,16},{2,19},{3,18},{4,21},{5,20},{6,23},{7,22},{8,25},{9,... | collective-permute-start | bytes 49160 | tf_op jit(solution)/shard_map/ppermute | solution.py:20
  4.2 1.8 %collective-permute-start.9 = (bf16[16,2048]{1,0:T(8,128)(2,1)}, bf16[16,2048]{1,0:T(8,128)(2,1)S(1)}, u32[]{:S(2)}, u32[]{:S(2)}) collective-permute-start(bf16[16,2048]{1,0:T(8,128)(2,1)} %bitcast.92), channel_id=1, source_target_pairs={{0,3},{1,2},{2,1},{3,0},{4,7},{5,6},{6,5},{7,4},{8,11},{9,10},{10,... | collective-permute-start | bytes 196616 | tf_op jit(solution)/shard_map/ppermute | solution.py:20
  6.0 0.7 constant_dynamic-update-slice_fusion.3
  7.6 1.3 %gather_fusion = s32[8]{0:T(128)S(1)} fusion(s32[8]{0:T(128)} %constant.55.clone, s32[1024]{0:T(1024)S(1)} %pad_clamp_fusion.2), kind=kCustom, calls=%fused_computation | custom fusion | bytes 96 | tf_op jit(solution)/shard_map/gather | solution.py:129
  8.9 0.8 pad_maximum_fusion.7
  9.7 1.1 %collective-permute-start.1 = (bf16[2,2,4096]{2,1,0:T(2,128)(2,1)S(1)}, bf16[2,2,4096]{2,1,0:T(2,128)(2,1)S(1)}, u32[]{:S(2)}, u32[]{:S(2)}) collective-permute-start(bf16[2,2,4096]{2,1,0:T(2,128)(2,1)S(1)} %pad_maximum_fusion.7), channel_id=1, source_target_pairs={{0,9},{1,8},{2,11},{3,10},{4,13},{5,12},{6,15},{7,14},{8,1},{9,0},... | collective-permute-start | bytes 98312 | tf_op jit(solution)/shard_map/ppermute | solution.py:20
  10.8 2.5 %collective-permute-done.1 = bf16[2,2,4096]{2,1,0:T(2,128)(2,1)S(1)} collective-permute-done((bf16[2,2,4096]{2,1,0:T(2,128)(2,1)S(1)}, bf16[2,2,4096]{2,1,0:T(2,128)(2,1)S(1)}, u32[]{:S(2)}, u32[]{:S(2)}) %collective-permute-start.1) | collective-permute-done | bytes 32800 | tf_op jit(solution)/shard_map/ppermute | solution.py:20
  13.3 0.8 %pad_maximum_fusion.6 = bf16[4,2,4096]{2,1,0:T(2,128)(2,1)S(1)} fusion(bf16[2,2,4096]{2,1,0:T(2,128)(2,1)S(1)} %collective-permute-done.1, bf16[1,2,4096]{2,1,0:T(2,128)(2,1)S(1)} %collective-permute-done, bf16[1,2,4096]{2,1,0:T(2,128)(2,1)} %param.7), kind=kLoop, calls=%fused_computation.36 | loop fusion | flops 65536 | bytes 131072 | tf_op jit(solution)/shard_map/concatenate | solution.py:103
  14.1 1.3 %collective-permute-start.2 = (bf16[4,2,4096]{2,1,0:T(2,128)(2,1)S(1)}, bf16[4,2,4096]{2,1,0:T(2,128)(2,1)S(1)}, u32[]{:S(2)}, u32[]{:S(2)}) collective-permute-start(bf16[4,2,4096]{2,1,0:T(2,128)(2,1)S(1)} %pad_maximum_fusion.6), channel_id=1, source_target_pairs={{0,5},{1,4},{2,7},{3,6},{4,1},{5,0},{6,3},{7,2},{8,13},{9,12},{10,... | collective-permute-start | bytes 196616 | tf_op jit(solution)/shard_map/ppermute | solution.py:20
  15.4 2.8 %collective-permute-done.2 = bf16[4,2,4096]{2,1,0:T(2,128)(2,1)S(1)} collective-permute-done((bf16[4,2,4096]{2,1,0:T(2,128)(2,1)S(1)}, bf16[4,2,4096]{2,1,0:T(2,128)(2,1)S(1)}, u32[]{:S(2)}, u32[]{:S(2)}) %collective-permute-start.2) | collective-permute-done | bytes 65568 | tf_op jit(solution)/shard_map/ppermute | solution.py:20
  18.8 5.1 %collective-permute-done.3 = bf16[8,2,4096]{2,1,0:T(2,128)(2,1)S(1)} collective-permute-done((bf16[8,2,4096]{2,1,0:T(2,128)(2,1)S(1)}, bf16[8,2,4096]{2,1,0:T(2,128)(2,1)S(1)}, u32[]{:S(2)}, u32[]{:S(2)}) %collective-permute-start.3) | collective-permute-done | bytes 131104 | tf_op jit(solution)/shard_map/ppermute | solution.py:20
  24.4 1.4 %collective-permute-done.4 = bf16[2,8,2,4096]{3,2,1,0:T(2,128)(2,1)S(1)} collective-permute-done((bf16[2,8,2,4096]{3,2,1,0:T(2,128)(2,1)S(1)}, bf16[2,8,2,4096]{3,2,1,0:T(2,128)(2,1)S(1)}, u32[]{:S(2)}, u32[]{:S(2)}) %collective-permute-start.4) | collective-permute-done | bytes 262176 | tf_op jit(solution)/shard_map/ppermute | solution.py:20
  25.8 1.3 %fusion.6 = (bf16[1,2,8,2,4096]{4,3,2,1,0:T(2,128)(2,1)S(1)}, bf16[1,2,8,2,4096]{4,3,2,1,0:T(2,128)(2,1)S(1)}) fusion(bf16[2,8,2,4096]{3,2,1,0:T(2,128)(2,1)S(1)} %collective-permute-done.4, pred[8]{0:T(512)(128)(4,1)} %constant.54.clone, bf16[1,8,2,4096]{3,2,1,0:T(2,128)(2,1)S(1)} %bitcast.91, bf16[1,8,2,4096]{3,2,1,0:T(2,128)(2,1)S(1)} %bitcast.88), kind=kLoop, calls=%fused_computation.23 | loop fusion | flops 393216 | bytes 1048584 | tf_op jit(solution)/shard_map/stack | solution.py:106
  27.2 0.7 pad_maximum_fusion
  28.1 3.2 %fusion.9 = f32[64,2048]{1,0:T(8,128)S(1)} fusion(bf16[1024,2048]{1,0:T(8,128)(2,1)} %param.9, bf16[64,4096]{1,0:T(8,128)(2,1)S(1)} %reshape.104.rows_ref, s32[]{:T(128)S(6)} %select_n.106), kind=kOutput, calls=%fused_computation.31 | convolution fusion | flops 268435456 | bytes 4849668 | tf_op jit(solution)/shard_map/dot_general | solution.py:111
  31.6 0.8 %fusion.11 = f32[64,2048]{1,0:T(8,128)S(1)} fusion(bf16[1024,2048]{1,0:T(8,128)(2,1)S(1)} %copy-done, bf16[64,4096]{1,0:T(8,128)(2,1)S(1)} %reshape.104.rows_ref, s32[]{:T(128)S(6)} %select_n.106), kind=kOutput, calls=%fused_computation.33 | convolution fusion | flops 268435456 | bytes 4849668 | tf_op jit(solution)/shard_map/dot_general | solution.py:111
  34.3 0.8 %gather_fusion.2 = bf16[8,2,2,2048]{3,2,1,0:T(2,128)(2,1)S(1)} fusion(bf16[2,8,2,2048]{3,2,1,0:T(2,128)(2,1)S(1)} %pad_maximum_fusion.5, s32[1024]{0:T(1024)S(1)} %get-tuple-element.27), kind=kCustom, calls=%fused_computation.2 | custom fusion | bytes 262176 | tf_op jit(solution)/shard_map/jit(_take)/gather | solution.py:125
  35.2 1.0 %collective-permute-start.6 = (bf16[32,2048]{1,0:T(8,128)(2,1)S(1)}, bf16[32,2048]{1,0:T(8,128)(2,1)S(1)}, u32[]{:S(2)}, u32[]{:S(2)}) collective-permute-start(bf16[32,2048]{1,0:T(8,128)(2,1)S(1)} %fusion.4), channel_id=1, source_target_pairs={{0,3},{1,2},{2,1},{3,0},{4,7},{5,6},{6,5},{7,4},{8,11},{9,10},{10,... | collective-permute-start | bytes 393224 | tf_op jit(solution)/shard_map/ppermute | solution.py:20
  36.2 2.3 %collective-permute-done.8 = bf16[32,2048]{1,0:T(8,128)(2,1)S(1)} collective-permute-done((bf16[32,2048]{1,0:T(8,128)(2,1)S(1)}, bf16[32,2048]{1,0:T(8,128)(2,1)S(1)}, u32[]{:S(2)}, u32[]{:S(2)}) %collective-permute-start.8) | collective-permute-done | bytes 131104 | tf_op jit(solution)/shard_map/ppermute | solution.py:20
  38.6 2.8 %collective-permute-done.6 = bf16[32,2048]{1,0:T(8,128)(2,1)S(1)} collective-permute-done((bf16[32,2048]{1,0:T(8,128)(2,1)S(1)}, bf16[32,2048]{1,0:T(8,128)(2,1)S(1)}, u32[]{:S(2)}, u32[]{:S(2)}) %collective-permute-start.6) | collective-permute-done | bytes 131104 | tf_op jit(solution)/shard_map/ppermute | solution.py:20
  41.6 0.7 gather_fusion.1
  43.0 0.7 broadcast_select_fusion.3
  43.8 3.6 %fusion.23 = f32[64,1024]{1,0:T(8,128)S(1)} fusion(bf16[1024,2048]{1,0:T(8,128)(2,1)} %param.9, bf16[32,2048]{1,0:T(8,128)(2,1)S(1)} %collective-permute-done.11, bf16[32,2048]{1,0:T(8,128)(2,1)S(1)} %get-tuple-element.8), kind=kOutput, calls=%fused_computation.78 | convolution fusion | flops 268959744 | bytes 4718592 | tf_op jit(solution)/shard_map/dot_general | solution.py:138
  47.4 1.4 %convolution_add_fusion = f32[64,1024]{1,0:T(8,128)S(1)} fusion(f32[64,1024]{1,0:T(8,128)S(1)} %fusion.23, bf16[1024,2048]{1,0:T(8,128)(2,1)S(1)} %copy-done.1, bf16[32,2048]{1,0:T(8,128)(2,1)S(1)} %collective-permute-done.10, bf16[32,2048]{1,0:T(8,128)(2,1)S(1)} %get-tuple-element.14), kind=kOutput, calls=%fused_computation.3 | convolution fusion | flops 269025280 | bytes 4980736 | tf_op jit(solution)/shard_map/dot_general | solution.py:137
  49.0 1.6 %collective-permute-start.12 = (f32[2,2,4,2,1024]{4,3,0,1,2:T(2,128)S(1)}, f32[2,2,4,2,1024]{4,3,0,1,2:T(2,128)S(1)}, u32[]{:S(2)}, u32[]{:S(2)}) collective-permute-start(f32[2,2,4,2,1024]{4,3,0,1,2:T(2,128)S(1)} %copy.25), channel_id=1, source_target_pairs={{0,4},{1,5},{2,6},{3,7},{4,0},{5,1},{6,2},{7,3},{8,12},{9,13},{10,... | collective-permute-start | bytes 393224 | tf_op jit(solution)/shard_map/ppermute | solution.py:20
  50.6 4.0 %collective-permute-done.12 = f32[2,2,4,2,1024]{4,3,0,1,2:T(2,128)S(1)} collective-permute-done((f32[2,2,4,2,1024]{4,3,0,1,2:T(2,128)S(1)}, f32[2,2,4,2,1024]{4,3,0,1,2:T(2,128)S(1)}, u32[]{:S(2)}, u32[]{:S(2)}) %collective-permute-start.12) | collective-permute-done | bytes 131104 | tf_op jit(solution)/shard_map/ppermute | solution.py:20
  54.7 1.8 %collective-permute-start.13 = (f32[2,2,2,2,1024]{4,3,0,1,2:T(2,128)S(1)}, f32[2,2,2,2,1024]{4,3,0,1,2:T(2,128)S(1)}, u32[]{:S(2)}, u32[]{:S(2)}) collective-permute-start(f32[2,2,2,2,1024]{4,3,0,1,2:T(2,128)S(1)} %slice.115), channel_id=1, source_target_pairs={{0,8},{1,9},{2,10},{3,11},{4,12},{5,13},{6,14},{7,15},{8,0},{9,1},... | collective-permute-start | bytes 196616 | tf_op jit(solution)/shard_map/ppermute | solution.py:20
  56.5 4.9 %shard_map.104.rest_0_ = bf16[4096,2048]{1,0:T(8,128)(2,1)} custom-call(bf16[64,4096]{1,0:T(8,128)(2,1)S(1)} %reshape.104.rows_ref, bf16[64,2048]{1,0:T(8,128)(2,1)S(1)} %pad_maximum_fusion.3.grad_ref), custom_call_target="tpu_custom_call" | custom-call | flops 536870912 | bytes 9175040 | tf_op jit(solution)/shard_map/pallas_call | solution.py:71
  61.8 4.7 %shard_map.105 = bf16[4096,2048]{1,0:T(8,128)(2,1)} custom-call(bf16[64,4096]{1,0:T(8,128)(2,1)S(1)} %reshape.104.rows_ref, bf16[64,2048]{1,0:T(8,128)(2,1)S(1)} %pad_maximum_fusion.3.grad_ref, bf16[4096,2048]{1,0:T(8,128)(2,1)} %shard_map.104.rest_0_), custom_call_target="tpu_custom_call", output_to_operand_aliasing={{}: (2, {})} | custom-call | flops 536870912 | bytes 9175040 | tf_op jit(solution)/shard_map/pallas_call | solution.py:71
  66.6 4.7 %shard_map.102.rest_0_ = bf16[4096,2048]{1,0:T(8,128)(2,1)} custom-call(bf16[64,4096]{1,0:T(8,128)(2,1)S(1)} %reshape.104.rows_ref, bf16[64,2048]{1,0:T(8,128)(2,1)S(1)} %pad_maximum_fusion.2.grad_ref), custom_call_target="tpu_custom_call" | custom-call | flops 536870912 | bytes 9175040 | tf_op jit(solution)/shard_map/pallas_call | solution.py:71
  71.3 1.7 %collective-permute-start.16 = (bf16[2,2,1024]{2,1,0:T(2,128)(2,1)S(1)}, bf16[2,2,1024]{2,1,0:T(2,128)(2,1)S(1)}, u32[]{:S(2)}, u32[]{:S(2)}) collective-permute-start(bf16[2,2,1024]{2,1,0:T(2,128)(2,1)S(1)} %fusion.14), channel_id=1, source_target_pairs={{0,1},{1,0},{2,3},{3,2},{4,5},{5,4},{6,7},{7,6},{8,9},{9,8},{10,11... | collective-permute-start | bytes 24584 | tf_op jit(solution)/shard_map/ppermute | solution.py:20
  73.0 4.7 %shard_map.103 = bf16[4096,2048]{1,0:T(8,128)(2,1)} custom-call(bf16[64,4096]{1,0:T(8,128)(2,1)S(1)} %reshape.104.rows_ref, bf16[64,2048]{1,0:T(8,128)(2,1)S(1)} %pad_maximum_fusion.2.grad_ref, bf16[4096,2048]{1,0:T(8,128)(2,1)} %shard_map.102.rest_0_), custom_call_target="tpu_custom_call", output_to_operand_aliasing={{}: (2, {})} | custom-call | flops 536870912 | bytes 9175040 | tf_op jit(solution)/shard_map/pallas_call | solution.py:71
  (70 shorter events, 7.0 us)
Async XLA Ops:
  0.6 8.2 %collective-permute-start = (bf16[1,2,4096]{2,1,0:T(2,128)(2,1)}, bf16[1,2,4096]{2,1,0:T(2,128)(2,1)S(1)}, u32[]{:S(2)}, u32[]{:S(2)}) collective-permute-start(bf16[1,2,4096]{2,1,0:T(2,128)(2,1)} %param.7), channel_id=1, source_target_pairs={{0,17},{1,16},{2,19},{3,18},{4,21},{5,20},{6,23},{7,22},{8,25},{9,... | collective-permute-start | bytes 49160 | tf_op jit(solution)/shard_map/ppermute | solution.py:20
  4.2 29.1 %collective-permute-start.9 = (bf16[16,2048]{1,0:T(8,128)(2,1)}, bf16[16,2048]{1,0:T(8,128)(2,1)S(1)}, u32[]{:S(2)}, u32[]{:S(2)}) collective-permute-start(bf16[16,2048]{1,0:T(8,128)(2,1)} %bitcast.92), channel_id=1, source_target_pairs={{0,3},{1,2},{2,1},{3,0},{4,7},{5,6},{6,5},{7,4},{8,11},{9,10},{10,... | collective-permute-start | bytes 196616 | tf_op jit(solution)/shard_map/ppermute | solution.py:20
  9.7 3.6 %collective-permute-start.1 = (bf16[2,2,4096]{2,1,0:T(2,128)(2,1)S(1)}, bf16[2,2,4096]{2,1,0:T(2,128)(2,1)S(1)}, u32[]{:S(2)}, u32[]{:S(2)}) collective-permute-start(bf16[2,2,4096]{2,1,0:T(2,128)(2,1)S(1)} %pad_maximum_fusion.7), channel_id=1, source_target_pairs={{0,9},{1,8},{2,11},{3,10},{4,13},{5,12},{6,15},{7,14},{8,1},{9,0},... | collective-permute-start | bytes 98312 | tf_op jit(solution)/shard_map/ppermute | solution.py:20
  14.1 4.2 %collective-permute-start.2 = (bf16[4,2,4096]{2,1,0:T(2,128)(2,1)S(1)}, bf16[4,2,4096]{2,1,0:T(2,128)(2,1)S(1)}, u32[]{:S(2)}, u32[]{:S(2)}) collective-permute-start(bf16[4,2,4096]{2,1,0:T(2,128)(2,1)S(1)} %pad_maximum_fusion.6), channel_id=1, source_target_pairs={{0,5},{1,4},{2,7},{3,6},{4,1},{5,0},{6,3},{7,2},{8,13},{9,12},{10,... | collective-permute-start | bytes 196616 | tf_op jit(solution)/shard_map/ppermute | solution.py:20
  18.3 5.6 %collective-permute-start.3 = (bf16[8,2,4096]{2,1,0:T(2,128)(2,1)S(1)}, bf16[8,2,4096]{2,1,0:T(2,128)(2,1)S(1)}, u32[]{:S(2)}, u32[]{:S(2)}) collective-permute-start(bf16[8,2,4096]{2,1,0:T(2,128)(2,1)S(1)} %constant_dynamic-update-slice_fusion), channel_id=1, source_target_pairs={{0,3},{1,2},{2,1},{3,0},{4,7},{5,6},{6,5},{7,4},{8,11},{9,10},{10,... | collective-permute-start | bytes 393224 | tf_op jit(solution)/shard_map/ppermute | solution.py:20
  24.2 1.6 %collective-permute-start.4 = (bf16[2,8,2,4096]{3,2,1,0:T(2,128)(2,1)S(1)}, bf16[2,8,2,4096]{3,2,1,0:T(2,128)(2,1)S(1)}, u32[]{:S(2)}, u32[]{:S(2)}) collective-permute-start(bf16[2,8,2,4096]{3,2,1,0:T(2,128)(2,1)S(1)} %pad_maximum_fusion.1), channel_id=1, source_target_pairs={{0,1},{1,0},{2,3},{3,2},{4,5},{5,4},{6,7},{7,6},{8,9},{9,8},{10,11... | collective-permute-start | bytes 786440 | tf_op jit(solution)/shard_map/ppermute | solution.py:20
  28.1 3.5 %copy-start = (bf16[1024,2048]{1,0:T(8,128)(2,1)S(1)}, bf16[1024,2048]{1,0:T(8,128)(2,1)}, u32[]{:S(2)}) copy-start(bf16[1024,2048]{1,0:T(8,128)(2,1)} %param.8) | copy-start | bytes 12582916
  31.3 2.0 %copy-start.2 = (bf16[1,16,2048]{2,1,0:T(8,128)(2,1)S(1)}, bf16[1,16,2048]{2,1,0:T(8,128)(2,1)}, u32[]{:S(2)}) copy-start(bf16[1,16,2048]{2,1,0:T(8,128)(2,1)} %param.10) | copy-start | bytes 196612
  31.4 1.6 %collective-permute-start.7 = (f32[32,2048]{1,0:T(8,128)S(1)}, f32[32,2048]{1,0:T(8,128)S(1)}, u32[]{:S(2)}, u32[]{:S(2)}) collective-permute-start(f32[32,2048]{1,0:T(8,128)S(1)} %slice.107), channel_id=1, source_target_pairs={{0,1},{1,0},{2,3},{3,2},{4,5},{5,4},{6,7},{7,6},{8,9},{9,8},{10,11... | collective-permute-start | bytes 786440 | tf_op jit(solution)/shard_map/ppermute | solution.py:20
  32.4 1.6 %collective-permute-start.5 = (f32[32,2048]{1,0:T(8,128)S(1)}, f32[32,2048]{1,0:T(8,128)S(1)}, u32[]{:S(2)}, u32[]{:S(2)}) collective-permute-start(f32[32,2048]{1,0:T(8,128)S(1)} %slice.103), channel_id=1, source_target_pairs={{0,1},{1,0},{2,3},{3,2},{4,5},{5,4},{6,7},{7,6},{8,9},{9,8},{10,11... | collective-permute-start | bytes 786440 | tf_op jit(solution)/shard_map/ppermute | solution.py:20
  33.0 5.5 %collective-permute-start.8 = (bf16[32,2048]{1,0:T(8,128)(2,1)S(1)}, bf16[32,2048]{1,0:T(8,128)(2,1)S(1)}, u32[]{:S(2)}, u32[]{:S(2)}) collective-permute-start(bf16[32,2048]{1,0:T(8,128)(2,1)S(1)} %fusion.3), channel_id=1, source_target_pairs={{0,3},{1,2},{2,1},{3,0},{4,7},{5,6},{6,5},{7,4},{8,11},{9,10},{10,... | collective-permute-start | bytes 393224 | tf_op jit(solution)/shard_map/ppermute | solution.py:20
  35.2 6.1 %collective-permute-start.6 = (bf16[32,2048]{1,0:T(8,128)(2,1)S(1)}, bf16[32,2048]{1,0:T(8,128)(2,1)S(1)}, u32[]{:S(2)}, u32[]{:S(2)}) collective-permute-start(bf16[32,2048]{1,0:T(8,128)(2,1)S(1)} %fusion.4), channel_id=1, source_target_pairs={{0,3},{1,2},{2,1},{3,0},{4,7},{5,6},{6,5},{7,4},{8,11},{9,10},{10,... | collective-permute-start | bytes 393224 | tf_op jit(solution)/shard_map/ppermute | solution.py:20
  42.4 5.0 %copy-start.1 = (bf16[1024,2048]{1,0:T(8,128)(2,1)S(1)}, bf16[1024,2048]{1,0:T(8,128)(2,1)}, u32[]{:S(2)}) copy-start(bf16[1024,2048]{1,0:T(8,128)(2,1)} %param.8) | copy-start | bytes 12582916
  42.4 1.4 %collective-permute-start.11 = (bf16[32,2048]{1,0:T(8,128)(2,1)S(1)}, bf16[32,2048]{1,0:T(8,128)(2,1)S(1)}, u32[]{:S(2)}, u32[]{:S(2)}) collective-permute-start(bf16[32,2048]{1,0:T(8,128)(2,1)S(1)} %get-tuple-element.8), channel_id=1, source_target_pairs={{0,1},{1,0},{2,3},{3,2},{4,5},{5,4},{6,7},{7,6},{8,9},{9,8},{10,11... | collective-permute-start | bytes 393224 | tf_op jit(solution)/shard_map/ppermute | solution.py:20
  42.6 4.8 %collective-permute-start.10 = (bf16[32,2048]{1,0:T(8,128)(2,1)S(1)}, bf16[32,2048]{1,0:T(8,128)(2,1)S(1)}, u32[]{:S(2)}, u32[]{:S(2)}) collective-permute-start(bf16[32,2048]{1,0:T(8,128)(2,1)S(1)} %get-tuple-element.14), channel_id=1, source_target_pairs={{0,1},{1,0},{2,3},{3,2},{4,5},{5,4},{6,7},{7,6},{8,9},{9,8},{10,11... | collective-permute-start | bytes 393224 | tf_op jit(solution)/shard_map/ppermute | solution.py:20
  49.0 5.6 %collective-permute-start.12 = (f32[2,2,4,2,1024]{4,3,0,1,2:T(2,128)S(1)}, f32[2,2,4,2,1024]{4,3,0,1,2:T(2,128)S(1)}, u32[]{:S(2)}, u32[]{:S(2)}) collective-permute-start(f32[2,2,4,2,1024]{4,3,0,1,2:T(2,128)S(1)} %copy.25), channel_id=1, source_target_pairs={{0,4},{1,5},{2,6},{3,7},{4,0},{5,1},{6,2},{7,3},{8,12},{9,13},{10,... | collective-permute-start | bytes 393224 | tf_op jit(solution)/shard_map/ppermute | solution.py:20
  54.7 6.7 %collective-permute-start.13 = (f32[2,2,2,2,1024]{4,3,0,1,2:T(2,128)S(1)}, f32[2,2,2,2,1024]{4,3,0,1,2:T(2,128)S(1)}, u32[]{:S(2)}, u32[]{:S(2)}) collective-permute-start(f32[2,2,2,2,1024]{4,3,0,1,2:T(2,128)S(1)} %slice.115), channel_id=1, source_target_pairs={{0,8},{1,9},{2,10},{3,11},{4,12},{5,13},{6,14},{7,15},{8,0},{9,1},... | collective-permute-start | bytes 196616 | tf_op jit(solution)/shard_map/ppermute | solution.py:20
  61.4 5.0 %collective-permute-start.14 = (f32[2,2,1,2,1024]{4,3,0,1,2:T(2,128)S(1)}, f32[2,2,1,2,1024]{4,3,0,1,2:T(2,128)S(1)}, u32[]{:S(2)}, u32[]{:S(2)}) collective-permute-start(f32[2,2,1,2,1024]{4,3,0,1,2:T(2,128)S(1)} %slice.117), channel_id=1, source_target_pairs={{0,16},{1,17},{2,18},{3,19},{4,20},{5,21},{6,22},{7,23},{8,24},{9,... | collective-permute-start | bytes 98312 | tf_op jit(solution)/shard_map/ppermute | solution.py:20
  66.5 4.8 %collective-permute-start.15 = (bf16[2,2,1024]{2,1,0:T(2,128)(2,1)S(1)}, bf16[2,2,1024]{2,1,0:T(2,128)(2,1)S(1)}, u32[]{:S(2)}, u32[]{:S(2)}) collective-permute-start(bf16[2,2,1024]{2,1,0:T(2,128)(2,1)S(1)} %get-tuple-element.26), channel_id=1, source_target_pairs={{0,3},{1,2},{2,1},{3,0},{4,7},{5,6},{6,5},{7,4},{8,11},{9,10},{10,... | collective-permute-start | bytes 24584 | tf_op jit(solution)/shard_map/ppermute | solution.py:20
  71.3 6.4 %collective-permute-start.16 = (bf16[2,2,1024]{2,1,0:T(2,128)(2,1)S(1)}, bf16[2,2,1024]{2,1,0:T(2,128)(2,1)S(1)}, u32[]{:S(2)}, u32[]{:S(2)}) collective-permute-start(bf16[2,2,1024]{2,1,0:T(2,128)(2,1)S(1)} %fusion.14), channel_id=1, source_target_pairs={{0,1},{1,0},{2,3},{3,2},{4,5},{5,4},{6,7},{7,6},{8,9},{9,8},{10,11... | collective-permute-start | bytes 24584 | tf_op jit(solution)/shard_map/ppermute | solution.py:20

commit v4 on v3

v4 whole, which is shorter than its diff:
```python
import functools

import jax
import jax.numpy as jnp
from jax import lax
from jax.experimental import pallas as pl
from jax.experimental.pallas import tpu as pltpu
from jax.sharding import PartitionSpec as P


F32 = jnp.float32
BF16 = jnp.bfloat16
VMEM = pl.BlockSpec(memory_space=pltpu.VMEM)
HBM = pl.BlockSpec(memory_space=pltpu.HBM)
COLS = (((1,), (1,)), ((), ()))
DOWN = (((0,), (0,)), ((), ()))
PIECES = 4


def swap(value, tp_mask, dp_mask):
    n_tp, n_dp = lax.axis_size("tp"), lax.axis_size("dp")
    pairs = [(t * n_dp + r, (t ^ tp_mask) * n_dp + (r ^ dp_mask)) for t in range(n_tp) for r in range(n_dp)]
    return lax.ppermute(value, ("tp", "dp"), pairs)


def bits_of(size):
    assert size & (size - 1) == 0
    return [1 << k for k in reversed(range(size.bit_length() - 1))]


def odd(value):
    return value.bit_count() % 2


def swish_parts(gate_pre):
    s = jax.nn.sigmoid(gate_pre)
    return gate_pre * s, s * (1.0 + gate_pre * (1.0 - s))


def hold_kernel(in_ref, out_ref):
    out_ref[...] = in_ref[...]


def hold(value):
    return pl.pallas_call(
        hold_kernel,
        in_specs=[VMEM],
        out_specs=VMEM,
        out_shape=jax.ShapeDtypeStruct(value.shape, value.dtype),
        compiler_params=pltpu.CompilerParams(vmem_limit_bytes=1 << 20),
        cost_estimate=pl.CostEstimate(flops=0, bytes_accessed=value.size, transcendentals=0),
    )(value)


def pieces_of(weight_ref, buf, sem):
    tall = buf.shape[1]
    return [
        pltpu.make_async_copy(weight_ref.at[pl.ds(i * tall, tall), :], buf.at[i], sem.at[i]) for i in range(PIECES)
    ]


def multiply(feats_ref, copies, buf, keep_ref, send_ref):
    depth = buf.shape[1] * PIECES
    half = keep_ref.shape[0]
    first = lax.axis_index("dp") * depth
    for i, copy in enumerate(copies):
        copy.wait()
        at = pl.multiple_of(first + i * buf.shape[1], buf.shape[1])
        out = jnp.dot(feats_ref[:, pl.ds(at, buf.shape[1])], buf[i], preferred_element_type=F32)
        keep_ref[...] = out[:half] if i == 0 else keep_ref[...] + out[:half]
        send_ref[...] = out[half:] if i == 0 else send_ref[...] + out[half:]


def gather_kernel(part_ref, far_ref, weight_ref, feats_ref, keep_ref, send_ref, buf, sem):
    copies = pieces_of(weight_ref, buf, sem)
    for copy in copies:
        copy.start()
    _, n_tp, rt, _ = part_ref.shape
    for core in range(2):
        for x in range(2):
            for k in range(n_tp):
                source = part_ref if odd(k) == core else far_ref
                row = ((core * 2 + x) * n_tp + k) * rt
                feats_ref[row : row + rt, :] = source[x, k]
    multiply(feats_ref, copies, buf, keep_ref, send_ref)


def ahead_kernel(feats_ref, weight_ref, keep_ref, send_ref, buf, sem):
    copies = pieces_of(weight_ref, buf, sem)
    for copy in copies:
        copy.start()
    multiply(feats_ref, copies, buf, keep_ref, send_ref)


def stream(kernel, args, weight, outs, flops):
    depth, width = weight.shape
    return pl.pallas_call(
        kernel,
        in_specs=[VMEM] * len(args) + [HBM],
        out_specs=[VMEM] * len(outs),
        out_shape=outs,
        scratch_shapes=[pltpu.VMEM((PIECES, depth // PIECES, width), BF16), pltpu.SemaphoreType.DMA((PIECES,))],
        compiler_params=pltpu.CompilerParams(vmem_limit_bytes=52 << 20),
        cost_estimate=pl.CostEstimate(flops=flops, bytes_accessed=2 * weight.size, transcendentals=0),
    )(*args, weight)


def gather_ahead(part, far, weight):
    _, n_tp, rt, d_model = part.shape
    count, width = 4 * n_tp * rt, weight.shape[1]
    half = jax.ShapeDtypeStruct((count // 2, width), F32)
    if n_tp <= 16:
        feats = jax.ShapeDtypeStruct((count, d_model), BF16)
        return stream(gather_kernel, (part, far), weight, [feats, half, half], 2 * count * weight.size)
    mask = jnp.array([odd(k) == 1 for k in range(n_tp)])[None, :, None, None]
    feats = jnp.stack([jnp.where(mask, far, part), jnp.where(mask, part, far)]).reshape(count, d_model)
    return feats, *ahead(feats, weight)


def ahead(feats, weight):
    half = jax.ShapeDtypeStruct((feats.shape[0] // 2, weight.shape[1]), F32)
    return stream(ahead_kernel, (feats,), weight, [half, half], 2 * feats.shape[0] * weight.size)


def back_kernel(*refs):
    grad_ref, weight_ref, out_ref, buf, sem = refs[0], *refs[-4:]
    copies = pieces_of(weight_ref, buf, sem)
    for copy in copies:
        copy.start()
    tall = buf.shape[1]
    for i, copy in enumerate(copies):
        copy.wait()
        out = lax.dot_general(grad_ref[...], buf[i], COLS, preferred_element_type=F32)
        at = slice(i * tall, (i + 1) * tall)
        out_ref[:, at] = out if len(refs) == 5 else refs[1][:, at] + out


def back(grad, weight, start=None):
    out = jax.ShapeDtypeStruct((grad.shape[0], weight.shape[0]), F32)
    args = (grad,) if start is None else (grad, start)
    return stream(back_kernel, args, weight, [out], 2 * grad.shape[0] * weight.size)[0]


def outer_kernel(rows_ref, grad_ref, *rest, base, scale):
    out_ref, buf, sem = rest[-3:]
    total, width = buf.shape
    wide = min(512, width)
    tall = min(512, total)
    sizes = [tall // 2] * 2 + [tall] * (total // tall - 1)
    copies = []
    top = 0
    for i, size in enumerate(sizes):
        for at in range(0, width, wide):
            acc = lax.dot_general(
                rows_ref[:, base + top : base + top + size],
                grad_ref[:, at : at + wide],
                DOWN,
                preferred_element_type=F32,
            )
            buf[top : top + size, at : at + wide] = (acc * scale).astype(BF16)
        source, target = buf.at[pl.ds(top, size), :], out_ref.at[pl.ds(base + top, size), :]
        copies.append(pltpu.make_async_copy(source, target, sem.at[i]))
        copies[-1].start()
        top += size
    for copy in copies:
        copy.wait()


def outer(rows, grad, scale, begin, share, whole=None):
    count, d_model = rows.shape
    width = grad.shape[1]
    part = d_model // share
    kernel = functools.partial(outer_kernel, base=begin * part, scale=scale)
    args = (rows, grad) if whole is None else (rows, grad, whole)
    return pl.pallas_call(
        kernel,
        in_specs=[VMEM, VMEM] + [HBM] * (len(args) - 2),
        out_specs=HBM,
        out_shape=jax.ShapeDtypeStruct((d_model, width), BF16),
        input_output_aliases={2: 0} if whole is not None else {},
        scratch_shapes=[pltpu.VMEM((part, width), BF16), pltpu.SemaphoreType.DMA((part // min(512, part) + 1,))],
        compiler_params=pltpu.CompilerParams(vmem_limit_bytes=32 << 20),
        cost_estimate=pl.CostEstimate(
            flops=2 * count * part * width,
            bytes_accessed=2 * part * width + 2 * count * (d_model + width),
            transcendentals=0,
        ),
    )(*args)


def shards(tokens, gate_weight, up_weight, cotangent):
    n_tp, n_dp = lax.axis_size("tp"), lax.axis_size("dp")
    assert n_dp == 4
    t, r = lax.axis_index("tp"), lax.axis_index("dp")
    _, rt, d_model = tokens.shape
    depth, width = gate_weight.shape
    rows = rt * n_tp
    order = t ^ jnp.arange(n_tp)

    part = hold(tokens)
    for i, bit in enumerate(bits_of(n_tp)):
        near = swap(part if i else tokens, bit, 1)
        part = jnp.stack([part, near], axis=1).reshape(-1, rt, d_model)
    part = jnp.stack([part, swap(part, 0, 3)])
    far = swap(part, 0, 1)
    feats, gate_keep, gate_send = gather_ahead(part, far, gate_weight)
    up_keep, up_send = ahead(feats, up_weight)

    def partial(keep, send):
        return (keep + swap(send, 0, 1)).astype(BF16)

    def summed(half):
        other = swap(half, 0, 3)
        other = jnp.concatenate([other[rows:], other[:rows]])
        return half.astype(F32) + other.astype(F32)

    half_gate, half_up = partial(gate_keep, gate_send), partial(up_keep, up_send)
    gate_pre = summed(half_gate)
    up_pre = summed(half_up)

    cot = swap(cotangent[0], 0, 3)
    near, cot, _ = lax.optimization_barrier((cotangent[0], cot, half_up))
    cot = jnp.stack([near, cot]).reshape(2, n_tp, rt, width)
    cot = jnp.take(cot, order, axis=1).reshape(2 * rows, width)

    act, slope = swish_parts(gate_pre)
    grad_hidden = cot.astype(F32)
    d_up = (grad_hidden * act).astype(BF16)
    d_up, act, slope = lax.optimization_barrier((d_up, act, slope))
    d_up = jnp.concatenate([d_up, swap(d_up, 0, 1)])
    total = back(d_up, up_weight)
    hidden = (act * up_pre)[:rows].astype(BF16).reshape(n_tp, rt, width)
    hidden = jnp.take(hidden, order, axis=0).reshape(1, rows, width)
    d_gate = (grad_hidden * up_pre * slope).astype(BF16)
    d_gate = jnp.concatenate([d_gate, swap(d_gate, 0, 1)])
    total = back(d_gate, gate_weight, total)

    total = total.reshape(2, 2, n_tp, rt, depth)
    for bit in reversed(bits_of(n_tp)):
        total = total.reshape(2, 2, -1, 2, rt, depth)
        total = total[:, :, :, 0] + swap(total[:, :, :, 1], bit, 0)
    total = total[:, :, 0]
    total = jnp.stack([total[:, 0], swap(total[:, 1], 0, 3)], axis=1)
    total = jnp.stack([total[0], swap(total[1], 0, 1)])
    total = [total[0, 0], total[1, 0], total[1, 1], total[0, 1]]
    for bit in (1, 2):
        total = [jnp.where(r & bit != 0, total[m ^ bit], total[m]) for m in range(n_dp)]
    grad_tokens = jnp.concatenate([v.astype(BF16) for v in total], axis=1)[None]

    inverse = 1.0 / n_dp
    grad_up = outer(feats, d_up, inverse, 0, 2)
    grad_up = outer(feats, d_up, inverse, 1, 2, grad_up)
    grad_gate = outer(feats, d_gate, inverse, 0, 2)
    grad_gate = outer(feats, d_gate, inverse, 1, 2, grad_gate)
    return hidden, grad_tokens, grad_gate, grad_up


def solution(mesh):
    in_specs = (P("dp", "tp", None), P("dp", "tp"), P("dp", "tp"), P("dp", None, "tp"))
    out_specs = (P("dp", None, "tp"), P("dp", "tp", None), P(None, "tp"), P(None, "tp"))

    return jax.shard_map(shards, mesh=mesh, in_specs=in_specs, out_specs=out_specs, check_vma=False)
```

time: 78.9 us -> 76.6 us (0.971)
  Pallas kernels: 19 us -> 29 us
  matrix products: 8.99 us -> 0 us
  starting transfers between devices: 16.2 us -> 23.4 us
  waiting for transfers between devices: 21.7 us -> 16.2 us
  other arithmetic: 6.74 us -> 2.77 us
    pallas_call x0 -> x5, Pallas kernels: none -> 12.9 us  [the longest x4 12.9 us: stream(): pl.pallas_call(kernel, in_specs=[VMEM] * len(args) + [HBM], out_specs=[VM...]
    dot_general x4 -> x0, matrix products: 8.99 us -> none  [the longest x2 4.02 us: partial(): out = jnp.dot(own, weight, preferred_element_type=F32)]
    ppermute x17, starting transfers between devices: 16.2 us -> 23.4 us  [swap(): return lax.ppermute(value, ('tp', 'dp'), pairs)]
    ppermute x17, waiting for transfers between devices: 21.7 us -> 16.2 us  [swap(): return lax.ppermute(value, ('tp', 'dp'), pairs)]
    pallas_call x4, Pallas kernels: 19 us -> 16.1 us  [outer(): pl.pallas_call(kernel, in_specs=[VMEM, VMEM] + [HBM] * (len(args) - 2), o...]
    another operation x3 -> x4, other arithmetic: 2.07 us -> 0.34 us  [the longest x3 0.33 us: shards(): part = jnp.stack([part, near], axis=1).reshape(-1, rt, d_model)]
    concatenate x3 -> x0, other arithmetic: 1.6 us -> none  [the longest x2 1.58 us: shards(): part = jnp.concatenate([part, swap(part, bit, 1)])]
    gather x6 -> x5, local copies, waits for them, and re-layouts: 2.97 us -> 1.67 us  [the longest x3 0.95 us: shards(): cot = jnp.take(cot, order, axis=1).reshape(2 * rows, width)]
  transfers between devices with their start and end apart: 17 -> 17, of which waited for: 10 -> 8; matrix products, arithmetic and copies ran while one was open for 22% -> 5% of each run, Pallas kernels for 24% -> 33%
where the time goes in v4:
time: 76.6 us; the launch traced here: 76.4 us
  Pallas kernels  29 us (38%)
  starting transfers between devices  23.4 us (31%)
  waiting for transfers between devices  16.2 us (21%)
  local copies, waits for them, and re-layouts  4.12 us (5%)
  other arithmetic  2.77 us (4%)
  between operations  0.96 us (1%)
    ppermute x17, starting transfers between devices, swap(): return lax.ppermute(value, ('tp', 'dp'), pairs)  23.4 us
    ppermute x17, waiting for transfers between devices, swap(): return lax.ppermute(value, ('tp', 'dp'), pairs)  16.2 us
    pallas_call x4, Pallas kernels, outer(): pl.pallas_call(kernel, in_specs=[VMEM, VMEM] + [HBM] * (len(args) - 2), o...  16.1 us
    pallas_call x4, Pallas kernels, stream(): pl.pallas_call(kernel, in_specs=[VMEM] * len(args) + [HBM], out_specs=[VM...  12.9 us
  transfers between devices with their start and end apart: 17, of which 8 were waited for; matrix products, arithmetic and copies ran while one was open for 5% of the time, Pallas kernels for 33%

profile of v4, /device:TPU:0, one launch (start us, length us, event | category | flops | bytes accessed | tf_op | source)
XLA Modules:
  0.0 76.4 jit_solution(6711022615383631494)
XLA Ops:
  0.6 3.6 %collective-permute-start.1 = (bf16[1,2,4096]{2,1,0:T(2,128)(2,1)}, bf16[1,2,4096]{2,1,0:T(2,128)(2,1)S(1)}, u32[]{:S(2)}, u32[]{:S(2)}) collective-permute-start(bf16[1,2,4096]{2,1,0:T(2,128)(2,1)} %in_ref.1), channel_id=1, source_target_pairs={{0,17},{1,16},{2,19},{3,18},{4,21},{5,20},{6,23},{7,22},{8,25},{9,... | collective-permute-start | bytes 49160 | tf_op jit(solution)/shard_map/ppermute | solution.py:23
  4.2 0.7 copy-done
  5.0 0.9 %collective-permute-done.1 = bf16[1,2,4096]{2,1,0:T(2,128)(2,1)S(1)} collective-permute-done((bf16[1,2,4096]{2,1,0:T(2,128)(2,1)}, bf16[1,2,4096]{2,1,0:T(2,128)(2,1)S(1)}, u32[]{:S(2)}, u32[]{:S(2)}) %collective-permute-start.1) | collective-permute-done | bytes 16416 | tf_op jit(solution)/shard_map/ppermute | solution.py:23
  5.9 2.0 %collective-permute-start.2 = (bf16[2,2,4096]{2,1,0:T(2,128)(2,1)S(1)}, bf16[2,2,4096]{2,1,0:T(2,128)(2,1)S(1)}, u32[]{:S(2)}, u32[]{:S(2)}) collective-permute-start(bf16[2,2,4096]{2,1,0:T(2,128)(2,1)S(1)} %get-tuple-element.38), channel_id=1, source_target_pairs={{0,9},{1,8},{2,11},{3,10},{4,13},{5,12},{6,15},{7,14},{8,1},{9,0},... | collective-permute-start | bytes 98312 | tf_op jit(solution)/shard_map/ppermute | solution.py:23
  7.9 1.6 %collective-permute-done.2 = bf16[2,2,4096]{2,1,0:T(2,128)(2,1)S(1)} collective-permute-done((bf16[2,2,4096]{2,1,0:T(2,128)(2,1)S(1)}, bf16[2,2,4096]{2,1,0:T(2,128)(2,1)S(1)}, u32[]{:S(2)}, u32[]{:S(2)}) %collective-permute-start.2) | collective-permute-done | bytes 32800 | tf_op jit(solution)/shard_map/ppermute | solution.py:23
  9.6 1.8 %collective-permute-start.3 = (bf16[4,2,4096]{2,1,0:T(2,128)(2,1)S(1)}, bf16[4,2,4096]{2,1,0:T(2,128)(2,1)S(1)}, u32[]{:S(2)}, u32[]{:S(2)}) collective-permute-start(bf16[4,2,4096]{2,1,0:T(2,128)(2,1)S(1)} %bitcast.112), channel_id=1, source_target_pairs={{0,5},{1,4},{2,7},{3,6},{4,1},{5,0},{6,3},{7,2},{8,13},{9,12},{10,... | collective-permute-start | bytes 196616 | tf_op jit(solution)/shard_map/ppermute | solution.py:23
  11.4 2.2 %collective-permute-done.3 = bf16[4,2,4096]{2,1,0:T(2,128)(2,1)S(1)} collective-permute-done((bf16[4,2,4096]{2,1,0:T(2,128)(2,1)S(1)}, bf16[4,2,4096]{2,1,0:T(2,128)(2,1)S(1)}, u32[]{:S(2)}, u32[]{:S(2)}) %collective-permute-start.3) | collective-permute-done | bytes 65568 | tf_op jit(solution)/shard_map/ppermute | solution.py:23
  13.9 1.9 %collective-permute-start.4 = (bf16[8,2,4096]{2,1,0:T(2,128)(2,1)S(1)}, bf16[8,2,4096]{2,1,0:T(2,128)(2,1)S(1)}, u32[]{:S(2)}, u32[]{:S(2)}) collective-permute-start(bf16[8,2,4096]{2,1,0:T(2,128)(2,1)S(1)} %bitcast.110), channel_id=1, source_target_pairs={{0,3},{1,2},{2,1},{3,0},{4,7},{5,6},{6,5},{7,4},{8,11},{9,10},{10,... | collective-permute-start | bytes 393224 | tf_op jit(solution)/shard_map/ppermute | solution.py:23
  15.8 3.6 %collective-permute-done.4 = bf16[8,2,4096]{2,1,0:T(2,128)(2,1)S(1)} collective-permute-done((bf16[8,2,4096]{2,1,0:T(2,128)(2,1)S(1)}, bf16[8,2,4096]{2,1,0:T(2,128)(2,1)S(1)}, u32[]{:S(2)}, u32[]{:S(2)}) %collective-permute-start.4) | collective-permute-done | bytes 131104 | tf_op jit(solution)/shard_map/ppermute | solution.py:23
  20.2 2.0 %collective-permute-start = (bf16[16,2048]{1,0:T(8,128)(2,1)}, bf16[16,2048]{1,0:T(8,128)(2,1)S(1)}, u32[]{:S(2)}, u32[]{:S(2)}) collective-permute-start(bf16[16,2048]{1,0:T(8,128)(2,1)} %bitcast.115), channel_id=1, source_target_pairs={{0,3},{1,2},{2,1},{3,0},{4,7},{5,6},{6,5},{7,4},{8,11},{9,10},{10,... | collective-permute-start | bytes 196616 | tf_op jit(solution)/shard_map/ppermute | solution.py:23
  22.2 2.5 %shard_map.76 = (bf16[64,4096]{1,0:T(8,128)(2,1)S(1)}, f32[32,2048]{1,0:T(8,128)S(1)}, f32[32,2048]{1,0:T(8,128)S(1)}) custom-call(bf16[2,8,2,4096]{3,2,1,0:T(2,128)(2,1)S(1)} %pad_maximum_fusion.part_ref, bf16[2,8,2,4096]{3,2,1,0:T(2,128)(2,1)S(1)} %collective-permute-done.5.far_ref, bf16[1024,2048]{1,0:T(8,128)(2,1)} %refs_2_.1), custom_call_target="tpu_custom_call" | custom-call | flops 268435456 | bytes 4194304 | tf_op jit(solution)/shard_map/pallas_call | solution.py:97
  25.2 2.5 %shard_map.77 = (f32[32,2048]{1,0:T(8,128)S(1)}, f32[32,2048]{1,0:T(8,128)S(1)}) custom-call(bf16[64,4096]{1,0:T(8,128)(2,1)S(1)} %get-tuple-element.14.feats_ref.rows_ref, bf16[1024,2048]{1,0:T(8,128)(2,1)} %refs_1_.1), custom_call_target="tpu_custom_call" | custom-call | flops 268435456 | bytes 4194304 | tf_op jit(solution)/shard_map/pallas_call | solution.py:97
  28.3 1.2 %collective-permute-start.8 = (bf16[32,2048]{1,0:T(8,128)(2,1)S(1)}, bf16[32,2048]{1,0:T(8,128)(2,1)S(1)}, u32[]{:S(2)}, u32[]{:S(2)}) collective-permute-start(bf16[32,2048]{1,0:T(8,128)(2,1)S(1)} %add_convert_fusion), channel_id=1, source_target_pairs={{0,3},{1,2},{2,1},{3,0},{4,7},{5,6},{6,5},{7,4},{8,11},{9,10},{10,... | collective-permute-start | bytes 393224 | tf_op jit(solution)/shard_map/ppermute | solution.py:23
  29.5 1.4 %collective-permute-start.9 = (bf16[32,2048]{1,0:T(8,128)(2,1)S(1)}, bf16[32,2048]{1,0:T(8,128)(2,1)S(1)}, u32[]{:S(2)}, u32[]{:S(2)}) collective-permute-start(bf16[32,2048]{1,0:T(8,128)(2,1)S(1)} %add_convert_fusion.1), channel_id=1, source_target_pairs={{0,3},{1,2},{2,1},{3,0},{4,7},{5,6},{6,5},{7,4},{8,11},{9,10},{10,... | collective-permute-start | bytes 393224 | tf_op jit(solution)/shard_map/ppermute | solution.py:23
  30.9 0.9 %stack.54 = bf16[1,8,2,2048]{3,2,1,0:T(2,128)(2,1)S(1)} reshape(bf16[16,2048]{1,0:T(8,128)(2,1)} %bitcast.116) | data formatting | bytes 131072 | tf_op jit(solution)/shard_map/stack | solution.py:223
  32.0 0.8 %gather_fusion = bf16[8,2,2,2048]{3,2,1,0:T(2,128)(2,1)S(1)} fusion(bf16[2,8,2,2048]{3,2,1,0:T(2,128)(2,1)S(1)} %pad_maximum_fusion.3, s32[1024]{0:T(1024)S(1)} %pad_clamp_fusion), kind=kCustom, calls=%fused_computation | custom fusion | bytes 262176 | tf_op jit(solution)/shard_map/jit(_take)/gather | solution.py:224
  33.0 0.8 %collective-permute-done.8 = bf16[32,2048]{1,0:T(8,128)(2,1)S(1)} collective-permute-done((bf16[32,2048]{1,0:T(8,128)(2,1)S(1)}, bf16[32,2048]{1,0:T(8,128)(2,1)S(1)}, u32[]{:S(2)}, u32[]{:S(2)}) %collective-permute-start.8) | collective-permute-done | bytes 131104 | tf_op jit(solution)/shard_map/ppermute | solution.py:23
  34.0 2.6 %collective-permute-done.9 = bf16[32,2048]{1,0:T(8,128)(2,1)S(1)} collective-permute-done((bf16[32,2048]{1,0:T(8,128)(2,1)S(1)}, bf16[32,2048]{1,0:T(8,128)(2,1)S(1)}, u32[]{:S(2)}, u32[]{:S(2)}) %collective-permute-start.9) | collective-permute-done | bytes 131104 | tf_op jit(solution)/shard_map/ppermute | solution.py:23
  37.3 1.0 %collective-permute-done.11 = bf16[32,2048]{1,0:T(8,128)(2,1)S(1)} collective-permute-done((bf16[32,2048]{1,0:T(8,128)(2,1)S(1)}, bf16[32,2048]{1,0:T(8,128)(2,1)S(1)}, u32[]{:S(2)}, u32[]{:S(2)}) %collective-permute-start.11) | collective-permute-done | bytes 131104 | tf_op jit(solution)/shard_map/ppermute | solution.py:23
  38.4 4.0 %shard_map.78.refs_1_ = f32[64,1024]{1,0:T(8,128)S(1)} custom-call(bf16[64,2048]{1,0:T(8,128)(2,1)S(1)} %constant_dynamic-update-slice_fusion.refs_0_.grad_ref, bf16[1024,2048]{1,0:T(8,128)(2,1)} %refs_1_.1), custom_call_target="tpu_custom_call" | custom-call | flops 268435456 | bytes 4194304 | tf_op jit(solution)/shard_map/pallas_call | solution.py:97
  42.4 4.0 %shard_map.79 = f32[64,1024]{1,0:T(8,128)S(1)} custom-call(bf16[64,2048]{1,0:T(8,128)(2,1)S(1)} %pad_maximum_fusion.1.refs_0_.grad_ref, f32[64,1024]{1,0:T(8,128)S(1)} %shard_map.78.refs_1_, bf16[1024,2048]{1,0:T(8,128)(2,1)} %refs_2_.1), custom_call_target="tpu_custom_call" | custom-call | flops 268435456 | bytes 4194304 | tf_op jit(solution)/shard_map/pallas_call | solution.py:97
  46.5 1.6 %collective-permute-start.12 = (f32[2,2,4,2,1024]{4,3,2,1,0:T(2,128)S(1)}, f32[2,2,4,2,1024]{4,3,2,1,0:T(2,128)S(1)}, u32[]{:S(2)}, u32[]{:S(2)}) collective-permute-start(f32[2,2,4,2,1024]{4,3,2,1,0:T(2,128)S(1)} %slice_bitcast_fusion), channel_id=1, source_target_pairs={{0,4},{1,5},{2,6},{3,7},{4,0},{5,1},{6,2},{7,3},{8,12},{9,13},{10,... | collective-permute-start | bytes 393224 | tf_op jit(solution)/shard_map/ppermute | solution.py:23
  48.2 0.7 gather_fusion.1
  48.9 3.4 %collective-permute-done.12 = f32[2,2,4,2,1024]{4,3,2,1,0:T(2,128)S(1)} collective-permute-done((f32[2,2,4,2,1024]{4,3,2,1,0:T(2,128)S(1)}, f32[2,2,4,2,1024]{4,3,2,1,0:T(2,128)S(1)}, u32[]{:S(2)}, u32[]{:S(2)}) %collective-permute-start.12) | collective-permute-done | bytes 131104 | tf_op jit(solution)/shard_map/ppermute | solution.py:23
  52.4 1.6 %collective-permute-start.13 = (f32[2,2,2,2,1024]{4,3,2,1,0:T(2,128)S(1)}, f32[2,2,2,2,1024]{4,3,2,1,0:T(2,128)S(1)}, u32[]{:S(2)}, u32[]{:S(2)}) collective-permute-start(f32[2,2,2,2,1024]{4,3,2,1,0:T(2,128)S(1)} %slice_bitcast_fusion.2), channel_id=1, source_target_pairs={{0,8},{1,9},{2,10},{3,11},{4,12},{5,13},{6,14},{7,15},{8,0},{9,1},... | collective-permute-start | bytes 196616 | tf_op jit(solution)/shard_map/ppermute | solution.py:23
  54.0 0.7 broadcast_select_fusion.1
  54.7 4.0 %shard_map.82.rest_0_ = bf16[4096,2048]{1,0:T(8,128)(2,1)} custom-call(bf16[64,4096]{1,0:T(8,128)(2,1)S(1)} %get-tuple-element.14.feats_ref.rows_ref, bf16[64,2048]{1,0:T(8,128)(2,1)S(1)} %constant_dynamic-update-slice_fusion.refs_0_.grad_ref), custom_call_target="tpu_custom_call" | custom-call | flops 536870912 | bytes 9175040 | tf_op jit(solution)/shard_map/pallas_call | solution.py:175
  58.8 3.1 %collective-permute-start.14 = (f32[2,2,1,2,1024]{4,3,1,0,2:T(2,128)S(1)}, f32[2,2,1,2,1024]{4,3,1,0,2:T(2,128)S(1)}, u32[]{:S(2)}, u32[]{:S(2)}) collective-permute-start(f32[2,2,1,2,1024]{4,3,1,0,2:T(2,128)S(1)} %slice_bitcast_fusion.4), channel_id=1, source_target_pairs={{0,16},{1,17},{2,18},{3,19},{4,20},{5,21},{6,22},{7,23},{8,24},{9,... | collective-permute-start | bytes 98312 | tf_op jit(solution)/shard_map/ppermute | solution.py:23
  61.8 4.0 %shard_map.80.rest_0_ = bf16[4096,2048]{1,0:T(8,128)(2,1)} custom-call(bf16[64,4096]{1,0:T(8,128)(2,1)S(1)} %get-tuple-element.14.feats_ref.rows_ref, bf16[64,2048]{1,0:T(8,128)(2,1)S(1)} %pad_maximum_fusion.1.refs_0_.grad_ref), custom_call_target="tpu_custom_call" | custom-call | flops 536870912 | bytes 9175040 | tf_op jit(solution)/shard_map/pallas_call | solution.py:175
  66.0 4.2 %shard_map.83 = bf16[4096,2048]{1,0:T(8,128)(2,1)} custom-call(bf16[64,4096]{1,0:T(8,128)(2,1)S(1)} %get-tuple-element.14.feats_ref.rows_ref, bf16[64,2048]{1,0:T(8,128)(2,1)S(1)} %constant_dynamic-update-slice_fusion.refs_0_.grad_ref, bf16[4096,2048]{1,0:T(8,128)(2,1)} %shard_map.82.rest_0_), custom_call_target="tpu_custom_call", output_to_operand_aliasing={{}: (2, {})} | custom-call | flops 536870912 | bytes 9175040 | tf_op jit(solution)/shard_map/pallas_call | solution.py:175
  70.2 1.6 %collective-permute-start.16 = (bf16[2,2,1024]{2,1,0:T(2,128)(2,1)S(1)}, bf16[2,2,1024]{2,1,0:T(2,128)(2,1)S(1)}, u32[]{:S(2)}, u32[]{:S(2)}) collective-permute-start(bf16[2,2,1024]{2,1,0:T(2,128)(2,1)S(1)} %fusion.10), channel_id=1, source_target_pairs={{0,1},{1,0},{2,3},{3,2},{4,5},{5,4},{6,7},{7,6},{8,9},{9,8},{10,11... | collective-permute-start | bytes 24584 | tf_op jit(solution)/shard_map/ppermute | solution.py:23
  71.7 4.0 %shard_map.81 = bf16[4096,2048]{1,0:T(8,128)(2,1)} custom-call(bf16[64,4096]{1,0:T(8,128)(2,1)S(1)} %get-tuple-element.14.feats_ref.rows_ref, bf16[64,2048]{1,0:T(8,128)(2,1)S(1)} %pad_maximum_fusion.1.refs_0_.grad_ref, bf16[4096,2048]{1,0:T(8,128)(2,1)} %shard_map.80.rest_0_), custom_call_target="tpu_custom_call", output_to_operand_aliasing={{}: (2, {})} | custom-call | flops 536870912 | bytes 9175040 | tf_op jit(solution)/shard_map/pallas_call | solution.py:175
  (57 shorter events, 4.7 us)
Async XLA Ops:
  0.6 5.2 %collective-permute-start.1 = (bf16[1,2,4096]{2,1,0:T(2,128)(2,1)}, bf16[1,2,4096]{2,1,0:T(2,128)(2,1)S(1)}, u32[]{:S(2)}, u32[]{:S(2)}) collective-permute-start(bf16[1,2,4096]{2,1,0:T(2,128)(2,1)} %in_ref.1), channel_id=1, source_target_pairs={{0,17},{1,16},{2,19},{3,18},{4,21},{5,20},{6,23},{7,22},{8,25},{9,... | collective-permute-start | bytes 49160 | tf_op jit(solution)/shard_map/ppermute | solution.py:23
  4.2 0.8 copy-start
  5.9 3.6 %collective-permute-start.2 = (bf16[2,2,4096]{2,1,0:T(2,128)(2,1)S(1)}, bf16[2,2,4096]{2,1,0:T(2,128)(2,1)S(1)}, u32[]{:S(2)}, u32[]{:S(2)}) collective-permute-start(bf16[2,2,4096]{2,1,0:T(2,128)(2,1)S(1)} %get-tuple-element.38), channel_id=1, source_target_pairs={{0,9},{1,8},{2,11},{3,10},{4,13},{5,12},{6,15},{7,14},{8,1},{9,0},... | collective-permute-start | bytes 98312 | tf_op jit(solution)/shard_map/ppermute | solution.py:23
  9.6 4.0 %collective-permute-start.3 = (bf16[4,2,4096]{2,1,0:T(2,128)(2,1)S(1)}, bf16[4,2,4096]{2,1,0:T(2,128)(2,1)S(1)}, u32[]{:S(2)}, u32[]{:S(2)}) collective-permute-start(bf16[4,2,4096]{2,1,0:T(2,128)(2,1)S(1)} %bitcast.112), channel_id=1, source_target_pairs={{0,5},{1,4},{2,7},{3,6},{4,1},{5,0},{6,3},{7,2},{8,13},{9,12},{10,... | collective-permute-start | bytes 196616 | tf_op jit(solution)/shard_map/ppermute | solution.py:23
  13.9 5.5 %collective-permute-start.4 = (bf16[8,2,4096]{2,1,0:T(2,128)(2,1)S(1)}, bf16[8,2,4096]{2,1,0:T(2,128)(2,1)S(1)}, u32[]{:S(2)}, u32[]{:S(2)}) collective-permute-start(bf16[8,2,4096]{2,1,0:T(2,128)(2,1)S(1)} %bitcast.110), channel_id=1, source_target_pairs={{0,3},{1,2},{2,1},{3,0},{4,7},{5,6},{6,5},{7,4},{8,11},{9,10},{10,... | collective-permute-start | bytes 393224 | tf_op jit(solution)/shard_map/ppermute | solution.py:23
  19.8 2.4 %collective-permute-start.5 = (bf16[2,8,2,4096]{3,2,1,0:T(2,128)(2,1)S(1)}, bf16[2,8,2,4096]{3,2,1,0:T(2,128)(2,1)S(1)}, u32[]{:S(2)}, u32[]{:S(2)}) collective-permute-start(bf16[2,8,2,4096]{3,2,1,0:T(2,128)(2,1)S(1)} %pad_maximum_fusion.part_ref), channel_id=1, source_target_pairs={{0,1},{1,0},{2,3},{3,2},{4,5},{5,4},{6,7},{7,6},{8,9},{9,8},{10,11... | collective-permute-start | bytes 786440 | tf_op jit(solution)/shard_map/ppermute | solution.py:23
  20.2 10.7 %collective-permute-start = (bf16[16,2048]{1,0:T(8,128)(2,1)}, bf16[16,2048]{1,0:T(8,128)(2,1)S(1)}, u32[]{:S(2)}, u32[]{:S(2)}) collective-permute-start(bf16[16,2048]{1,0:T(8,128)(2,1)} %bitcast.115), channel_id=1, source_target_pairs={{0,3},{1,2},{2,1},{3,0},{4,7},{5,6},{6,5},{7,4},{8,11},{9,10},{10,... | collective-permute-start | bytes 196616 | tf_op jit(solution)/shard_map/ppermute | solution.py:23
  24.7 3.5 %collective-permute-start.7 = (f32[32,2048]{1,0:T(8,128)S(1)}, f32[32,2048]{1,0:T(8,128)S(1)}, u32[]{:S(2)}, u32[]{:S(2)}) collective-permute-start(f32[32,2048]{1,0:T(8,128)S(1)} %get-tuple-element.20), channel_id=1, source_target_pairs={{0,1},{1,0},{2,3},{3,2},{4,5},{5,4},{6,7},{7,6},{8,9},{9,8},{10,11... | collective-permute-start | bytes 786440 | tf_op jit(solution)/shard_map/ppermute | solution.py:23
  27.8 1.7 %collective-permute-start.6 = (f32[32,2048]{1,0:T(8,128)S(1)}, f32[32,2048]{1,0:T(8,128)S(1)}, u32[]{:S(2)}, u32[]{:S(2)}) collective-permute-start(f32[32,2048]{1,0:T(8,128)S(1)} %get-tuple-element.16), channel_id=1, source_target_pairs={{0,1},{1,0},{2,3},{3,2},{4,5},{5,4},{6,7},{7,6},{8,9},{9,8},{10,11... | collective-permute-start | bytes 786440 | tf_op jit(solution)/shard_map/ppermute | solution.py:23
  28.3 5.6 %collective-permute-start.8 = (bf16[32,2048]{1,0:T(8,128)(2,1)S(1)}, bf16[32,2048]{1,0:T(8,128)(2,1)S(1)}, u32[]{:S(2)}, u32[]{:S(2)}) collective-permute-start(bf16[32,2048]{1,0:T(8,128)(2,1)S(1)} %add_convert_fusion), channel_id=1, source_target_pairs={{0,3},{1,2},{2,1},{3,0},{4,7},{5,6},{6,5},{7,4},{8,11},{9,10},{10,... | collective-permute-start | bytes 393224 | tf_op jit(solution)/shard_map/ppermute | solution.py:23
  29.5 7.1 %collective-permute-start.9 = (bf16[32,2048]{1,0:T(8,128)(2,1)S(1)}, bf16[32,2048]{1,0:T(8,128)(2,1)S(1)}, u32[]{:S(2)}, u32[]{:S(2)}) collective-permute-start(bf16[32,2048]{1,0:T(8,128)(2,1)S(1)} %add_convert_fusion.1), channel_id=1, source_target_pairs={{0,3},{1,2},{2,1},{3,0},{4,7},{5,6},{6,5},{7,4},{8,11},{9,10},{10,... | collective-permute-start | bytes 393224 | tf_op jit(solution)/shard_map/ppermute | solution.py:23
  36.8 5.6 %collective-permute-start.10 = (bf16[32,2048]{1,0:T(8,128)(2,1)S(1)}, bf16[32,2048]{1,0:T(8,128)(2,1)S(1)}, u32[]{:S(2)}, u32[]{:S(2)}) collective-permute-start(bf16[32,2048]{1,0:T(8,128)(2,1)S(1)} %get-tuple-element.26), channel_id=1, source_target_pairs={{0,1},{1,0},{2,3},{3,2},{4,5},{5,4},{6,7},{7,6},{8,9},{9,8},{10,11... | collective-permute-start | bytes 393224 | tf_op jit(solution)/shard_map/ppermute | solution.py:23
  36.9 1.4 %collective-permute-start.11 = (bf16[32,2048]{1,0:T(8,128)(2,1)S(1)}, bf16[32,2048]{1,0:T(8,128)(2,1)S(1)}, u32[]{:S(2)}, u32[]{:S(2)}) collective-permute-start(bf16[32,2048]{1,0:T(8,128)(2,1)S(1)} %get-tuple-element.23), channel_id=1, source_target_pairs={{0,1},{1,0},{2,3},{3,2},{4,5},{5,4},{6,7},{7,6},{8,9},{9,8},{10,11... | collective-permute-start | bytes 393224 | tf_op jit(solution)/shard_map/ppermute | solution.py:23
  46.5 5.8 %collective-permute-start.12 = (f32[2,2,4,2,1024]{4,3,2,1,0:T(2,128)S(1)}, f32[2,2,4,2,1024]{4,3,2,1,0:T(2,128)S(1)}, u32[]{:S(2)}, u32[]{:S(2)}) collective-permute-start(f32[2,2,4,2,1024]{4,3,2,1,0:T(2,128)S(1)} %slice_bitcast_fusion), channel_id=1, source_target_pairs={{0,4},{1,5},{2,6},{3,7},{4,0},{5,1},{6,2},{7,3},{8,12},{9,13},{10,... | collective-permute-start | bytes 393224 | tf_op jit(solution)/shard_map/ppermute | solution.py:23
  52.4 6.3 %collective-permute-start.13 = (f32[2,2,2,2,1024]{4,3,2,1,0:T(2,128)S(1)}, f32[2,2,2,2,1024]{4,3,2,1,0:T(2,128)S(1)}, u32[]{:S(2)}, u32[]{:S(2)}) collective-permute-start(f32[2,2,2,2,1024]{4,3,2,1,0:T(2,128)S(1)} %slice_bitcast_fusion.2), channel_id=1, source_target_pairs={{0,8},{1,9},{2,10},{3,11},{4,12},{5,13},{6,14},{7,15},{8,0},{9,1},... | collective-permute-start | bytes 196616 | tf_op jit(solution)/shard_map/ppermute | solution.py:23
  58.8 7.1 %collective-permute-start.14 = (f32[2,2,1,2,1024]{4,3,1,0,2:T(2,128)S(1)}, f32[2,2,1,2,1024]{4,3,1,0,2:T(2,128)S(1)}, u32[]{:S(2)}, u32[]{:S(2)}) collective-permute-start(f32[2,2,1,2,1024]{4,3,1,0,2:T(2,128)S(1)} %slice_bitcast_fusion.4), channel_id=1, source_target_pairs={{0,16},{1,17},{2,18},{3,19},{4,20},{5,21},{6,22},{7,23},{8,24},{9,... | collective-permute-start | bytes 98312 | tf_op jit(solution)/shard_map/ppermute | solution.py:23
  65.9 4.3 %collective-permute-start.15 = (bf16[2,2,1024]{2,1,0:T(2,128)(2,1)S(1)}, bf16[2,2,1024]{2,1,0:T(2,128)(2,1)S(1)}, u32[]{:S(2)}, u32[]{:S(2)}) collective-permute-start(bf16[2,2,1024]{2,1,0:T(2,128)(2,1)S(1)} %get-tuple-element.40), channel_id=1, source_target_pairs={{0,3},{1,2},{2,1},{3,0},{4,7},{5,6},{6,5},{7,4},{8,11},{9,10},{10,... | collective-permute-start | bytes 24584 | tf_op jit(solution)/shard_map/ppermute | solution.py:23
  70.2 5.5 %collective-permute-start.16 = (bf16[2,2,1024]{2,1,0:T(2,128)(2,1)S(1)}, bf16[2,2,1024]{2,1,0:T(2,128)(2,1)S(1)}, u32[]{:S(2)}, u32[]{:S(2)}) collective-permute-start(bf16[2,2,1024]{2,1,0:T(2,128)(2,1)S(1)} %fusion.10), channel_id=1, source_target_pairs={{0,1},{1,0},{2,3},{3,2},{4,5},{5,4},{6,7},{7,6},{8,9},{9,8},{10,11... | collective-permute-start | bytes 24584 | tf_op jit(solution)/shard_map/ppermute | solution.py:23

commit v5 on v4

--- a/solution.py
+++ b/solution.py
@@ -92,14 +92,15 @@
     multiply(feats_ref, copies, buf, keep_ref, send_ref)
 
 
-def stream(kernel, args, weight, outs, flops):
+def stream(kernel, args, weight, outs, flops, pieces=None):
     depth, width = weight.shape
+    pieces = pieces or (PIECES, depth // PIECES, width)
     return pl.pallas_call(
         kernel,
         in_specs=[VMEM] * len(args) + [HBM],
         out_specs=[VMEM] * len(outs),
         out_shape=outs,
-        scratch_shapes=[pltpu.VMEM((PIECES, depth // PIECES, width), BF16), pltpu.SemaphoreType.DMA((PIECES,))],
+        scratch_shapes=[pltpu.VMEM(pieces, BF16), pltpu.SemaphoreType.DMA((pieces[0],))],
         compiler_params=pltpu.CompilerParams(vmem_limit_bytes=52 << 20),
         cost_estimate=pl.CostEstimate(flops=flops, bytes_accessed=2 * weight.size, transcendentals=0),
     )(*args, weight)
@@ -124,21 +125,26 @@
 
 def back_kernel(*refs):
     grad_ref, weight_ref, out_ref, buf, sem = refs[0], *refs[-4:]
-    copies = pieces_of(weight_ref, buf, sem)
+    count, _, wide = buf.shape
+    parts = [pl.ds(i * wide, wide) for i in range(count)]
+    copies = [pltpu.make_async_copy(weight_ref.at[:, at], buf.at[i], sem.at[i]) for i, at in enumerate(parts)]
     for copy in copies:
         copy.start()
-    tall = buf.shape[1]
     for i, copy in enumerate(copies):
         copy.wait()
-        out = lax.dot_general(grad_ref[...], buf[i], COLS, preferred_element_type=F32)
-        at = slice(i * tall, (i + 1) * tall)
-        out_ref[:, at] = out if len(refs) == 5 else refs[1][:, at] + out
+        out = lax.dot_general(grad_ref[:, parts[i]], buf[i], COLS, preferred_element_type=F32)
+        if i:
+            out_ref[...] += out
+        else:
+            out_ref[...] = out if len(refs) == 5 else refs[1][...] + out
 
 
 def back(grad, weight, start=None):
-    out = jax.ShapeDtypeStruct((grad.shape[0], weight.shape[0]), F32)
+    depth, width = weight.shape
+    pieces = PIECES if width % (128 * PIECES) == 0 else 1
+    out = jax.ShapeDtypeStruct((grad.shape[0], depth), F32)
     args = (grad,) if start is None else (grad, start)
-    return stream(back_kernel, args, weight, [out], 2 * grad.shape[0] * weight.size)[0]
+    return stream(back_kernel, args, weight, [out], 2 * grad.shape[0] * weight.size, (pieces, depth, width // pieces))[0]
 
 
 def outer_kernel(rows_ref, grad_ref, *rest, base, scale):
@@ -207,32 +213,36 @@
     up_keep, up_send = ahead(feats, up_weight)
 
     def partial(keep, send):
-        return (keep + swap(send, 0, 1)).astype(BF16)
+        other = swap(send, 0, 1)
+        return (keep + other).astype(BF16)
 
     def summed(half):
         other = swap(half, 0, 3)
         other = jnp.concatenate([other[rows:], other[:rows]])
         return half.astype(F32) + other.astype(F32)
 
-    half_gate, half_up = partial(gate_keep, gate_send), partial(up_keep, up_send)
+    half_gate = partial(gate_keep, gate_send)
+    half_up = partial(up_keep, up_send)
     gate_pre = summed(half_gate)
     up_pre = summed(half_up)
 
     cot = swap(cotangent[0], 0, 3)
-    near, cot, _ = lax.optimization_barrier((cotangent[0], cot, half_up))
+    near, cot, _ = lax.optimization_barrier((cotangent[0], cot, up_keep))
     cot = jnp.stack([near, cot]).reshape(2, n_tp, rt, width)
     cot = jnp.take(cot, order, axis=1).reshape(2 * rows, width)
 
+    grad_hidden = cot.astype(F32)
     act, slope = swish_parts(gate_pre)
-    grad_hidden = cot.astype(F32)
     d_up = (grad_hidden * act).astype(BF16)
     d_up, act, slope = lax.optimization_barrier((d_up, act, slope))
-    d_up = jnp.concatenate([d_up, swap(d_up, 0, 1)])
+    far = swap(d_up, 0, 1)
+    d_up = jnp.concatenate([d_up, far])
     total = back(d_up, up_weight)
     hidden = (act * up_pre)[:rows].astype(BF16).reshape(n_tp, rt, width)
     hidden = jnp.take(hidden, order, axis=0).reshape(1, rows, width)
     d_gate = (grad_hidden * up_pre * slope).astype(BF16)
-    d_gate = jnp.concatenate([d_gate, swap(d_gate, 0, 1)])
+    far = swap(d_gate, 0, 1)
+    d_gate = jnp.concatenate([d_gate, far])
     total = back(d_gate, gate_weight, total)
 
     total = total.reshape(2, 2, n_tp, rt, depth)

time: 76.6 us -> 76.2 us (level)
  Pallas kernels: 29 us -> 26.5 us
  waiting for transfers between devices: 16.2 us -> 18.3 us
    pallas_call x4, Pallas kernels: 12.9 us -> 10.4 us  [stream(): pl.pallas_call(kernel, in_specs=[VMEM] * len(args) + [HBM], out_specs=[VM...]
    ppermute x17, waiting for transfers between devices: 16.2 us -> 18.3 us  [swap(): return lax.ppermute(value, ('tp', 'dp'), pairs)]
  transfers between devices with their start and end apart: 17 -> 17, of which waited for: 8 -> 8; matrix products, arithmetic and copies ran while one was open for 5% -> 5% of each run, Pallas kernels for 33% -> 31%
where the time goes in v5:
time: 76.2 us; the launch traced here: 76 us
  Pallas kernels  26.5 us (35%)
  starting transfers between devices  23.3 us (31%)
  waiting for transfers between devices  18.3 us (24%)
  local copies, waits for them, and re-layouts  4.13 us (5%)
  other arithmetic  2.76 us (4%)
  between operations  0.96 us (1%)
    ppermute x17, starting transfers between devices, swap(): return lax.ppermute(value, ('tp', 'dp'), pairs)  23.3 us
    ppermute x17, waiting for transfers between devices, swap(): return lax.ppermute(value, ('tp', 'dp'), pairs)  18.3 us
    pallas_call x4, Pallas kernels, outer(): pl.pallas_call(kernel, in_specs=[VMEM, VMEM] + [HBM] * (len(args) - 2), o...  16.1 us
    pallas_call x4, Pallas kernels, stream(): pl.pallas_call(kernel, in_specs=[VMEM] * len(args) + [HBM], out_specs=[VM...  10.4 us
  transfers between devices with their start and end apart: 17, of which 8 were waited for; matrix products, arithmetic and copies ran while one was open for 5% of the time, Pallas kernels for 31%

profile of v5, /device:TPU:0, one launch (start us, length us, event | category | flops | bytes accessed | tf_op | source)
XLA Modules:
  0.0 76.0 jit_solution(5836073242818039377)
XLA Ops:
  0.6 3.6 %collective-permute-start.1 = (bf16[1,2,4096]{2,1,0:T(2,128)(2,1)}, bf16[1,2,4096]{2,1,0:T(2,128)(2,1)S(1)}, u32[]{:S(2)}, u32[]{:S(2)}) collective-permute-start(bf16[1,2,4096]{2,1,0:T(2,128)(2,1)} %in_ref.1), channel_id=1, source_target_pairs={{0,17},{1,16},{2,19},{3,18},{4,21},{5,20},{6,23},{7,22},{8,25},{9,... | collective-permute-start | bytes 49160 | tf_op jit(solution)/shard_map/ppermute | solution.py:23
  4.2 0.7 copy-done
  5.0 0.9 %collective-permute-done.1 = bf16[1,2,4096]{2,1,0:T(2,128)(2,1)S(1)} collective-permute-done((bf16[1,2,4096]{2,1,0:T(2,128)(2,1)}, bf16[1,2,4096]{2,1,0:T(2,128)(2,1)S(1)}, u32[]{:S(2)}, u32[]{:S(2)}) %collective-permute-start.1) | collective-permute-done | bytes 16416 | tf_op jit(solution)/shard_map/ppermute | solution.py:23
  5.9 2.0 %collective-permute-start.2 = (bf16[2,2,4096]{2,1,0:T(2,128)(2,1)S(1)}, bf16[2,2,4096]{2,1,0:T(2,128)(2,1)S(1)}, u32[]{:S(2)}, u32[]{:S(2)}) collective-permute-start(bf16[2,2,4096]{2,1,0:T(2,128)(2,1)S(1)} %get-tuple-element.38), channel_id=1, source_target_pairs={{0,9},{1,8},{2,11},{3,10},{4,13},{5,12},{6,15},{7,14},{8,1},{9,0},... | collective-permute-start | bytes 98312 | tf_op jit(solution)/shard_map/ppermute | solution.py:23
  7.9 1.6 %collective-permute-done.2 = bf16[2,2,4096]{2,1,0:T(2,128)(2,1)S(1)} collective-permute-done((bf16[2,2,4096]{2,1,0:T(2,128)(2,1)S(1)}, bf16[2,2,4096]{2,1,0:T(2,128)(2,1)S(1)}, u32[]{:S(2)}, u32[]{:S(2)}) %collective-permute-start.2) | collective-permute-done | bytes 32800 | tf_op jit(solution)/shard_map/ppermute | solution.py:23
  9.6 1.8 %collective-permute-start.3 = (bf16[4,2,4096]{2,1,0:T(2,128)(2,1)S(1)}, bf16[4,2,4096]{2,1,0:T(2,128)(2,1)S(1)}, u32[]{:S(2)}, u32[]{:S(2)}) collective-permute-start(bf16[4,2,4096]{2,1,0:T(2,128)(2,1)S(1)} %bitcast.112), channel_id=1, source_target_pairs={{0,5},{1,4},{2,7},{3,6},{4,1},{5,0},{6,3},{7,2},{8,13},{9,12},{10,... | collective-permute-start | bytes 196616 | tf_op jit(solution)/shard_map/ppermute | solution.py:23
  11.4 2.2 %collective-permute-done.3 = bf16[4,2,4096]{2,1,0:T(2,128)(2,1)S(1)} collective-permute-done((bf16[4,2,4096]{2,1,0:T(2,128)(2,1)S(1)}, bf16[4,2,4096]{2,1,0:T(2,128)(2,1)S(1)}, u32[]{:S(2)}, u32[]{:S(2)}) %collective-permute-start.3) | collective-permute-done | bytes 65568 | tf_op jit(solution)/shard_map/ppermute | solution.py:23
  13.9 1.9 %collective-permute-start.4 = (bf16[8,2,4096]{2,1,0:T(2,128)(2,1)S(1)}, bf16[8,2,4096]{2,1,0:T(2,128)(2,1)S(1)}, u32[]{:S(2)}, u32[]{:S(2)}) collective-permute-start(bf16[8,2,4096]{2,1,0:T(2,128)(2,1)S(1)} %bitcast.110), channel_id=1, source_target_pairs={{0,3},{1,2},{2,1},{3,0},{4,7},{5,6},{6,5},{7,4},{8,11},{9,10},{10,... | collective-permute-start | bytes 393224 | tf_op jit(solution)/shard_map/ppermute | solution.py:23
  15.8 3.6 %collective-permute-done.4 = bf16[8,2,4096]{2,1,0:T(2,128)(2,1)S(1)} collective-permute-done((bf16[8,2,4096]{2,1,0:T(2,128)(2,1)S(1)}, bf16[8,2,4096]{2,1,0:T(2,128)(2,1)S(1)}, u32[]{:S(2)}, u32[]{:S(2)}) %collective-permute-start.4) | collective-permute-done | bytes 131104 | tf_op jit(solution)/shard_map/ppermute | solution.py:23
  20.2 2.0 %collective-permute-start = (bf16[16,2048]{1,0:T(8,128)(2,1)}, bf16[16,2048]{1,0:T(8,128)(2,1)S(1)}, u32[]{:S(2)}, u32[]{:S(2)}) collective-permute-start(bf16[16,2048]{1,0:T(8,128)(2,1)} %bitcast.115), channel_id=1, source_target_pairs={{0,3},{1,2},{2,1},{3,0},{4,7},{5,6},{6,5},{7,4},{8,11},{9,10},{10,... | collective-permute-start | bytes 196616 | tf_op jit(solution)/shard_map/ppermute | solution.py:23
  22.2 2.5 %shard_map.76 = (bf16[64,4096]{1,0:T(8,128)(2,1)S(1)}, f32[32,2048]{1,0:T(8,128)S(1)}, f32[32,2048]{1,0:T(8,128)S(1)}) custom-call(bf16[2,8,2,4096]{3,2,1,0:T(2,128)(2,1)S(1)} %pad_maximum_fusion.part_ref, bf16[2,8,2,4096]{3,2,1,0:T(2,128)(2,1)S(1)} %collective-permute-done.5.far_ref, bf16[1024,2048]{1,0:T(8,128)(2,1)} %refs_2_.1), custom_call_target="tpu_custom_call" | custom-call | flops 268435456 | bytes 4194304 | tf_op jit(solution)/shard_map/pallas_call | solution.py:98
  25.2 2.5 %shard_map.77 = (f32[32,2048]{1,0:T(8,128)S(1)}, f32[32,2048]{1,0:T(8,128)S(1)}) custom-call(bf16[64,4096]{1,0:T(8,128)(2,1)S(1)} %get-tuple-element.14.feats_ref.rows_ref, bf16[1024,2048]{1,0:T(8,128)(2,1)} %refs_1_.1), custom_call_target="tpu_custom_call" | custom-call | flops 268435456 | bytes 4194304 | tf_op jit(solution)/shard_map/pallas_call | solution.py:98
  27.8 0.9 %stack.54 = bf16[1,8,2,2048]{3,2,1,0:T(2,128)(2,1)S(1)} reshape(bf16[16,2048]{1,0:T(8,128)(2,1)} %bitcast.116) | data formatting | bytes 131072 | tf_op jit(solution)/shard_map/stack | solution.py:231
  28.9 0.8 %gather_fusion = bf16[8,2,2,2048]{3,2,1,0:T(2,128)(2,1)S(1)} fusion(bf16[2,8,2,2048]{3,2,1,0:T(2,128)(2,1)S(1)} %pad_maximum_fusion.3, s32[1024]{0:T(1024)S(1)} %pad_clamp_fusion), kind=kCustom, calls=%fused_computation | custom fusion | bytes 262176 | tf_op jit(solution)/shard_map/jit(_take)/gather | solution.py:232
  30.4 1.2 %collective-permute-start.7 = (bf16[32,2048]{1,0:T(8,128)(2,1)S(1)}, bf16[32,2048]{1,0:T(8,128)(2,1)S(1)}, u32[]{:S(2)}, u32[]{:S(2)}) collective-permute-start(bf16[32,2048]{1,0:T(8,128)(2,1)S(1)} %add_convert_fusion.1), channel_id=1, source_target_pairs={{0,3},{1,2},{2,1},{3,0},{4,7},{5,6},{6,5},{7,4},{8,11},{9,10},{10,... | collective-permute-start | bytes 393224 | tf_op jit(solution)/shard_map/ppermute | solution.py:23
  31.6 1.4 %collective-permute-start.9 = (bf16[32,2048]{1,0:T(8,128)(2,1)S(1)}, bf16[32,2048]{1,0:T(8,128)(2,1)S(1)}, u32[]{:S(2)}, u32[]{:S(2)}) collective-permute-start(bf16[32,2048]{1,0:T(8,128)(2,1)S(1)} %add_convert_fusion), channel_id=1, source_target_pairs={{0,3},{1,2},{2,1},{3,0},{4,7},{5,6},{6,5},{7,4},{8,11},{9,10},{10,... | collective-permute-start | bytes 393224 | tf_op jit(solution)/shard_map/ppermute | solution.py:23
  33.0 3.0 %collective-permute-done.7 = bf16[32,2048]{1,0:T(8,128)(2,1)S(1)} collective-permute-done((bf16[32,2048]{1,0:T(8,128)(2,1)S(1)}, bf16[32,2048]{1,0:T(8,128)(2,1)S(1)}, u32[]{:S(2)}, u32[]{:S(2)}) %collective-permute-start.7) | collective-permute-done | bytes 131104 | tf_op jit(solution)/shard_map/ppermute | solution.py:23
  36.1 2.6 %collective-permute-done.9 = bf16[32,2048]{1,0:T(8,128)(2,1)S(1)} collective-permute-done((bf16[32,2048]{1,0:T(8,128)(2,1)S(1)}, bf16[32,2048]{1,0:T(8,128)(2,1)S(1)}, u32[]{:S(2)}, u32[]{:S(2)}) %collective-permute-start.9) | collective-permute-done | bytes 131104 | tf_op jit(solution)/shard_map/ppermute | solution.py:23
  39.5 1.0 %collective-permute-done.11 = bf16[32,2048]{1,0:T(8,128)(2,1)S(1)} collective-permute-done((bf16[32,2048]{1,0:T(8,128)(2,1)S(1)}, bf16[32,2048]{1,0:T(8,128)(2,1)S(1)}, u32[]{:S(2)}, u32[]{:S(2)}) %collective-permute-start.11) | collective-permute-done | bytes 131104 | tf_op jit(solution)/shard_map/ppermute | solution.py:23
  40.5 2.7 %shard_map.78.refs_1_ = f32[64,1024]{1,0:T(8,128)S(1)} custom-call(bf16[64,2048]{1,0:T(8,128)(2,1)S(1)} %constant_dynamic-update-slice_fusion.refs_0_.grad_ref, bf16[1024,2048]{1,0:T(8,128)(2,1)} %refs_1_.1), custom_call_target="tpu_custom_call" | custom-call | flops 268435456 | bytes 4194304 | tf_op jit(solution)/shard_map/pallas_call | solution.py:98
  43.2 2.7 %shard_map.79 = f32[64,1024]{1,0:T(8,128)S(1)} custom-call(bf16[64,2048]{1,0:T(8,128)(2,1)S(1)} %pad_maximum_fusion.1.refs_0_.grad_ref, f32[64,1024]{1,0:T(8,128)S(1)} %shard_map.78.refs_1_, bf16[1024,2048]{1,0:T(8,128)(2,1)} %refs_2_.1), custom_call_target="tpu_custom_call" | custom-call | flops 268435456 | bytes 4194304 | tf_op jit(solution)/shard_map/pallas_call | solution.py:98
  46.1 1.6 %collective-permute-start.12 = (f32[2,2,4,2,1024]{4,3,2,1,0:T(2,128)S(1)}, f32[2,2,4,2,1024]{4,3,2,1,0:T(2,128)S(1)}, u32[]{:S(2)}, u32[]{:S(2)}) collective-permute-start(f32[2,2,4,2,1024]{4,3,2,1,0:T(2,128)S(1)} %slice_bitcast_fusion), channel_id=1, source_target_pairs={{0,4},{1,5},{2,6},{3,7},{4,0},{5,1},{6,2},{7,3},{8,12},{9,13},{10,... | collective-permute-start | bytes 393224 | tf_op jit(solution)/shard_map/ppermute | solution.py:23
  47.8 0.7 gather_fusion.1
  48.5 3.4 %collective-permute-done.12 = f32[2,2,4,2,1024]{4,3,2,1,0:T(2,128)S(1)} collective-permute-done((f32[2,2,4,2,1024]{4,3,2,1,0:T(2,128)S(1)}, f32[2,2,4,2,1024]{4,3,2,1,0:T(2,128)S(1)}, u32[]{:S(2)}, u32[]{:S(2)}) %collective-permute-start.12) | collective-permute-done | bytes 131104 | tf_op jit(solution)/shard_map/ppermute | solution.py:23
  52.0 1.6 %collective-permute-start.13 = (f32[2,2,2,2,1024]{4,3,2,1,0:T(2,128)S(1)}, f32[2,2,2,2,1024]{4,3,2,1,0:T(2,128)S(1)}, u32[]{:S(2)}, u32[]{:S(2)}) collective-permute-start(f32[2,2,2,2,1024]{4,3,2,1,0:T(2,128)S(1)} %slice_bitcast_fusion.2), channel_id=1, source_target_pairs={{0,8},{1,9},{2,10},{3,11},{4,12},{5,13},{6,14},{7,15},{8,0},{9,1},... | collective-permute-start | bytes 196616 | tf_op jit(solution)/shard_map/ppermute | solution.py:23
  53.6 0.7 broadcast_select_fusion.1
  54.3 4.0 %shard_map.82.rest_0_ = bf16[4096,2048]{1,0:T(8,128)(2,1)} custom-call(bf16[64,4096]{1,0:T(8,128)(2,1)S(1)} %get-tuple-element.14.feats_ref.rows_ref, bf16[64,2048]{1,0:T(8,128)(2,1)S(1)} %constant_dynamic-update-slice_fusion.refs_0_.grad_ref), custom_call_target="tpu_custom_call" | custom-call | flops 536870912 | bytes 9175040 | tf_op jit(solution)/shard_map/pallas_call | solution.py:181
  58.4 3.1 %collective-permute-start.14 = (f32[2,2,1,2,1024]{4,3,1,0,2:T(2,128)S(1)}, f32[2,2,1,2,1024]{4,3,1,0,2:T(2,128)S(1)}, u32[]{:S(2)}, u32[]{:S(2)}) collective-permute-start(f32[2,2,1,2,1024]{4,3,1,0,2:T(2,128)S(1)} %slice_bitcast_fusion.4), channel_id=1, source_target_pairs={{0,16},{1,17},{2,18},{3,19},{4,20},{5,21},{6,22},{7,23},{8,24},{9,... | collective-permute-start | bytes 98312 | tf_op jit(solution)/shard_map/ppermute | solution.py:23
  61.5 4.0 %shard_map.80.rest_0_ = bf16[4096,2048]{1,0:T(8,128)(2,1)} custom-call(bf16[64,4096]{1,0:T(8,128)(2,1)S(1)} %get-tuple-element.14.feats_ref.rows_ref, bf16[64,2048]{1,0:T(8,128)(2,1)S(1)} %pad_maximum_fusion.1.refs_0_.grad_ref), custom_call_target="tpu_custom_call" | custom-call | flops 536870912 | bytes 9175040 | tf_op jit(solution)/shard_map/pallas_call | solution.py:181
  65.6 4.2 %shard_map.83 = bf16[4096,2048]{1,0:T(8,128)(2,1)} custom-call(bf16[64,4096]{1,0:T(8,128)(2,1)S(1)} %get-tuple-element.14.feats_ref.rows_ref, bf16[64,2048]{1,0:T(8,128)(2,1)S(1)} %constant_dynamic-update-slice_fusion.refs_0_.grad_ref, bf16[4096,2048]{1,0:T(8,128)(2,1)} %shard_map.82.rest_0_), custom_call_target="tpu_custom_call", output_to_operand_aliasing={{}: (2, {})} | custom-call | flops 536870912 | bytes 9175040 | tf_op jit(solution)/shard_map/pallas_call | solution.py:181
  69.8 1.5 %collective-permute-start.16 = (bf16[2,2,1024]{2,1,0:T(2,128)(2,1)S(1)}, bf16[2,2,1024]{2,1,0:T(2,128)(2,1)S(1)}, u32[]{:S(2)}, u32[]{:S(2)}) collective-permute-start(bf16[2,2,1024]{2,1,0:T(2,128)(2,1)S(1)} %fusion.10), channel_id=1, source_target_pairs={{0,1},{1,0},{2,3},{3,2},{4,5},{5,4},{6,7},{7,6},{8,9},{9,8},{10,11... | collective-permute-start | bytes 24584 | tf_op jit(solution)/shard_map/ppermute | solution.py:23
  71.3 4.0 %shard_map.81 = bf16[4096,2048]{1,0:T(8,128)(2,1)} custom-call(bf16[64,4096]{1,0:T(8,128)(2,1)S(1)} %get-tuple-element.14.feats_ref.rows_ref, bf16[64,2048]{1,0:T(8,128)(2,1)S(1)} %pad_maximum_fusion.1.refs_0_.grad_ref, bf16[4096,2048]{1,0:T(8,128)(2,1)} %shard_map.80.rest_0_), custom_call_target="tpu_custom_call", output_to_operand_aliasing={{}: (2, {})} | custom-call | flops 536870912 | bytes 9175040 | tf_op jit(solution)/shard_map/pallas_call | solution.py:181
  (57 shorter events, 4.7 us)
Async XLA Ops:
  0.6 5.2 %collective-permute-start.1 = (bf16[1,2,4096]{2,1,0:T(2,128)(2,1)}, bf16[1,2,4096]{2,1,0:T(2,128)(2,1)S(1)}, u32[]{:S(2)}, u32[]{:S(2)}) collective-permute-start(bf16[1,2,4096]{2,1,0:T(2,128)(2,1)} %in_ref.1), channel_id=1, source_target_pairs={{0,17},{1,16},{2,19},{3,18},{4,21},{5,20},{6,23},{7,22},{8,25},{9,... | collective-permute-start | bytes 49160 | tf_op jit(solution)/shard_map/ppermute | solution.py:23
  4.2 0.8 copy-start
  5.9 3.6 %collective-permute-start.2 = (bf16[2,2,4096]{2,1,0:T(2,128)(2,1)S(1)}, bf16[2,2,4096]{2,1,0:T(2,128)(2,1)S(1)}, u32[]{:S(2)}, u32[]{:S(2)}) collective-permute-start(bf16[2,2,4096]{2,1,0:T(2,128)(2,1)S(1)} %get-tuple-element.38), channel_id=1, source_target_pairs={{0,9},{1,8},{2,11},{3,10},{4,13},{5,12},{6,15},{7,14},{8,1},{9,0},... | collective-permute-start | bytes 98312 | tf_op jit(solution)/shard_map/ppermute | solution.py:23
  9.6 4.0 %collective-permute-start.3 = (bf16[4,2,4096]{2,1,0:T(2,128)(2,1)S(1)}, bf16[4,2,4096]{2,1,0:T(2,128)(2,1)S(1)}, u32[]{:S(2)}, u32[]{:S(2)}) collective-permute-start(bf16[4,2,4096]{2,1,0:T(2,128)(2,1)S(1)} %bitcast.112), channel_id=1, source_target_pairs={{0,5},{1,4},{2,7},{3,6},{4,1},{5,0},{6,3},{7,2},{8,13},{9,12},{10,... | collective-permute-start | bytes 196616 | tf_op jit(solution)/shard_map/ppermute | solution.py:23
  13.9 5.5 %collective-permute-start.4 = (bf16[8,2,4096]{2,1,0:T(2,128)(2,1)S(1)}, bf16[8,2,4096]{2,1,0:T(2,128)(2,1)S(1)}, u32[]{:S(2)}, u32[]{:S(2)}) collective-permute-start(bf16[8,2,4096]{2,1,0:T(2,128)(2,1)S(1)} %bitcast.110), channel_id=1, source_target_pairs={{0,3},{1,2},{2,1},{3,0},{4,7},{5,6},{6,5},{7,4},{8,11},{9,10},{10,... | collective-permute-start | bytes 393224 | tf_op jit(solution)/shard_map/ppermute | solution.py:23
  19.8 2.4 %collective-permute-start.5 = (bf16[2,8,2,4096]{3,2,1,0:T(2,128)(2,1)S(1)}, bf16[2,8,2,4096]{3,2,1,0:T(2,128)(2,1)S(1)}, u32[]{:S(2)}, u32[]{:S(2)}) collective-permute-start(bf16[2,8,2,4096]{3,2,1,0:T(2,128)(2,1)S(1)} %pad_maximum_fusion.part_ref), channel_id=1, source_target_pairs={{0,1},{1,0},{2,3},{3,2},{4,5},{5,4},{6,7},{7,6},{8,9},{9,8},{10,11... | collective-permute-start | bytes 786440 | tf_op jit(solution)/shard_map/ppermute | solution.py:23
  20.2 7.6 %collective-permute-start = (bf16[16,2048]{1,0:T(8,128)(2,1)}, bf16[16,2048]{1,0:T(8,128)(2,1)S(1)}, u32[]{:S(2)}, u32[]{:S(2)}) collective-permute-start(bf16[16,2048]{1,0:T(8,128)(2,1)} %bitcast.115), channel_id=1, source_target_pairs={{0,3},{1,2},{2,1},{3,0},{4,7},{5,6},{6,5},{7,4},{8,11},{9,10},{10,... | collective-permute-start | bytes 196616 | tf_op jit(solution)/shard_map/ppermute | solution.py:23
  24.7 5.6 %collective-permute-start.6 = (f32[32,2048]{1,0:T(8,128)S(1)}, f32[32,2048]{1,0:T(8,128)S(1)}, u32[]{:S(2)}, u32[]{:S(2)}) collective-permute-start(f32[32,2048]{1,0:T(8,128)S(1)} %get-tuple-element.19), channel_id=1, source_target_pairs={{0,1},{1,0},{2,3},{3,2},{4,5},{5,4},{6,7},{7,6},{8,9},{9,8},{10,11... | collective-permute-start | bytes 786440 | tf_op jit(solution)/shard_map/ppermute | solution.py:23
  29.9 1.7 %collective-permute-start.8 = (f32[32,2048]{1,0:T(8,128)S(1)}, f32[32,2048]{1,0:T(8,128)S(1)}, u32[]{:S(2)}, u32[]{:S(2)}) collective-permute-start(f32[32,2048]{1,0:T(8,128)S(1)} %get-tuple-element.21), channel_id=1, source_target_pairs={{0,1},{1,0},{2,3},{3,2},{4,5},{5,4},{6,7},{7,6},{8,9},{9,8},{10,11... | collective-permute-start | bytes 786440 | tf_op jit(solution)/shard_map/ppermute | solution.py:23
  30.4 5.6 %collective-permute-start.7 = (bf16[32,2048]{1,0:T(8,128)(2,1)S(1)}, bf16[32,2048]{1,0:T(8,128)(2,1)S(1)}, u32[]{:S(2)}, u32[]{:S(2)}) collective-permute-start(bf16[32,2048]{1,0:T(8,128)(2,1)S(1)} %add_convert_fusion.1), channel_id=1, source_target_pairs={{0,3},{1,2},{2,1},{3,0},{4,7},{5,6},{6,5},{7,4},{8,11},{9,10},{10,... | collective-permute-start | bytes 393224 | tf_op jit(solution)/shard_map/ppermute | solution.py:23
  31.6 7.1 %collective-permute-start.9 = (bf16[32,2048]{1,0:T(8,128)(2,1)S(1)}, bf16[32,2048]{1,0:T(8,128)(2,1)S(1)}, u32[]{:S(2)}, u32[]{:S(2)}) collective-permute-start(bf16[32,2048]{1,0:T(8,128)(2,1)S(1)} %add_convert_fusion), channel_id=1, source_target_pairs={{0,3},{1,2},{2,1},{3,0},{4,7},{5,6},{6,5},{7,4},{8,11},{9,10},{10,... | collective-permute-start | bytes 393224 | tf_op jit(solution)/shard_map/ppermute | solution.py:23
  38.9 4.3 %collective-permute-start.10 = (bf16[32,2048]{1,0:T(8,128)(2,1)S(1)}, bf16[32,2048]{1,0:T(8,128)(2,1)S(1)}, u32[]{:S(2)}, u32[]{:S(2)}) collective-permute-start(bf16[32,2048]{1,0:T(8,128)(2,1)S(1)} %get-tuple-element.26), channel_id=1, source_target_pairs={{0,1},{1,0},{2,3},{3,2},{4,5},{5,4},{6,7},{7,6},{8,9},{9,8},{10,11... | collective-permute-start | bytes 393224 | tf_op jit(solution)/shard_map/ppermute | solution.py:23
  39.1 1.4 %collective-permute-start.11 = (bf16[32,2048]{1,0:T(8,128)(2,1)S(1)}, bf16[32,2048]{1,0:T(8,128)(2,1)S(1)}, u32[]{:S(2)}, u32[]{:S(2)}) collective-permute-start(bf16[32,2048]{1,0:T(8,128)(2,1)S(1)} %get-tuple-element.23), channel_id=1, source_target_pairs={{0,1},{1,0},{2,3},{3,2},{4,5},{5,4},{6,7},{7,6},{8,9},{9,8},{10,11... | collective-permute-start | bytes 393224 | tf_op jit(solution)/shard_map/ppermute | solution.py:23
  46.1 5.8 %collective-permute-start.12 = (f32[2,2,4,2,1024]{4,3,2,1,0:T(2,128)S(1)}, f32[2,2,4,2,1024]{4,3,2,1,0:T(2,128)S(1)}, u32[]{:S(2)}, u32[]{:S(2)}) collective-permute-start(f32[2,2,4,2,1024]{4,3,2,1,0:T(2,128)S(1)} %slice_bitcast_fusion), channel_id=1, source_target_pairs={{0,4},{1,5},{2,6},{3,7},{4,0},{5,1},{6,2},{7,3},{8,12},{9,13},{10,... | collective-permute-start | bytes 393224 | tf_op jit(solution)/shard_map/ppermute | solution.py:23
  52.0 6.3 %collective-permute-start.13 = (f32[2,2,2,2,1024]{4,3,2,1,0:T(2,128)S(1)}, f32[2,2,2,2,1024]{4,3,2,1,0:T(2,128)S(1)}, u32[]{:S(2)}, u32[]{:S(2)}) collective-permute-start(f32[2,2,2,2,1024]{4,3,2,1,0:T(2,128)S(1)} %slice_bitcast_fusion.2), channel_id=1, source_target_pairs={{0,8},{1,9},{2,10},{3,11},{4,12},{5,13},{6,14},{7,15},{8,0},{9,1},... | collective-permute-start | bytes 196616 | tf_op jit(solution)/shard_map/ppermute | solution.py:23
  58.4 7.1 %collective-permute-start.14 = (f32[2,2,1,2,1024]{4,3,1,0,2:T(2,128)S(1)}, f32[2,2,1,2,1024]{4,3,1,0,2:T(2,128)S(1)}, u32[]{:S(2)}, u32[]{:S(2)}) collective-permute-start(f32[2,2,1,2,1024]{4,3,1,0,2:T(2,128)S(1)} %slice_bitcast_fusion.4), channel_id=1, source_target_pairs={{0,16},{1,17},{2,18},{3,19},{4,20},{5,21},{6,22},{7,23},{8,24},{9,... | collective-permute-start | bytes 98312 | tf_op jit(solution)/shard_map/ppermute | solution.py:23
  65.5 4.3 %collective-permute-start.15 = (bf16[2,2,1024]{2,1,0:T(2,128)(2,1)S(1)}, bf16[2,2,1024]{2,1,0:T(2,128)(2,1)S(1)}, u32[]{:S(2)}, u32[]{:S(2)}) collective-permute-start(bf16[2,2,1024]{2,1,0:T(2,128)(2,1)S(1)} %get-tuple-element.40), channel_id=1, source_target_pairs={{0,3},{1,2},{2,1},{3,0},{4,7},{5,6},{6,5},{7,4},{8,11},{9,10},{10,... | collective-permute-start | bytes 24584 | tf_op jit(solution)/shard_map/ppermute | solution.py:23
  69.8 5.5 %collective-permute-start.16 = (bf16[2,2,1024]{2,1,0:T(2,128)(2,1)S(1)}, bf16[2,2,1024]{2,1,0:T(2,128)(2,1)S(1)}, u32[]{:S(2)}, u32[]{:S(2)}) collective-permute-start(bf16[2,2,1024]{2,1,0:T(2,128)(2,1)S(1)} %fusion.10), channel_id=1, source_target_pairs={{0,1},{1,0},{2,3},{3,2},{4,5},{5,4},{6,7},{7,6},{8,9},{9,8},{10,11... | collective-permute-start | bytes 24584 | tf_op jit(solution)/shard_map/ppermute | solution.py:23

commit v6 on v5

--- a/solution.py
+++ b/solution.py
@@ -227,8 +227,7 @@
     up_pre = summed(half_up)
 
     cot = swap(cotangent[0], 0, 3)
-    near, cot, _ = lax.optimization_barrier((cotangent[0], cot, up_keep))
-    cot = jnp.stack([near, cot]).reshape(2, n_tp, rt, width)
+    cot = jnp.stack([cotangent[0], cot]).reshape(2, n_tp, rt, width)
     cot = jnp.take(cot, order, axis=1).reshape(2 * rows, width)
 
     grad_hidden = cot.astype(F32)
@@ -261,7 +260,8 @@
     grad_up = outer(feats, d_up, inverse, 0, 2)
     grad_up = outer(feats, d_up, inverse, 1, 2, grad_up)
     grad_gate = outer(feats, d_gate, inverse, 0, 2)
-    grad_gate = outer(feats, d_gate, inverse, 1, 2, grad_gate)
+    grad_gate = outer(feats, d_gate, inverse, 2, 4, grad_gate)
+    grad_gate = outer(feats, d_gate, inverse, 3, 4, grad_gate)
     return hidden, grad_tokens, grad_gate, grad_up
 
 

time: 76.2 us -> 76.3 us (level)
  Pallas kernels: 26.5 us -> 27.7 us
  waiting for transfers between devices: 18.3 us -> 17.1 us
    pallas_call x4 -> x5, Pallas kernels: 16.1 us -> 17.3 us  [outer(): pl.pallas_call(kernel, in_specs=[VMEM, VMEM] + [HBM] * (len(args) - 2), o...]
    ppermute x17, waiting for transfers between devices: 18.3 us -> 17.1 us  [swap(): return lax.ppermute(value, ('tp', 'dp'), pairs)]
  transfers between devices with their start and end apart: 17 -> 17, of which waited for: 8 -> 8; matrix products, arithmetic and copies ran while one was open for 5% -> 6% of each run, Pallas kernels for 31% -> 33%
where the time goes in v6:
time: 76.3 us; the launch traced here: 76 us
  Pallas kernels  27.7 us (36%)
  starting transfers between devices  23.3 us (31%)
  waiting for transfers between devices  17.1 us (22%)
  local copies, waits for them, and re-layouts  4.12 us (5%)
  other arithmetic  2.77 us (4%)
  between operations  0.98 us (1%)
    ppermute x17, starting transfers between devices, swap(): return lax.ppermute(value, ('tp', 'dp'), pairs)  23.3 us
    pallas_call x5, Pallas kernels, outer(): pl.pallas_call(kernel, in_specs=[VMEM, VMEM] + [HBM] * (len(args) - 2), o...  17.3 us
    ppermute x17, waiting for transfers between devices, swap(): return lax.ppermute(value, ('tp', 'dp'), pairs)  17.1 us
    pallas_call x4, Pallas kernels, stream(): pl.pallas_call(kernel, in_specs=[VMEM] * len(args) + [HBM], out_specs=[VM...  10.4 us
  transfers between devices with their start and end apart: 17, of which 8 were waited for; matrix products, arithmetic and copies ran while one was open for 6% of the time, Pallas kernels for 33%

profile of v6, /device:TPU:0, one launch (start us, length us, event | category | flops | bytes accessed | tf_op | source)
XLA Modules:
  0.0 76.0 jit_solution(2524156596919234604)
XLA Ops:
  0.6 3.6 %collective-permute-start.1 = (bf16[1,2,4096]{2,1,0:T(2,128)(2,1)}, bf16[1,2,4096]{2,1,0:T(2,128)(2,1)S(1)}, u32[]{:S(2)}, u32[]{:S(2)}) collective-permute-start(bf16[1,2,4096]{2,1,0:T(2,128)(2,1)} %in_ref.1), channel_id=1, source_target_pairs={{0,17},{1,16},{2,19},{3,18},{4,21},{5,20},{6,23},{7,22},{8,25},{9,... | collective-permute-start | bytes 49160 | tf_op jit(solution)/shard_map/ppermute | solution.py:23
  4.2 0.7 copy-done
  5.0 0.9 %collective-permute-done.1 = bf16[1,2,4096]{2,1,0:T(2,128)(2,1)S(1)} collective-permute-done((bf16[1,2,4096]{2,1,0:T(2,128)(2,1)}, bf16[1,2,4096]{2,1,0:T(2,128)(2,1)S(1)}, u32[]{:S(2)}, u32[]{:S(2)}) %collective-permute-start.1) | collective-permute-done | bytes 16416 | tf_op jit(solution)/shard_map/ppermute | solution.py:23
  5.9 2.0 %collective-permute-start.2 = (bf16[2,2,4096]{2,1,0:T(2,128)(2,1)S(1)}, bf16[2,2,4096]{2,1,0:T(2,128)(2,1)S(1)}, u32[]{:S(2)}, u32[]{:S(2)}) collective-permute-start(bf16[2,2,4096]{2,1,0:T(2,128)(2,1)S(1)} %get-tuple-element.34), channel_id=1, source_target_pairs={{0,9},{1,8},{2,11},{3,10},{4,13},{5,12},{6,15},{7,14},{8,1},{9,0},... | collective-permute-start | bytes 98312 | tf_op jit(solution)/shard_map/ppermute | solution.py:23
  7.9 1.6 %collective-permute-done.2 = bf16[2,2,4096]{2,1,0:T(2,128)(2,1)S(1)} collective-permute-done((bf16[2,2,4096]{2,1,0:T(2,128)(2,1)S(1)}, bf16[2,2,4096]{2,1,0:T(2,128)(2,1)S(1)}, u32[]{:S(2)}, u32[]{:S(2)}) %collective-permute-start.2) | collective-permute-done | bytes 32800 | tf_op jit(solution)/shard_map/ppermute | solution.py:23
  9.6 1.8 %collective-permute-start.3 = (bf16[4,2,4096]{2,1,0:T(2,128)(2,1)S(1)}, bf16[4,2,4096]{2,1,0:T(2,128)(2,1)S(1)}, u32[]{:S(2)}, u32[]{:S(2)}) collective-permute-start(bf16[4,2,4096]{2,1,0:T(2,128)(2,1)S(1)} %bitcast.112), channel_id=1, source_target_pairs={{0,5},{1,4},{2,7},{3,6},{4,1},{5,0},{6,3},{7,2},{8,13},{9,12},{10,... | collective-permute-start | bytes 196616 | tf_op jit(solution)/shard_map/ppermute | solution.py:23
  11.4 2.2 %collective-permute-done.3 = bf16[4,2,4096]{2,1,0:T(2,128)(2,1)S(1)} collective-permute-done((bf16[4,2,4096]{2,1,0:T(2,128)(2,1)S(1)}, bf16[4,2,4096]{2,1,0:T(2,128)(2,1)S(1)}, u32[]{:S(2)}, u32[]{:S(2)}) %collective-permute-start.3) | collective-permute-done | bytes 65568 | tf_op jit(solution)/shard_map/ppermute | solution.py:23
  13.9 1.9 %collective-permute-start.4 = (bf16[8,2,4096]{2,1,0:T(2,128)(2,1)S(1)}, bf16[8,2,4096]{2,1,0:T(2,128)(2,1)S(1)}, u32[]{:S(2)}, u32[]{:S(2)}) collective-permute-start(bf16[8,2,4096]{2,1,0:T(2,128)(2,1)S(1)} %bitcast.110), channel_id=1, source_target_pairs={{0,3},{1,2},{2,1},{3,0},{4,7},{5,6},{6,5},{7,4},{8,11},{9,10},{10,... | collective-permute-start | bytes 393224 | tf_op jit(solution)/shard_map/ppermute | solution.py:23
  15.8 3.6 %collective-permute-done.4 = bf16[8,2,4096]{2,1,0:T(2,128)(2,1)S(1)} collective-permute-done((bf16[8,2,4096]{2,1,0:T(2,128)(2,1)S(1)}, bf16[8,2,4096]{2,1,0:T(2,128)(2,1)S(1)}, u32[]{:S(2)}, u32[]{:S(2)}) %collective-permute-start.4) | collective-permute-done | bytes 131104 | tf_op jit(solution)/shard_map/ppermute | solution.py:23
  20.2 2.0 %collective-permute-start = (bf16[16,2048]{1,0:T(8,128)(2,1)}, bf16[16,2048]{1,0:T(8,128)(2,1)S(1)}, u32[]{:S(2)}, u32[]{:S(2)}) collective-permute-start(bf16[16,2048]{1,0:T(8,128)(2,1)} %bitcast.115), channel_id=1, source_target_pairs={{0,3},{1,2},{2,1},{3,0},{4,7},{5,6},{6,5},{7,4},{8,11},{9,10},{10,... | collective-permute-start | bytes 196616 | tf_op jit(solution)/shard_map/ppermute | solution.py:23
  22.2 2.5 %shard_map.76 = (bf16[64,4096]{1,0:T(8,128)(2,1)S(1)}, f32[32,2048]{1,0:T(8,128)S(1)}, f32[32,2048]{1,0:T(8,128)S(1)}) custom-call(bf16[2,8,2,4096]{3,2,1,0:T(2,128)(2,1)S(1)} %pad_maximum_fusion.part_ref, bf16[2,8,2,4096]{3,2,1,0:T(2,128)(2,1)S(1)} %collective-permute-done.5.far_ref, bf16[1024,2048]{1,0:T(8,128)(2,1)} %refs_2_.1), custom_call_target="tpu_custom_call" | custom-call | flops 268435456 | bytes 4194304 | tf_op jit(solution)/shard_map/pallas_call | solution.py:98
  24.9 0.9 %stack.44 = bf16[1,8,2,2048]{3,2,1,0:T(2,128)(2,1)S(1)} reshape(bf16[1,16,2048]{2,1,0:T(8,128)(2,1)} %param.7) | data formatting | bytes 131072 | tf_op jit(solution)/shard_map/stack | solution.py:230
  26.4 0.8 %gather_fusion = bf16[8,2,2,2048]{3,2,1,0:T(2,128)(2,1)S(1)} fusion(bf16[2,8,2,2048]{3,2,1,0:T(2,128)(2,1)S(1)} %pad_maximum_fusion.2, s32[1024]{0:T(1024)S(1)} %pad_clamp_fusion), kind=kCustom, calls=%fused_computation | custom fusion | bytes 262176 | tf_op jit(solution)/shard_map/jit(_take)/gather | solution.py:231
  27.4 2.5 %shard_map.77 = (f32[32,2048]{1,0:T(8,128)S(1)}, f32[32,2048]{1,0:T(8,128)S(1)}) custom-call(bf16[64,4096]{1,0:T(8,128)(2,1)S(1)} %get-tuple-element.15.feats_ref.rows_ref, bf16[1024,2048]{1,0:T(8,128)(2,1)} %refs_1_.1), custom_call_target="tpu_custom_call" | custom-call | flops 268435456 | bytes 4194304 | tf_op jit(solution)/shard_map/pallas_call | solution.py:98
  30.4 1.2 %collective-permute-start.7 = (bf16[32,2048]{1,0:T(8,128)(2,1)S(1)}, bf16[32,2048]{1,0:T(8,128)(2,1)S(1)}, u32[]{:S(2)}, u32[]{:S(2)}) collective-permute-start(bf16[32,2048]{1,0:T(8,128)(2,1)S(1)} %add_convert_fusion.1), channel_id=1, source_target_pairs={{0,3},{1,2},{2,1},{3,0},{4,7},{5,6},{6,5},{7,4},{8,11},{9,10},{10,... | collective-permute-start | bytes 393224 | tf_op jit(solution)/shard_map/ppermute | solution.py:23
  31.6 1.4 %collective-permute-start.9 = (bf16[32,2048]{1,0:T(8,128)(2,1)S(1)}, bf16[32,2048]{1,0:T(8,128)(2,1)S(1)}, u32[]{:S(2)}, u32[]{:S(2)}) collective-permute-start(bf16[32,2048]{1,0:T(8,128)(2,1)S(1)} %add_convert_fusion), channel_id=1, source_target_pairs={{0,3},{1,2},{2,1},{3,0},{4,7},{5,6},{6,5},{7,4},{8,11},{9,10},{10,... | collective-permute-start | bytes 393224 | tf_op jit(solution)/shard_map/ppermute | solution.py:23
  33.0 3.0 %collective-permute-done.7 = bf16[32,2048]{1,0:T(8,128)(2,1)S(1)} collective-permute-done((bf16[32,2048]{1,0:T(8,128)(2,1)S(1)}, bf16[32,2048]{1,0:T(8,128)(2,1)S(1)}, u32[]{:S(2)}, u32[]{:S(2)}) %collective-permute-start.7) | collective-permute-done | bytes 131104 | tf_op jit(solution)/shard_map/ppermute | solution.py:23
  36.1 0.8 %collective-permute-start.11 = (bf16[32,2048]{1,0:T(8,128)(2,1)S(1)}, bf16[32,2048]{1,0:T(8,128)(2,1)S(1)}, u32[]{:S(2)}, u32[]{:S(2)}) collective-permute-start(bf16[32,2048]{1,0:T(8,128)(2,1)S(1)} %get-tuple-element.19), channel_id=1, source_target_pairs={{0,1},{1,0},{2,3},{3,2},{4,5},{5,4},{6,7},{7,6},{8,9},{9,8},{10,11... | collective-permute-start | bytes 393224 | tf_op jit(solution)/shard_map/ppermute | solution.py:23
  36.9 1.9 %collective-permute-done.9 = bf16[32,2048]{1,0:T(8,128)(2,1)S(1)} collective-permute-done((bf16[32,2048]{1,0:T(8,128)(2,1)S(1)}, bf16[32,2048]{1,0:T(8,128)(2,1)S(1)}, u32[]{:S(2)}, u32[]{:S(2)}) %collective-permute-start.9) | collective-permute-done | bytes 131104 | tf_op jit(solution)/shard_map/ppermute | solution.py:23
  39.9 2.7 %shard_map.78.refs_1_ = f32[64,1024]{1,0:T(8,128)S(1)} custom-call(bf16[64,2048]{1,0:T(8,128)(2,1)S(1)} %constant_dynamic-update-slice_fusion.refs_0_.grad_ref, bf16[1024,2048]{1,0:T(8,128)(2,1)} %refs_1_.1), custom_call_target="tpu_custom_call" | custom-call | flops 268435456 | bytes 4194304 | tf_op jit(solution)/shard_map/pallas_call | solution.py:98
  42.7 2.7 %shard_map.79 = f32[64,1024]{1,0:T(8,128)S(1)} custom-call(bf16[64,2048]{1,0:T(8,128)(2,1)S(1)} %pad_maximum_fusion.1.refs_0_.grad_ref, f32[64,1024]{1,0:T(8,128)S(1)} %shard_map.78.refs_1_, bf16[1024,2048]{1,0:T(8,128)(2,1)} %refs_2_.1), custom_call_target="tpu_custom_call" | custom-call | flops 268435456 | bytes 4194304 | tf_op jit(solution)/shard_map/pallas_call | solution.py:98
  45.5 1.6 %collective-permute-start.12 = (f32[2,2,4,2,1024]{4,3,2,1,0:T(2,128)S(1)}, f32[2,2,4,2,1024]{4,3,2,1,0:T(2,128)S(1)}, u32[]{:S(2)}, u32[]{:S(2)}) collective-permute-start(f32[2,2,4,2,1024]{4,3,2,1,0:T(2,128)S(1)} %slice_bitcast_fusion), channel_id=1, source_target_pairs={{0,4},{1,5},{2,6},{3,7},{4,0},{5,1},{6,2},{7,3},{8,12},{9,13},{10,... | collective-permute-start | bytes 393224 | tf_op jit(solution)/shard_map/ppermute | solution.py:23
  47.1 0.7 broadcast_select_fusion.1
  47.8 3.6 %collective-permute-done.12 = f32[2,2,4,2,1024]{4,3,2,1,0:T(2,128)S(1)} collective-permute-done((f32[2,2,4,2,1024]{4,3,2,1,0:T(2,128)S(1)}, f32[2,2,4,2,1024]{4,3,2,1,0:T(2,128)S(1)}, u32[]{:S(2)}, u32[]{:S(2)}) %collective-permute-start.12) | collective-permute-done | bytes 131104 | tf_op jit(solution)/shard_map/ppermute | solution.py:23
  51.5 1.6 %collective-permute-start.13 = (f32[2,2,2,2,1024]{4,3,2,1,0:T(2,128)S(1)}, f32[2,2,2,2,1024]{4,3,2,1,0:T(2,128)S(1)}, u32[]{:S(2)}, u32[]{:S(2)}) collective-permute-start(f32[2,2,2,2,1024]{4,3,2,1,0:T(2,128)S(1)} %slice_bitcast_fusion.2), channel_id=1, source_target_pairs={{0,8},{1,9},{2,10},{3,11},{4,12},{5,13},{6,14},{7,15},{8,0},{9,1},... | collective-permute-start | bytes 196616 | tf_op jit(solution)/shard_map/ppermute | solution.py:23
  53.1 4.0 %shard_map.80.rest_0_ = bf16[4096,2048]{1,0:T(8,128)(2,1)} custom-call(bf16[64,4096]{1,0:T(8,128)(2,1)S(1)} %get-tuple-element.15.feats_ref.rows_ref, bf16[64,2048]{1,0:T(8,128)(2,1)S(1)} %pad_maximum_fusion.1.refs_0_.grad_ref), custom_call_target="tpu_custom_call" | custom-call | flops 536870912 | bytes 9175040 | tf_op jit(solution)/shard_map/pallas_call | solution.py:181
  57.1 4.0 %shard_map.83.rest_0_ = bf16[4096,2048]{1,0:T(8,128)(2,1)} custom-call(bf16[64,4096]{1,0:T(8,128)(2,1)S(1)} %get-tuple-element.15.feats_ref.rows_ref, bf16[64,2048]{1,0:T(8,128)(2,1)S(1)} %constant_dynamic-update-slice_fusion.refs_0_.grad_ref), custom_call_target="tpu_custom_call" | custom-call | flops 536870912 | bytes 9175040 | tf_op jit(solution)/shard_map/pallas_call | solution.py:181
  61.1 3.1 %collective-permute-start.14 = (f32[2,2,1,2,1024]{4,3,1,0,2:T(2,128)S(1)}, f32[2,2,1,2,1024]{4,3,1,0,2:T(2,128)S(1)}, u32[]{:S(2)}, u32[]{:S(2)}) collective-permute-start(f32[2,2,1,2,1024]{4,3,1,0,2:T(2,128)S(1)} %slice_bitcast_fusion.4), channel_id=1, source_target_pairs={{0,16},{1,17},{2,18},{3,19},{4,20},{5,21},{6,22},{7,23},{8,24},{9,... | collective-permute-start | bytes 98312 | tf_op jit(solution)/shard_map/ppermute | solution.py:23
  64.2 4.2 %shard_map.84 = bf16[4096,2048]{1,0:T(8,128)(2,1)} custom-call(bf16[64,4096]{1,0:T(8,128)(2,1)S(1)} %get-tuple-element.15.feats_ref.rows_ref, bf16[64,2048]{1,0:T(8,128)(2,1)S(1)} %constant_dynamic-update-slice_fusion.refs_0_.grad_ref, bf16[4096,2048]{1,0:T(8,128)(2,1)} %shard_map.83.rest_0_), custom_call_target="tpu_custom_call", output_to_operand_aliasing={{}: (2, {})} | custom-call | flops 536870912 | bytes 9175040 | tf_op jit(solution)/shard_map/pallas_call | solution.py:181
  68.5 2.6 %shard_map.81.rest_0_ = bf16[4096,2048]{1,0:T(8,128)(2,1)} custom-call(bf16[64,4096]{1,0:T(8,128)(2,1)S(1)} %get-tuple-element.15.feats_ref.rows_ref, bf16[64,2048]{1,0:T(8,128)(2,1)S(1)} %pad_maximum_fusion.1.refs_0_.grad_ref, bf16[4096,2048]{1,0:T(8,128)(2,1)} %shard_map.80.rest_0_), custom_call_target="tpu_custom_call", output_to_operand_aliasing={{}: (2, {})} | custom-call | flops 268435456 | bytes 4980736 | tf_op jit(solution)/shard_map/pallas_call | solution.py:181
  71.6 1.1 %collective-permute-start.16 = (bf16[2,2,1024]{2,1,0:T(2,128)(2,1)S(1)}, bf16[2,2,1024]{2,1,0:T(2,128)(2,1)S(1)}, u32[]{:S(2)}, u32[]{:S(2)}) collective-permute-start(bf16[2,2,1024]{2,1,0:T(2,128)(2,1)S(1)} %fusion.10), channel_id=1, source_target_pairs={{0,1},{1,0},{2,3},{3,2},{4,5},{5,4},{6,7},{7,6},{8,9},{9,8},{10,11... | collective-permute-start | bytes 24584 | tf_op jit(solution)/shard_map/ppermute | solution.py:23
  72.7 2.6 %shard_map.82 = bf16[4096,2048]{1,0:T(8,128)(2,1)} custom-call(bf16[64,4096]{1,0:T(8,128)(2,1)S(1)} %get-tuple-element.15.feats_ref.rows_ref, bf16[64,2048]{1,0:T(8,128)(2,1)S(1)} %pad_maximum_fusion.1.refs_0_.grad_ref, bf16[4096,2048]{1,0:T(8,128)(2,1)} %shard_map.81.rest_0_), custom_call_target="tpu_custom_call", output_to_operand_aliasing={{}: (2, {})} | custom-call | flops 268435456 | bytes 4980736 | tf_op jit(solution)/shard_map/pallas_call | solution.py:181
  (58 shorter events, 5.5 us)
Async XLA Ops:
  0.6 5.2 %collective-permute-start.1 = (bf16[1,2,4096]{2,1,0:T(2,128)(2,1)}, bf16[1,2,4096]{2,1,0:T(2,128)(2,1)S(1)}, u32[]{:S(2)}, u32[]{:S(2)}) collective-permute-start(bf16[1,2,4096]{2,1,0:T(2,128)(2,1)} %in_ref.1), channel_id=1, source_target_pairs={{0,17},{1,16},{2,19},{3,18},{4,21},{5,20},{6,23},{7,22},{8,25},{9,... | collective-permute-start | bytes 49160 | tf_op jit(solution)/shard_map/ppermute | solution.py:23
  4.2 0.8 copy-start
  5.9 3.6 %collective-permute-start.2 = (bf16[2,2,4096]{2,1,0:T(2,128)(2,1)S(1)}, bf16[2,2,4096]{2,1,0:T(2,128)(2,1)S(1)}, u32[]{:S(2)}, u32[]{:S(2)}) collective-permute-start(bf16[2,2,4096]{2,1,0:T(2,128)(2,1)S(1)} %get-tuple-element.34), channel_id=1, source_target_pairs={{0,9},{1,8},{2,11},{3,10},{4,13},{5,12},{6,15},{7,14},{8,1},{9,0},... | collective-permute-start | bytes 98312 | tf_op jit(solution)/shard_map/ppermute | solution.py:23
  9.6 4.0 %collective-permute-start.3 = (bf16[4,2,4096]{2,1,0:T(2,128)(2,1)S(1)}, bf16[4,2,4096]{2,1,0:T(2,128)(2,1)S(1)}, u32[]{:S(2)}, u32[]{:S(2)}) collective-permute-start(bf16[4,2,4096]{2,1,0:T(2,128)(2,1)S(1)} %bitcast.112), channel_id=1, source_target_pairs={{0,5},{1,4},{2,7},{3,6},{4,1},{5,0},{6,3},{7,2},{8,13},{9,12},{10,... | collective-permute-start | bytes 196616 | tf_op jit(solution)/shard_map/ppermute | solution.py:23
  13.9 5.5 %collective-permute-start.4 = (bf16[8,2,4096]{2,1,0:T(2,128)(2,1)S(1)}, bf16[8,2,4096]{2,1,0:T(2,128)(2,1)S(1)}, u32[]{:S(2)}, u32[]{:S(2)}) collective-permute-start(bf16[8,2,4096]{2,1,0:T(2,128)(2,1)S(1)} %bitcast.110), channel_id=1, source_target_pairs={{0,3},{1,2},{2,1},{3,0},{4,7},{5,6},{6,5},{7,4},{8,11},{9,10},{10,... | collective-permute-start | bytes 393224 | tf_op jit(solution)/shard_map/ppermute | solution.py:23
  19.8 2.4 %collective-permute-start.5 = (bf16[2,8,2,4096]{3,2,1,0:T(2,128)(2,1)S(1)}, bf16[2,8,2,4096]{3,2,1,0:T(2,128)(2,1)S(1)}, u32[]{:S(2)}, u32[]{:S(2)}) collective-permute-start(bf16[2,8,2,4096]{3,2,1,0:T(2,128)(2,1)S(1)} %pad_maximum_fusion.part_ref), channel_id=1, source_target_pairs={{0,1},{1,0},{2,3},{3,2},{4,5},{5,4},{6,7},{7,6},{8,9},{9,8},{10,11... | collective-permute-start | bytes 786440 | tf_op jit(solution)/shard_map/ppermute | solution.py:23
  20.2 6.0 %collective-permute-start = (bf16[16,2048]{1,0:T(8,128)(2,1)}, bf16[16,2048]{1,0:T(8,128)(2,1)S(1)}, u32[]{:S(2)}, u32[]{:S(2)}) collective-permute-start(bf16[16,2048]{1,0:T(8,128)(2,1)} %bitcast.115), channel_id=1, source_target_pairs={{0,3},{1,2},{2,1},{3,0},{4,7},{5,6},{6,5},{7,4},{8,11},{9,10},{10,... | collective-permute-start | bytes 196616 | tf_op jit(solution)/shard_map/ppermute | solution.py:23
  24.7 5.6 %collective-permute-start.6 = (f32[32,2048]{1,0:T(8,128)S(1)}, f32[32,2048]{1,0:T(8,128)S(1)}, u32[]{:S(2)}, u32[]{:S(2)}) collective-permute-start(f32[32,2048]{1,0:T(8,128)S(1)} %get-tuple-element.13), channel_id=1, source_target_pairs={{0,1},{1,0},{2,3},{3,2},{4,5},{5,4},{6,7},{7,6},{8,9},{9,8},{10,11... | collective-permute-start | bytes 786440 | tf_op jit(solution)/shard_map/ppermute | solution.py:23
  29.9 1.7 %collective-permute-start.8 = (f32[32,2048]{1,0:T(8,128)S(1)}, f32[32,2048]{1,0:T(8,128)S(1)}, u32[]{:S(2)}, u32[]{:S(2)}) collective-permute-start(f32[32,2048]{1,0:T(8,128)S(1)} %get-tuple-element.17), channel_id=1, source_target_pairs={{0,1},{1,0},{2,3},{3,2},{4,5},{5,4},{6,7},{7,6},{8,9},{9,8},{10,11... | collective-permute-start | bytes 786440 | tf_op jit(solution)/shard_map/ppermute | solution.py:23
  30.4 5.6 %collective-permute-start.7 = (bf16[32,2048]{1,0:T(8,128)(2,1)S(1)}, bf16[32,2048]{1,0:T(8,128)(2,1)S(1)}, u32[]{:S(2)}, u32[]{:S(2)}) collective-permute-start(bf16[32,2048]{1,0:T(8,128)(2,1)S(1)} %add_convert_fusion.1), channel_id=1, source_target_pairs={{0,3},{1,2},{2,1},{3,0},{4,7},{5,6},{6,5},{7,4},{8,11},{9,10},{10,... | collective-permute-start | bytes 393224 | tf_op jit(solution)/shard_map/ppermute | solution.py:23
  31.6 7.1 %collective-permute-start.9 = (bf16[32,2048]{1,0:T(8,128)(2,1)S(1)}, bf16[32,2048]{1,0:T(8,128)(2,1)S(1)}, u32[]{:S(2)}, u32[]{:S(2)}) collective-permute-start(bf16[32,2048]{1,0:T(8,128)(2,1)S(1)} %add_convert_fusion), channel_id=1, source_target_pairs={{0,3},{1,2},{2,1},{3,0},{4,7},{5,6},{6,5},{7,4},{8,11},{9,10},{10,... | collective-permute-start | bytes 393224 | tf_op jit(solution)/shard_map/ppermute | solution.py:23
  36.1 3.8 %collective-permute-start.11 = (bf16[32,2048]{1,0:T(8,128)(2,1)S(1)}, bf16[32,2048]{1,0:T(8,128)(2,1)S(1)}, u32[]{:S(2)}, u32[]{:S(2)}) collective-permute-start(bf16[32,2048]{1,0:T(8,128)(2,1)S(1)} %get-tuple-element.19), channel_id=1, source_target_pairs={{0,1},{1,0},{2,3},{3,2},{4,5},{5,4},{6,7},{7,6},{8,9},{9,8},{10,11... | collective-permute-start | bytes 393224 | tf_op jit(solution)/shard_map/ppermute | solution.py:23
  39.7 2.9 %collective-permute-start.10 = (bf16[32,2048]{1,0:T(8,128)(2,1)S(1)}, bf16[32,2048]{1,0:T(8,128)(2,1)S(1)}, u32[]{:S(2)}, u32[]{:S(2)}) collective-permute-start(bf16[32,2048]{1,0:T(8,128)(2,1)S(1)} %get-tuple-element.22), channel_id=1, source_target_pairs={{0,1},{1,0},{2,3},{3,2},{4,5},{5,4},{6,7},{7,6},{8,9},{9,8},{10,11... | collective-permute-start | bytes 393224 | tf_op jit(solution)/shard_map/ppermute | solution.py:23
  45.5 5.9 %collective-permute-start.12 = (f32[2,2,4,2,1024]{4,3,2,1,0:T(2,128)S(1)}, f32[2,2,4,2,1024]{4,3,2,1,0:T(2,128)S(1)}, u32[]{:S(2)}, u32[]{:S(2)}) collective-permute-start(f32[2,2,4,2,1024]{4,3,2,1,0:T(2,128)S(1)} %slice_bitcast_fusion), channel_id=1, source_target_pairs={{0,4},{1,5},{2,6},{3,7},{4,0},{5,1},{6,2},{7,3},{8,12},{9,13},{10,... | collective-permute-start | bytes 393224 | tf_op jit(solution)/shard_map/ppermute | solution.py:23
  51.5 9.6 %collective-permute-start.13 = (f32[2,2,2,2,1024]{4,3,2,1,0:T(2,128)S(1)}, f32[2,2,2,2,1024]{4,3,2,1,0:T(2,128)S(1)}, u32[]{:S(2)}, u32[]{:S(2)}) collective-permute-start(f32[2,2,2,2,1024]{4,3,2,1,0:T(2,128)S(1)} %slice_bitcast_fusion.2), channel_id=1, source_target_pairs={{0,8},{1,9},{2,10},{3,11},{4,12},{5,13},{6,14},{7,15},{8,0},{9,1},... | collective-permute-start | bytes 196616 | tf_op jit(solution)/shard_map/ppermute | solution.py:23
  61.1 7.2 %collective-permute-start.14 = (f32[2,2,1,2,1024]{4,3,1,0,2:T(2,128)S(1)}, f32[2,2,1,2,1024]{4,3,1,0,2:T(2,128)S(1)}, u32[]{:S(2)}, u32[]{:S(2)}) collective-permute-start(f32[2,2,1,2,1024]{4,3,1,0,2:T(2,128)S(1)} %slice_bitcast_fusion.4), channel_id=1, source_target_pairs={{0,16},{1,17},{2,18},{3,19},{4,20},{5,21},{6,22},{7,23},{8,24},{9,... | collective-permute-start | bytes 98312 | tf_op jit(solution)/shard_map/ppermute | solution.py:23
  68.4 3.2 %collective-permute-start.15 = (bf16[2,2,1024]{2,1,0:T(2,128)(2,1)S(1)}, bf16[2,2,1024]{2,1,0:T(2,128)(2,1)S(1)}, u32[]{:S(2)}, u32[]{:S(2)}) collective-permute-start(bf16[2,2,1024]{2,1,0:T(2,128)(2,1)S(1)} %get-tuple-element.36), channel_id=1, source_target_pairs={{0,3},{1,2},{2,1},{3,0},{4,7},{5,6},{6,5},{7,4},{8,11},{9,10},{10,... | collective-permute-start | bytes 24584 | tf_op jit(solution)/shard_map/ppermute | solution.py:23
  71.6 3.7 %collective-permute-start.16 = (bf16[2,2,1024]{2,1,0:T(2,128)(2,1)S(1)}, bf16[2,2,1024]{2,1,0:T(2,128)(2,1)S(1)}, u32[]{:S(2)}, u32[]{:S(2)}) collective-permute-start(bf16[2,2,1024]{2,1,0:T(2,128)(2,1)S(1)} %fusion.10), channel_id=1, source_target_pairs={{0,1},{1,0},{2,3},{3,2},{4,5},{5,4},{6,7},{7,6},{8,9},{9,8},{10,11... | collective-permute-start | bytes 24584 | tf_op jit(solution)/shard_map/ppermute | solution.py:23

commit v7 on v5

--- a/solution.py
+++ b/solution.py
@@ -52,29 +52,87 @@
     )(value)
 
 
-def pieces_of(weight_ref, buf, sem):
-    tall = buf.shape[1]
-    return [
-        pltpu.make_async_copy(weight_ref.at[pl.ds(i * tall, tall), :], buf.at[i], sem.at[i]) for i in range(PIECES)
+def reorder_kernel(in_ref, out_ref, *, rt):
+    rows = in_ref.shape[0]
+    to = lax.broadcasted_iota(jnp.int32, (rows, rows), 0)
+    source = lax.broadcasted_iota(jnp.int32, (rows, rows), 1)
+    pick = ((to ^ (lax.axis_index("tp") * rt)) == source).astype(F32).astype(BF16)
+    out_ref[...] = jnp.dot(pick, in_ref[...], preferred_element_type=F32).astype(BF16)
+
+
+def reorder(value, rt):
+    assert rt & (rt - 1) == 0
+    return pl.pallas_call(
+        functools.partial(reorder_kernel, rt=rt),
+        in_specs=[VMEM],
+        out_specs=VMEM,
+        out_shape=jax.ShapeDtypeStruct(value.shape, BF16),
+        compiler_params=pltpu.CompilerParams(vmem_limit_bytes=8 << 20),
+        cost_estimate=pl.CostEstimate(flops=0, bytes_accessed=4 * value.size, transcendentals=0),
+    )(value)
+
+
+def load_kernel(weight_ref, out_ref, sem, *, begin):
+    tall = out_ref.shape[0] // 2
+    copies = [
+        pltpu.make_async_copy(
+            weight_ref.at[pl.ds(begin + i * tall, tall), :], out_ref.at[pl.ds(i * tall, tall), :], sem.at[i]
+        )
+        for i in range(2)
     ]
-
-
-def multiply(feats_ref, copies, buf, keep_ref, send_ref):
-    depth = buf.shape[1] * PIECES
+    for copy in copies:
+        copy.start()
+    for copy in copies:
+        copy.wait()
+
+
+def load(weight, part, parts):
+    depth, width = weight.shape
+    depth //= parts
+    return pl.pallas_call(
+        functools.partial(load_kernel, begin=part * depth),
+        in_specs=[HBM],
+        out_specs=VMEM,
+        out_shape=jax.ShapeDtypeStruct((depth, width), BF16),
+        scratch_shapes=[pltpu.SemaphoreType.DMA((2,))],
+        compiler_params=pltpu.CompilerParams(vmem_limit_bytes=48 << 20),
+        cost_estimate=pl.CostEstimate(flops=0, bytes_accessed=2 * depth * width, transcendentals=0),
+    )(weight)
+
+
+def add_product(feats_ref, at, weight, keep_ref, send_ref):
     half = keep_ref.shape[0]
-    first = lax.axis_index("dp") * depth
+    start = pl.multiple_of(lax.axis_index("dp") * at[1] + at[0], weight.shape[0])
+    out = jnp.dot(feats_ref[:, pl.ds(start, weight.shape[0])], weight, preferred_element_type=F32)
+    if at[0]:
+        keep_ref[...] += out[:half]
+        send_ref[...] += out[half:]
+    else:
+        keep_ref[...] = out[:half]
+        send_ref[...] = out[half:]
+
+
+def stream_product(feats_ref, copies, held_ref, keep_ref, send_ref):
+    depth = held_ref.shape[0]
+    tall = depth // PIECES
     for i, copy in enumerate(copies):
         copy.wait()
-        at = pl.multiple_of(first + i * buf.shape[1], buf.shape[1])
-        out = jnp.dot(feats_ref[:, pl.ds(at, buf.shape[1])], buf[i], preferred_element_type=F32)
-        keep_ref[...] = out[:half] if i == 0 else keep_ref[...] + out[:half]
-        send_ref[...] = out[half:] if i == 0 else send_ref[...] + out[half:]
-
-
-def gather_kernel(part_ref, far_ref, weight_ref, feats_ref, keep_ref, send_ref, buf, sem):
-    copies = pieces_of(weight_ref, buf, sem)
+        add_product(feats_ref, (i * tall, depth), held_ref[i * tall : (i + 1) * tall, :], keep_ref, send_ref)
+
+
+def start_copies(weight_ref, held_ref, sem):
+    tall = held_ref.shape[0] // PIECES
+    parts = [pl.ds(i * tall, tall) for i in range(PIECES)]
+    copies = [
+        pltpu.make_async_copy(weight_ref.at[at, :], held_ref.at[at, :], sem.at[i]) for i, at in enumerate(parts)
+    ]
     for copy in copies:
         copy.start()
+    return copies
+
+
+def gather_kernel(part_ref, far_ref, weight_ref, held_ref, keep_ref, send_ref, feats_ref, sem):
+    copies = start_copies(weight_ref, held_ref, sem)
     _, n_tp, rt, _ = part_ref.shape
     for core in range(2):
         for x in range(2):
@@ -82,69 +140,84 @@
                 source = part_ref if odd(k) == core else far_ref
                 row = ((core * 2 + x) * n_tp + k) * rt
                 feats_ref[row : row + rt, :] = source[x, k]
-    multiply(feats_ref, copies, buf, keep_ref, send_ref)
-
-
-def ahead_kernel(feats_ref, weight_ref, keep_ref, send_ref, buf, sem):
-    copies = pieces_of(weight_ref, buf, sem)
-    for copy in copies:
-        copy.start()
-    multiply(feats_ref, copies, buf, keep_ref, send_ref)
-
-
-def stream(kernel, args, weight, outs, flops, pieces=None):
-    depth, width = weight.shape
-    pieces = pieces or (PIECES, depth // PIECES, width)
-    return pl.pallas_call(
-        kernel,
-        in_specs=[VMEM] * len(args) + [HBM],
-        out_specs=[VMEM] * len(outs),
-        out_shape=outs,
-        scratch_shapes=[pltpu.VMEM(pieces, BF16), pltpu.SemaphoreType.DMA((pieces[0],))],
-        compiler_params=pltpu.CompilerParams(vmem_limit_bytes=52 << 20),
-        cost_estimate=pl.CostEstimate(flops=flops, bytes_accessed=2 * weight.size, transcendentals=0),
-    )(*args, weight)
+    stream_product(feats_ref, copies, held_ref, keep_ref, send_ref)
+
+
+def stream_kernel(feats_ref, weight_ref, held_ref, keep_ref, send_ref, sem):
+    copies = start_copies(weight_ref, held_ref, sem)
+    stream_product(feats_ref, copies, held_ref, keep_ref, send_ref)
 
 
 def gather_ahead(part, far, weight):
     _, n_tp, rt, d_model = part.shape
     count, width = 4 * n_tp * rt, weight.shape[1]
     half = jax.ShapeDtypeStruct((count // 2, width), F32)
+    outs = [jax.ShapeDtypeStruct(weight.shape, BF16), half, half]
     if n_tp <= 16:
-        feats = jax.ShapeDtypeStruct((count, d_model), BF16)
-        return stream(gather_kernel, (part, far), weight, [feats, half, half], 2 * count * weight.size)
-    mask = jnp.array([odd(k) == 1 for k in range(n_tp)])[None, :, None, None]
-    feats = jnp.stack([jnp.where(mask, far, part), jnp.where(mask, part, far)]).reshape(count, d_model)
-    return feats, *ahead(feats, weight)
-
-
-def ahead(feats, weight):
-    half = jax.ShapeDtypeStruct((feats.shape[0] // 2, weight.shape[1]), F32)
-    return stream(ahead_kernel, (feats,), weight, [half, half], 2 * feats.shape[0] * weight.size)
-
-
-def back_kernel(*refs):
-    grad_ref, weight_ref, out_ref, buf, sem = refs[0], *refs[-4:]
-    count, _, wide = buf.shape
-    parts = [pl.ds(i * wide, wide) for i in range(count)]
-    copies = [pltpu.make_async_copy(weight_ref.at[:, at], buf.at[i], sem.at[i]) for i, at in enumerate(parts)]
-    for copy in copies:
-        copy.start()
-    for i, copy in enumerate(copies):
-        copy.wait()
-        out = lax.dot_general(grad_ref[:, parts[i]], buf[i], COLS, preferred_element_type=F32)
-        if i:
-            out_ref[...] += out
-        else:
-            out_ref[...] = out if len(refs) == 5 else refs[1][...] + out
-
-
-def back(grad, weight, start=None):
-    depth, width = weight.shape
-    pieces = PIECES if width % (128 * PIECES) == 0 else 1
-    out = jax.ShapeDtypeStruct((grad.shape[0], depth), F32)
-    args = (grad,) if start is None else (grad, start)
-    return stream(back_kernel, args, weight, [out], 2 * grad.shape[0] * weight.size, (pieces, depth, width // pieces))[0]
+        outs.append(jax.ShapeDtypeStruct((count, d_model), BF16))
+        kernel, args = gather_kernel, (part, far, weight)
+    else:
+        mask = jnp.array([odd(k) == 1 for k in range(n_tp)])[None, :, None, None]
+        feats = jnp.stack([jnp.where(mask, far, part), jnp.where(mask, part, far)]).reshape(count, d_model)
+        kernel, args = stream_kernel, (feats, weight)
+    held, keep, send, *rest = pl.pallas_call(
+        kernel,
+        in_specs=[VMEM] * (len(args) - 1) + [HBM],
+        out_specs=[VMEM] * len(outs),
+        out_shape=outs,
+        scratch_shapes=[pltpu.SemaphoreType.DMA((PIECES,))],
+        compiler_params=pltpu.CompilerParams(vmem_limit_bytes=46 << 20),
+        cost_estimate=pl.CostEstimate(
+            flops=2 * count * weight.size, bytes_accessed=2 * weight.size, transcendentals=0
+        ),
+    )(*args)
+    return rest[0] if rest else feats, held, keep, send
+
+
+def ahead_kernel(feats_ref, *refs):
+    weights, (keep_ref, send_ref) = refs[:-2], refs[-2:]
+    depth = sum(ref.shape[0] for ref in weights)
+    at = 0
+    for ref in weights:
+        add_product(feats_ref, (at, depth), ref[...], keep_ref, send_ref)
+        at += ref.shape[0]
+
+
+def ahead(feats, *weights):
+    half = jax.ShapeDtypeStruct((feats.shape[0] // 2, weights[0].shape[1]), F32)
+    return pl.pallas_call(
+        ahead_kernel,
+        in_specs=[VMEM] * (1 + len(weights)),
+        out_specs=[VMEM] * 2,
+        out_shape=[half, half],
+        compiler_params=pltpu.CompilerParams(vmem_limit_bytes=10 << 20),
+        cost_estimate=pl.CostEstimate(
+            flops=2 * feats.shape[0] * sum(w.size for w in weights), bytes_accessed=1 << 20, transcendentals=0
+        ),
+    )(feats, *weights)
+
+
+def back_kernel(*refs, parts):
+    grad_ref, weights, out_ref = refs[0], refs[1 : 1 + parts], refs[-1]
+    at = 0
+    for ref in weights:
+        out = lax.dot_general(grad_ref[...], ref[...], COLS, preferred_element_type=F32)
+        here = slice(at, at + ref.shape[0])
+        out_ref[:, here] = out if len(refs) == parts + 2 else refs[-2][:, here] + out
+        at += ref.shape[0]
+
+
+def back(grad, weights, start=None):
+    depth = sum(w.shape[0] for w in weights)
+    args = (grad, *weights) if start is None else (grad, *weights, start)
+    return pl.pallas_call(
+        functools.partial(back_kernel, parts=len(weights)),
+        in_specs=[VMEM] * len(args),
+        out_specs=VMEM,
+        out_shape=jax.ShapeDtypeStruct((grad.shape[0], depth), F32),
+        compiler_params=pltpu.CompilerParams(vmem_limit_bytes=10 << 20),
+        cost_estimate=pl.CostEstimate(flops=2 * grad.size * depth, bytes_accessed=1 << 20, transcendentals=0),
+    )(*args)
 
 
 def outer_kernel(rows_ref, grad_ref, *rest, base, scale):
@@ -197,11 +270,10 @@
 def shards(tokens, gate_weight, up_weight, cotangent):
     n_tp, n_dp = lax.axis_size("tp"), lax.axis_size("dp")
     assert n_dp == 4
-    t, r = lax.axis_index("tp"), lax.axis_index("dp")
+    r = lax.axis_index("dp")
     _, rt, d_model = tokens.shape
-    depth, width = gate_weight.shape
+    depth, _ = gate_weight.shape
     rows = rt * n_tp
-    order = t ^ jnp.arange(n_tp)
 
     part = hold(tokens)
     for i, bit in enumerate(bits_of(n_tp)):
@@ -209,8 +281,10 @@
         part = jnp.stack([part, near], axis=1).reshape(-1, rt, d_model)
     part = jnp.stack([part, swap(part, 0, 3)])
     far = swap(part, 0, 1)
-    feats, gate_keep, gate_send = gather_ahead(part, far, gate_weight)
-    up_keep, up_send = ahead(feats, up_weight)
+    feats, gate_held, gate_keep, gate_send = gather_ahead(part, far, gate_weight)
+    up_first = load(up_weight, 0, 2)
+    up_second = load(up_weight, 1, 2)
+    up_keep, up_send = ahead(feats, up_first, up_second)
 
     def partial(keep, send):
         other = swap(send, 0, 1)
@@ -226,10 +300,9 @@
     gate_pre = summed(half_gate)
     up_pre = summed(half_up)
 
-    cot = swap(cotangent[0], 0, 3)
-    near, cot, _ = lax.optimization_barrier((cotangent[0], cot, up_keep))
-    cot = jnp.stack([near, cot]).reshape(2, n_tp, rt, width)
-    cot = jnp.take(cot, order, axis=1).reshape(2 * rows, width)
+    cot = reorder(cotangent[0], rt)
+    far = swap(cot, 0, 3)
+    cot = jnp.concatenate([cot, far])
 
     grad_hidden = cot.astype(F32)
     act, slope = swish_parts(gate_pre)
@@ -237,13 +310,13 @@
     d_up, act, slope = lax.optimization_barrier((d_up, act, slope))
     far = swap(d_up, 0, 1)
     d_up = jnp.concatenate([d_up, far])
-    total = back(d_up, up_weight)
-    hidden = (act * up_pre)[:rows].astype(BF16).reshape(n_tp, rt, width)
-    hidden = jnp.take(hidden, order, axis=0).reshape(1, rows, width)
+    total = back(d_up, (up_first, up_second))
+    hidden = (act * up_pre)[:rows].astype(BF16)
+    hidden = reorder(hidden, rt)[None]
     d_gate = (grad_hidden * up_pre * slope).astype(BF16)
     far = swap(d_gate, 0, 1)
     d_gate = jnp.concatenate([d_gate, far])
-    total = back(d_gate, gate_weight, total)
+    total = back(d_gate, (gate_held,), total)
 
     total = total.reshape(2, 2, n_tp, rt, depth)
     for bit in reversed(bits_of(n_tp)):

time: 76.2 us -> 71.4 us (0.937)
  local copies, waits for them, and re-layouts: 4.13 us -> 1.12 us
  starting transfers between devices: 23.3 us -> 21.7 us
  waiting for transfers between devices: 18.3 us -> 19.6 us
  other arithmetic: 2.76 us -> 1.79 us
    gather x5 -> x0, local copies, waits for them, and re-layouts: 1.67 us -> none  [the longest x3 0.95 us: shards(): cot = jnp.take(cot, order, axis=1).reshape(2 * rows, width)]
    ppermute x17, starting transfers between devices: 23.3 us -> 21.7 us  [swap(): return lax.ppermute(value, ('tp', 'dp'), pairs)]
    ppermute x17, waiting for transfers between devices: 18.3 us -> 19.6 us  [swap(): return lax.ppermute(value, ('tp', 'dp'), pairs)]
    another operation x2 -> x0, local copies, waits for them, and re-layouts: 0.95 us -> none  [shards(): cot = jnp.stack([near, cot]).reshape(2, n_tp, rt, width)]
    pallas_call x4 -> x8, Pallas kernels: 10.4 us -> 10.1 us  [the longest x2 3.12 us: load(): pl.pallas_call(functools.partial(load_kernel, begin=part * depth), in_spe...]
  transfers between devices with their start and end apart: 17 -> 17, of which waited for: 8 -> 9; matrix products, arithmetic and copies ran while one was open for 5% -> 0% of each run, Pallas kernels for 31% -> 31%
where the time goes in v7:
time: 71.4 us; the launch traced here: 71.1 us
  Pallas kernels  26 us (36%)
  starting transfers between devices  21.7 us (30%)
  waiting for transfers between devices  19.6 us (27%)
  other arithmetic  1.79 us (3%)
  local copies, waits for them, and re-layouts  1.12 us (2%)
  between operations  0.93 us (1%)
    ppermute x17, starting transfers between devices, swap(): return lax.ppermute(value, ('tp', 'dp'), pairs)  21.7 us
    ppermute x17, waiting for transfers between devices, swap(): return lax.ppermute(value, ('tp', 'dp'), pairs)  19.6 us
    pallas_call x4, Pallas kernels, outer(): pl.pallas_call(kernel, in_specs=[VMEM, VMEM] + [HBM] * (len(args) - 2), o...  15.9 us
    pallas_call x2, Pallas kernels, load(): pl.pallas_call(functools.partial(load_kernel, begin=part * depth), in_spe...  3.12 us
    pallas_call x2, Pallas kernels, back(): pl.pallas_call(functools.partial(back_kernel, parts=len(weights)), in_spe...  2.78 us
    pallas_call x1, Pallas kernels, gather_ahead(): pl.pallas_call(kernel, in_specs=[VMEM] * (len(args) - 1) + [HBM], out_spe...  2.51 us
  transfers between devices with their start and end apart: 17, of which 9 were waited for; matrix products, arithmetic and copies ran while one was open for 0% of the time, Pallas kernels for 31%

profile of v7, /device:TPU:0, one launch (start us, length us, event | category | flops | bytes accessed | tf_op | source)
XLA Modules:
  0.0 71.1 jit_solution(8901406955783464234)
XLA Ops:
  0.6 3.6 %collective-permute-start.1 = (bf16[1,2,4096]{2,1,0:T(2,128)(2,1)}, bf16[1,2,4096]{2,1,0:T(2,128)(2,1)S(1)}, u32[]{:S(2)}, u32[]{:S(2)}) collective-permute-start(bf16[1,2,4096]{2,1,0:T(2,128)(2,1)} %in_ref.1), channel_id=1, source_target_pairs={{0,17},{1,16},{2,19},{3,18},{4,21},{5,20},{6,23},{7,22},{8,25},{9,... | collective-permute-start | bytes 49160 | tf_op jit(solution)/shard_map/ppermute | solution.py:23
  4.2 0.7 %copy-done.1 = bf16[1,2,4096]{2,1,0:T(2,128)(2,1)S(1)} copy-done((bf16[1,2,4096]{2,1,0:T(2,128)(2,1)S(1)}, bf16[1,2,4096]{2,1,0:T(2,128)(2,1)}, u32[]{:S(2)}) %copy-start.1) | copy-done | bytes 16408
  5.0 0.9 %collective-permute-done.1 = bf16[1,2,4096]{2,1,0:T(2,128)(2,1)S(1)} collective-permute-done((bf16[1,2,4096]{2,1,0:T(2,128)(2,1)}, bf16[1,2,4096]{2,1,0:T(2,128)(2,1)S(1)}, u32[]{:S(2)}, u32[]{:S(2)}) %collective-permute-start.1) | collective-permute-done | bytes 16416 | tf_op jit(solution)/shard_map/ppermute | solution.py:23
  5.9 2.0 %collective-permute-start.2 = (bf16[2,2,4096]{2,1,0:T(2,128)(2,1)S(1)}, bf16[2,2,4096]{2,1,0:T(2,128)(2,1)S(1)}, u32[]{:S(2)}, u32[]{:S(2)}) collective-permute-start(bf16[2,2,4096]{2,1,0:T(2,128)(2,1)S(1)} %get-tuple-element.36), channel_id=1, source_target_pairs={{0,9},{1,8},{2,11},{3,10},{4,13},{5,12},{6,15},{7,14},{8,1},{9,0},... | collective-permute-start | bytes 98312 | tf_op jit(solution)/shard_map/ppermute | solution.py:23
  7.9 1.6 %collective-permute-done.2 = bf16[2,2,4096]{2,1,0:T(2,128)(2,1)S(1)} collective-permute-done((bf16[2,2,4096]{2,1,0:T(2,128)(2,1)S(1)}, bf16[2,2,4096]{2,1,0:T(2,128)(2,1)S(1)}, u32[]{:S(2)}, u32[]{:S(2)}) %collective-permute-start.2) | collective-permute-done | bytes 32800 | tf_op jit(solution)/shard_map/ppermute | solution.py:23
  9.6 1.8 %collective-permute-start.3 = (bf16[4,2,4096]{2,1,0:T(2,128)(2,1)S(1)}, bf16[4,2,4096]{2,1,0:T(2,128)(2,1)S(1)}, u32[]{:S(2)}, u32[]{:S(2)}) collective-permute-start(bf16[4,2,4096]{2,1,0:T(2,128)(2,1)S(1)} %bitcast.110), channel_id=1, source_target_pairs={{0,5},{1,4},{2,7},{3,6},{4,1},{5,0},{6,3},{7,2},{8,13},{9,12},{10,... | collective-permute-start | bytes 196616 | tf_op jit(solution)/shard_map/ppermute | solution.py:23
  11.4 2.2 %collective-permute-done.3 = bf16[4,2,4096]{2,1,0:T(2,128)(2,1)S(1)} collective-permute-done((bf16[4,2,4096]{2,1,0:T(2,128)(2,1)S(1)}, bf16[4,2,4096]{2,1,0:T(2,128)(2,1)S(1)}, u32[]{:S(2)}, u32[]{:S(2)}) %collective-permute-start.3) | collective-permute-done | bytes 65568 | tf_op jit(solution)/shard_map/ppermute | solution.py:23
  13.9 1.9 %collective-permute-start.4 = (bf16[8,2,4096]{2,1,0:T(2,128)(2,1)S(1)}, bf16[8,2,4096]{2,1,0:T(2,128)(2,1)S(1)}, u32[]{:S(2)}, u32[]{:S(2)}) collective-permute-start(bf16[8,2,4096]{2,1,0:T(2,128)(2,1)S(1)} %bitcast.108), channel_id=1, source_target_pairs={{0,3},{1,2},{2,1},{3,0},{4,7},{5,6},{6,5},{7,4},{8,11},{9,10},{10,... | collective-permute-start | bytes 393224 | tf_op jit(solution)/shard_map/ppermute | solution.py:23
  15.9 3.6 %collective-permute-done.4 = bf16[8,2,4096]{2,1,0:T(2,128)(2,1)S(1)} collective-permute-done((bf16[8,2,4096]{2,1,0:T(2,128)(2,1)S(1)}, bf16[8,2,4096]{2,1,0:T(2,128)(2,1)S(1)}, u32[]{:S(2)}, u32[]{:S(2)}) %collective-permute-start.4) | collective-permute-done | bytes 131104 | tf_op jit(solution)/shard_map/ppermute | solution.py:23
  20.2 1.2 %collective-permute-done.5.far_ref = bf16[2,8,2,4096]{3,2,1,0:T(2,128)(2,1)S(1)} collective-permute-done((bf16[2,8,2,4096]{3,2,1,0:T(2,128)(2,1)S(1)}, bf16[2,8,2,4096]{3,2,1,0:T(2,128)(2,1)S(1)}, u32[]{:S(2)}, u32[]{:S(2)}) %collective-permute-start.5) | collective-permute-done | bytes 262176 | tf_op jit(solution)/shard_map/ppermute | solution.py:23
  21.4 2.5 %shard_map.77 = (bf16[1024,2048]{1,0:T(8,128)(2,1)S(1)}, f32[32,2048]{1,0:T(8,128)S(1)}, f32[32,2048]{1,0:T(8,128)S(1)}, bf16[64,4096]{1,0:T(8,128)(2,1)S(1)}) custom-call(bf16[2,8,2,4096]{3,2,1,0:T(2,128)(2,1)S(1)} %pad_maximum_fusion.part_ref, bf16[2,8,2,4096]{3,2,1,0:T(2,128)(2,1)S(1)} %collective-permute-done.5.far_ref, bf16[1024,2048]{1,0:T(8,128)(2,1)} %weight_ref.3), custom_call_target="tpu_custom_call" | custom-call | flops 268435456 | bytes 4194304 | tf_op jit(solution)/shard_map/pallas_call | solution.py:163
  24.4 2.1 %collective-permute-start = (bf16[16,2048]{1,0:T(8,128)(2,1)S(1)}, bf16[16,2048]{1,0:T(8,128)(2,1)S(1)}, u32[]{:S(2)}, u32[]{:S(2)}) collective-permute-start(bf16[16,2048]{1,0:T(8,128)(2,1)S(1)} %shard_map.75), channel_id=1, source_target_pairs={{0,3},{1,2},{2,1},{3,0},{4,7},{5,6},{6,5},{7,4},{8,11},{9,10},{10,... | collective-permute-start | bytes 196616 | tf_op jit(solution)/shard_map/ppermute | solution.py:23
  26.5 1.6 %shard_map.79.refs_1_.refs_2_ = bf16[512,2048]{1,0:T(8,128)(2,1)S(1)} custom-call(bf16[1024,2048]{1,0:T(8,128)(2,1)} %weight_ref.5), custom_call_target="tpu_custom_call" | custom-call | bytes 2097152 | tf_op jit(solution)/shard_map/pallas_call | solution.py:92
  28.1 1.6 %shard_map.78.refs_0_.refs_1_ = bf16[512,2048]{1,0:T(8,128)(2,1)S(1)} custom-call(bf16[1024,2048]{1,0:T(8,128)(2,1)} %weight_ref.5), custom_call_target="tpu_custom_call" | custom-call | bytes 2097152 | tf_op jit(solution)/shard_map/pallas_call | solution.py:92
  29.6 0.8 %shard_map.80 = (f32[32,2048]{1,0:T(8,128)S(1)}, f32[32,2048]{1,0:T(8,128)S(1)}) custom-call(bf16[64,4096]{1,0:T(8,128)(2,1)S(1)} %get-tuple-element.16.feats_ref.rows_ref, bf16[512,2048]{1,0:T(8,128)(2,1)S(1)} %shard_map.78.refs_0_.refs_1_, bf16[512,2048]{1,0:T(8,128)(2,1)S(1)} %shard_map.79.refs_1_.refs_2_), custom_call_target="tpu_custom_call" | custom-call | flops 268435456 | bytes 1048576 | tf_op jit(solution)/shard_map/pallas_call | solution.py:188
  30.8 1.3 %collective-permute-done.8 = f32[32,2048]{1,0:T(8,128)S(1)} collective-permute-done((f32[32,2048]{1,0:T(8,128)S(1)}, f32[32,2048]{1,0:T(8,128)S(1)}, u32[]{:S(2)}, u32[]{:S(2)}) %collective-permute-start.8) | collective-permute-done | bytes 262176 | tf_op jit(solution)/shard_map/ppermute | solution.py:23
  32.6 3.4 %collective-permute-done.7 = bf16[32,2048]{1,0:T(8,128)(2,1)S(1)} collective-permute-done((bf16[32,2048]{1,0:T(8,128)(2,1)S(1)}, bf16[32,2048]{1,0:T(8,128)(2,1)S(1)}, u32[]{:S(2)}, u32[]{:S(2)}) %collective-permute-start.7) | collective-permute-done | bytes 131104 | tf_op jit(solution)/shard_map/ppermute | solution.py:23
  36.2 1.3 %collective-permute-start.11 = (bf16[32,2048]{1,0:T(8,128)(2,1)S(1)}, bf16[32,2048]{1,0:T(8,128)(2,1)S(1)}, u32[]{:S(2)}, u32[]{:S(2)}) collective-permute-start(bf16[32,2048]{1,0:T(8,128)(2,1)S(1)} %get-tuple-element.21), channel_id=1, source_target_pairs={{0,1},{1,0},{2,3},{3,2},{4,5},{5,4},{6,7},{7,6},{8,9},{9,8},{10,11... | collective-permute-start | bytes 393224 | tf_op jit(solution)/shard_map/ppermute | solution.py:23
  37.5 1.4 %collective-permute-done.9 = bf16[32,2048]{1,0:T(8,128)(2,1)S(1)} collective-permute-done((bf16[32,2048]{1,0:T(8,128)(2,1)S(1)}, bf16[32,2048]{1,0:T(8,128)(2,1)S(1)}, u32[]{:S(2)}, u32[]{:S(2)}) %collective-permute-start.9) | collective-permute-done | bytes 131104 | tf_op jit(solution)/shard_map/ppermute | solution.py:23
  39.4 1.4 %shard_map.82.refs_2_ = f32[64,1024]{1,0:T(8,128)S(1)} custom-call(bf16[64,2048]{1,0:T(8,128)(2,1)S(1)} %constant_dynamic-update-slice_fusion.refs_0_.grad_ref, bf16[512,2048]{1,0:T(8,128)(2,1)S(1)} %shard_map.78.refs_0_.refs_1_, bf16[512,2048]{1,0:T(8,128)(2,1)S(1)} %shard_map.79.refs_1_.refs_2_), custom_call_target="tpu_custom_call" | custom-call | flops 268435456 | bytes 1048576 | tf_op jit(solution)/shard_map/pallas_call | solution.py:213
  40.8 1.4 %shard_map.83 = f32[64,1024]{1,0:T(8,128)S(1)} custom-call(bf16[64,2048]{1,0:T(8,128)(2,1)S(1)} %pad_maximum_fusion.1.refs_0_.grad_ref, bf16[1024,2048]{1,0:T(8,128)(2,1)S(1)} %get-tuple-element.20.refs_1_, f32[64,1024]{1,0:T(8,128)S(1)} %shard_map.82.refs_2_), custom_call_target="tpu_custom_call" | custom-call | flops 268435456 | bytes 1048576 | tf_op jit(solution)/shard_map/pallas_call | solution.py:213
  42.4 1.6 %collective-permute-start.12 = (f32[2,2,4,2,1024]{4,3,2,1,0:T(2,128)S(1)}, f32[2,2,4,2,1024]{4,3,2,1,0:T(2,128)S(1)}, u32[]{:S(2)}, u32[]{:S(2)}) collective-permute-start(f32[2,2,4,2,1024]{4,3,2,1,0:T(2,128)S(1)} %slice_bitcast_fusion), channel_id=1, source_target_pairs={{0,4},{1,5},{2,6},{3,7},{4,0},{5,1},{6,2},{7,3},{8,12},{9,13},{10,... | collective-permute-start | bytes 393224 | tf_op jit(solution)/shard_map/ppermute | solution.py:23
  44.0 4.0 %collective-permute-done.12 = f32[2,2,4,2,1024]{4,3,2,1,0:T(2,128)S(1)} collective-permute-done((f32[2,2,4,2,1024]{4,3,2,1,0:T(2,128)S(1)}, f32[2,2,4,2,1024]{4,3,2,1,0:T(2,128)S(1)}, u32[]{:S(2)}, u32[]{:S(2)}) %collective-permute-start.12) | collective-permute-done | bytes 131104 | tf_op jit(solution)/shard_map/ppermute | solution.py:23
  48.1 1.6 %collective-permute-start.13 = (f32[2,2,2,2,1024]{4,3,2,1,0:T(2,128)S(1)}, f32[2,2,2,2,1024]{4,3,2,1,0:T(2,128)S(1)}, u32[]{:S(2)}, u32[]{:S(2)}) collective-permute-start(f32[2,2,2,2,1024]{4,3,2,1,0:T(2,128)S(1)} %slice_bitcast_fusion.2), channel_id=1, source_target_pairs={{0,8},{1,9},{2,10},{3,11},{4,12},{5,13},{6,14},{7,15},{8,0},{9,1},... | collective-permute-start | bytes 196616 | tf_op jit(solution)/shard_map/ppermute | solution.py:23
  49.7 0.8 %shard_map.81 = bf16[16,2048]{1,0:T(8,128)(2,1)} custom-call(bf16[16,2048]{1,0:T(8,128)(2,1)S(1)} %fusion.5.in_ref), custom_call_target="tpu_custom_call" | custom-call | bytes 131072 | tf_op jit(solution)/shard_map/pallas_call | solution.py:65
  50.5 4.0 %shard_map.84.rest_0_ = bf16[4096,2048]{1,0:T(8,128)(2,1)} custom-call(bf16[64,4096]{1,0:T(8,128)(2,1)S(1)} %get-tuple-element.16.feats_ref.rows_ref, bf16[64,2048]{1,0:T(8,128)(2,1)S(1)} %pad_maximum_fusion.1.refs_0_.grad_ref), custom_call_target="tpu_custom_call" | custom-call | flops 536870912 | bytes 9175040 | tf_op jit(solution)/shard_map/pallas_call | solution.py:254
  54.5 3.1 %collective-permute-start.14 = (f32[2,2,1,2,1024]{4,3,1,0,2:T(2,128)S(1)}, f32[2,2,1,2,1024]{4,3,1,0,2:T(2,128)S(1)}, u32[]{:S(2)}, u32[]{:S(2)}) collective-permute-start(f32[2,2,1,2,1024]{4,3,1,0,2:T(2,128)S(1)} %slice_bitcast_fusion.4), channel_id=1, source_target_pairs={{0,16},{1,17},{2,18},{3,19},{4,20},{5,21},{6,22},{7,23},{8,24},{9,... | collective-permute-start | bytes 98312 | tf_op jit(solution)/shard_map/ppermute | solution.py:23
  57.6 4.0 %shard_map.86.rest_0_ = bf16[4096,2048]{1,0:T(8,128)(2,1)} custom-call(bf16[64,4096]{1,0:T(8,128)(2,1)S(1)} %get-tuple-element.16.feats_ref.rows_ref, bf16[64,2048]{1,0:T(8,128)(2,1)S(1)} %constant_dynamic-update-slice_fusion.refs_0_.grad_ref), custom_call_target="tpu_custom_call" | custom-call | flops 536870912 | bytes 9175040 | tf_op jit(solution)/shard_map/pallas_call | solution.py:254
  61.7 4.0 %shard_map.85 = bf16[4096,2048]{1,0:T(8,128)(2,1)} custom-call(bf16[64,4096]{1,0:T(8,128)(2,1)S(1)} %get-tuple-element.16.feats_ref.rows_ref, bf16[64,2048]{1,0:T(8,128)(2,1)S(1)} %pad_maximum_fusion.1.refs_0_.grad_ref, bf16[4096,2048]{1,0:T(8,128)(2,1)} %shard_map.84.rest_0_), custom_call_target="tpu_custom_call", output_to_operand_aliasing={{}: (2, {})} | custom-call | flops 536870912 | bytes 9175040 | tf_op jit(solution)/shard_map/pallas_call | solution.py:254
  65.8 0.7 collective-permute-start.16
  66.5 4.0 %shard_map.87 = bf16[4096,2048]{1,0:T(8,128)(2,1)} custom-call(bf16[64,4096]{1,0:T(8,128)(2,1)S(1)} %get-tuple-element.16.feats_ref.rows_ref, bf16[64,2048]{1,0:T(8,128)(2,1)S(1)} %constant_dynamic-update-slice_fusion.refs_0_.grad_ref, bf16[4096,2048]{1,0:T(8,128)(2,1)} %shard_map.86.rest_0_), custom_call_target="tpu_custom_call", output_to_operand_aliasing={{}: (2, {})} | custom-call | flops 536870912 | bytes 9175040 | tf_op jit(solution)/shard_map/pallas_call | solution.py:254
  70.5 0.6 maximum_bitcast_fusion
  (46 shorter events, 3.7 us)
Async XLA Ops:
  0.6 23.7 %copy-start = (bf16[1,16,2048]{2,1,0:T(8,128)(2,1)S(1)}, bf16[1,16,2048]{2,1,0:T(8,128)(2,1)}, u32[]{:S(2)}) copy-start(bf16[1,16,2048]{2,1,0:T(8,128)(2,1)} %param.7) | copy-start | bytes 196612
  0.6 5.2 %collective-permute-start.1 = (bf16[1,2,4096]{2,1,0:T(2,128)(2,1)}, bf16[1,2,4096]{2,1,0:T(2,128)(2,1)S(1)}, u32[]{:S(2)}, u32[]{:S(2)}) collective-permute-start(bf16[1,2,4096]{2,1,0:T(2,128)(2,1)} %in_ref.1), channel_id=1, source_target_pairs={{0,17},{1,16},{2,19},{3,18},{4,21},{5,20},{6,23},{7,22},{8,25},{9,... | collective-permute-start | bytes 49160 | tf_op jit(solution)/shard_map/ppermute | solution.py:23
  4.2 0.8 %copy-start.1 = (bf16[1,2,4096]{2,1,0:T(2,128)(2,1)S(1)}, bf16[1,2,4096]{2,1,0:T(2,128)(2,1)}, u32[]{:S(2)}) copy-start(bf16[1,2,4096]{2,1,0:T(2,128)(2,1)} %in_ref.1) | copy-start | bytes 49156
  5.9 3.6 %collective-permute-start.2 = (bf16[2,2,4096]{2,1,0:T(2,128)(2,1)S(1)}, bf16[2,2,4096]{2,1,0:T(2,128)(2,1)S(1)}, u32[]{:S(2)}, u32[]{:S(2)}) collective-permute-start(bf16[2,2,4096]{2,1,0:T(2,128)(2,1)S(1)} %get-tuple-element.36), channel_id=1, source_target_pairs={{0,9},{1,8},{2,11},{3,10},{4,13},{5,12},{6,15},{7,14},{8,1},{9,0},... | collective-permute-start | bytes 98312 | tf_op jit(solution)/shard_map/ppermute | solution.py:23
  9.6 4.0 %collective-permute-start.3 = (bf16[4,2,4096]{2,1,0:T(2,128)(2,1)S(1)}, bf16[4,2,4096]{2,1,0:T(2,128)(2,1)S(1)}, u32[]{:S(2)}, u32[]{:S(2)}) collective-permute-start(bf16[4,2,4096]{2,1,0:T(2,128)(2,1)S(1)} %bitcast.110), channel_id=1, source_target_pairs={{0,5},{1,4},{2,7},{3,6},{4,1},{5,0},{6,3},{7,2},{8,13},{9,12},{10,... | collective-permute-start | bytes 196616 | tf_op jit(solution)/shard_map/ppermute | solution.py:23
  13.9 5.5 %collective-permute-start.4 = (bf16[8,2,4096]{2,1,0:T(2,128)(2,1)S(1)}, bf16[8,2,4096]{2,1,0:T(2,128)(2,1)S(1)}, u32[]{:S(2)}, u32[]{:S(2)}) collective-permute-start(bf16[8,2,4096]{2,1,0:T(2,128)(2,1)S(1)} %bitcast.108), channel_id=1, source_target_pairs={{0,3},{1,2},{2,1},{3,0},{4,7},{5,6},{6,5},{7,4},{8,11},{9,10},{10,... | collective-permute-start | bytes 393224 | tf_op jit(solution)/shard_map/ppermute | solution.py:23
  19.8 1.6 %collective-permute-start.5 = (bf16[2,8,2,4096]{3,2,1,0:T(2,128)(2,1)S(1)}, bf16[2,8,2,4096]{3,2,1,0:T(2,128)(2,1)S(1)}, u32[]{:S(2)}, u32[]{:S(2)}) collective-permute-start(bf16[2,8,2,4096]{3,2,1,0:T(2,128)(2,1)S(1)} %pad_maximum_fusion.part_ref), channel_id=1, source_target_pairs={{0,1},{1,0},{2,3},{3,2},{4,5},{5,4},{6,7},{7,6},{8,9},{9,8},{10,11... | collective-permute-start | bytes 786440 | tf_op jit(solution)/shard_map/ppermute | solution.py:23
  23.9 6.7 %collective-permute-start.6 = (f32[32,2048]{1,0:T(8,128)S(1)}, f32[32,2048]{1,0:T(8,128)S(1)}, u32[]{:S(2)}, u32[]{:S(2)}) collective-permute-start(f32[32,2048]{1,0:T(8,128)S(1)} %get-tuple-element.14), channel_id=1, source_target_pairs={{0,1},{1,0},{2,3},{3,2},{4,5},{5,4},{6,7},{7,6},{8,9},{9,8},{10,11... | collective-permute-start | bytes 786440 | tf_op jit(solution)/shard_map/ppermute | solution.py:23
  24.4 11.6 %collective-permute-start = (bf16[16,2048]{1,0:T(8,128)(2,1)S(1)}, bf16[16,2048]{1,0:T(8,128)(2,1)S(1)}, u32[]{:S(2)}, u32[]{:S(2)}) collective-permute-start(bf16[16,2048]{1,0:T(8,128)(2,1)S(1)} %shard_map.75), channel_id=1, source_target_pairs={{0,3},{1,2},{2,1},{3,0},{4,7},{5,6},{6,5},{7,4},{8,11},{9,10},{10,... | collective-permute-start | bytes 196616 | tf_op jit(solution)/shard_map/ppermute | solution.py:23
  30.5 1.6 %collective-permute-start.8 = (f32[32,2048]{1,0:T(8,128)S(1)}, f32[32,2048]{1,0:T(8,128)S(1)}, u32[]{:S(2)}, u32[]{:S(2)}) collective-permute-start(f32[32,2048]{1,0:T(8,128)S(1)} %get-tuple-element.18), channel_id=1, source_target_pairs={{0,1},{1,0},{2,3},{3,2},{4,5},{5,4},{6,7},{7,6},{8,9},{9,8},{10,11... | collective-permute-start | bytes 786440 | tf_op jit(solution)/shard_map/ppermute | solution.py:23
  30.7 5.3 %collective-permute-start.7 = (bf16[32,2048]{1,0:T(8,128)(2,1)S(1)}, bf16[32,2048]{1,0:T(8,128)(2,1)S(1)}, u32[]{:S(2)}, u32[]{:S(2)}) collective-permute-start(bf16[32,2048]{1,0:T(8,128)(2,1)S(1)} %add_convert_fusion.1), channel_id=1, source_target_pairs={{0,3},{1,2},{2,1},{3,0},{4,7},{5,6},{6,5},{7,4},{8,11},{9,10},{10,... | collective-permute-start | bytes 393224 | tf_op jit(solution)/shard_map/ppermute | solution.py:23
  32.1 6.7 %collective-permute-start.9 = (bf16[32,2048]{1,0:T(8,128)(2,1)S(1)}, bf16[32,2048]{1,0:T(8,128)(2,1)S(1)}, u32[]{:S(2)}, u32[]{:S(2)}) collective-permute-start(bf16[32,2048]{1,0:T(8,128)(2,1)S(1)} %add_convert_fusion), channel_id=1, source_target_pairs={{0,3},{1,2},{2,1},{3,0},{4,7},{5,6},{6,5},{7,4},{8,11},{9,10},{10,... | collective-permute-start | bytes 393224 | tf_op jit(solution)/shard_map/ppermute | solution.py:23
  36.2 3.2 %collective-permute-start.11 = (bf16[32,2048]{1,0:T(8,128)(2,1)S(1)}, bf16[32,2048]{1,0:T(8,128)(2,1)S(1)}, u32[]{:S(2)}, u32[]{:S(2)}) collective-permute-start(bf16[32,2048]{1,0:T(8,128)(2,1)S(1)} %get-tuple-element.21), channel_id=1, source_target_pairs={{0,1},{1,0},{2,3},{3,2},{4,5},{5,4},{6,7},{7,6},{8,9},{9,8},{10,11... | collective-permute-start | bytes 393224 | tf_op jit(solution)/shard_map/ppermute | solution.py:23
  38.9 1.9 %collective-permute-start.10 = (bf16[32,2048]{1,0:T(8,128)(2,1)S(1)}, bf16[32,2048]{1,0:T(8,128)(2,1)S(1)}, u32[]{:S(2)}, u32[]{:S(2)}) collective-permute-start(bf16[32,2048]{1,0:T(8,128)(2,1)S(1)} %get-tuple-element.24), channel_id=1, source_target_pairs={{0,1},{1,0},{2,3},{3,2},{4,5},{5,4},{6,7},{7,6},{8,9},{9,8},{10,11... | collective-permute-start | bytes 393224 | tf_op jit(solution)/shard_map/ppermute | solution.py:23
  42.4 5.6 %collective-permute-start.12 = (f32[2,2,4,2,1024]{4,3,2,1,0:T(2,128)S(1)}, f32[2,2,4,2,1024]{4,3,2,1,0:T(2,128)S(1)}, u32[]{:S(2)}, u32[]{:S(2)}) collective-permute-start(f32[2,2,4,2,1024]{4,3,2,1,0:T(2,128)S(1)} %slice_bitcast_fusion), channel_id=1, source_target_pairs={{0,4},{1,5},{2,6},{3,7},{4,0},{5,1},{6,2},{7,3},{8,12},{9,13},{10,... | collective-permute-start | bytes 393224 | tf_op jit(solution)/shard_map/ppermute | solution.py:23
  48.1 6.4 %collective-permute-start.13 = (f32[2,2,2,2,1024]{4,3,2,1,0:T(2,128)S(1)}, f32[2,2,2,2,1024]{4,3,2,1,0:T(2,128)S(1)}, u32[]{:S(2)}, u32[]{:S(2)}) collective-permute-start(f32[2,2,2,2,1024]{4,3,2,1,0:T(2,128)S(1)} %slice_bitcast_fusion.2), channel_id=1, source_target_pairs={{0,8},{1,9},{2,10},{3,11},{4,12},{5,13},{6,14},{7,15},{8,0},{9,1},... | collective-permute-start | bytes 196616 | tf_op jit(solution)/shard_map/ppermute | solution.py:23
  54.5 7.0 %collective-permute-start.14 = (f32[2,2,1,2,1024]{4,3,1,0,2:T(2,128)S(1)}, f32[2,2,1,2,1024]{4,3,1,0,2:T(2,128)S(1)}, u32[]{:S(2)}, u32[]{:S(2)}) collective-permute-start(f32[2,2,1,2,1024]{4,3,1,0,2:T(2,128)S(1)} %slice_bitcast_fusion.4), channel_id=1, source_target_pairs={{0,16},{1,17},{2,18},{3,19},{4,20},{5,21},{6,22},{7,23},{8,24},{9,... | collective-permute-start | bytes 98312 | tf_op jit(solution)/shard_map/ppermute | solution.py:23
  61.6 4.1 %collective-permute-start.15 = (bf16[2,2,1024]{2,1,0:T(2,128)(2,1)S(1)}, bf16[2,2,1024]{2,1,0:T(2,128)(2,1)S(1)}, u32[]{:S(2)}, u32[]{:S(2)}) collective-permute-start(bf16[2,2,1024]{2,1,0:T(2,128)(2,1)S(1)} %get-tuple-element.38), channel_id=1, source_target_pairs={{0,3},{1,2},{2,1},{3,0},{4,7},{5,6},{6,5},{7,4},{8,11},{9,10},{10,... | collective-permute-start | bytes 24584 | tf_op jit(solution)/shard_map/ppermute | solution.py:23
  65.8 4.7 %collective-permute-start.16 = (bf16[2,2,1024]{2,1,0:T(2,128)(2,1)S(1)}, bf16[2,2,1024]{2,1,0:T(2,128)(2,1)S(1)}, u32[]{:S(2)}, u32[]{:S(2)}) collective-permute-start(bf16[2,2,1024]{2,1,0:T(2,128)(2,1)S(1)} %fusion.10), channel_id=1, source_target_pairs={{0,1},{1,0},{2,3},{3,2},{4,5},{5,4},{6,7},{7,6},{8,9},{9,8},{10,11... | collective-permute-start | bytes 24584 | tf_op jit(solution)/shard_map/ppermute | solution.py:23

commit v8 on v7

--- a/solution.py
+++ b/solution.py
@@ -323,9 +323,10 @@
         total = total.reshape(2, 2, -1, 2, rt, depth)
         total = total[:, :, :, 0] + swap(total[:, :, :, 1], bit, 0)
     total = total[:, :, 0]
-    total = jnp.stack([total[:, 0], swap(total[:, 1], 0, 3)], axis=1)
-    total = jnp.stack([total[0], swap(total[1], 0, 1)])
-    total = [total[0, 0], total[1, 0], total[1, 1], total[0, 1]]
+    third = swap(total[0, 1], 0, 3)
+    second = swap(total[1, 1], 0, 2)
+    first = swap(total[1, 0], 0, 1)
+    total = [total[0, 0], first, second, third]
     for bit in (1, 2):
         total = [jnp.where(r & bit != 0, total[m ^ bit], total[m]) for m in range(n_dp)]
     grad_tokens = jnp.concatenate([v.astype(BF16) for v in total], axis=1)[None]

time: 71.4 us -> 77.5 us (1.085)
  local copies, waits for them, and re-layouts: 1.12 us -> 6.04 us
  starting transfers between devices: 21.7 us -> 23.7 us
  waiting for transfers between devices: 19.6 us -> 17.8 us
  other arithmetic: 1.79 us -> 2.73 us
    unnamed x6 -> x15, local copies, waits for them, and re-layouts: 0.78 us -> 5.69 us
    ppermute x17 -> x18, starting transfers between devices: 21.7 us -> 23.7 us  [swap(): return lax.ppermute(value, ('tp', 'dp'), pairs)]
    ppermute x17 -> x18, waiting for transfers between devices: 19.6 us -> 17.8 us  [swap(): return lax.ppermute(value, ('tp', 'dp'), pairs)]
    convert_element_type x2, other arithmetic: 0.06 us -> 1.01 us  [partial(): return (keep + other).astype(BF16)]
  transfers between devices with their start and end apart: 17 -> 18, of which waited for: 9 -> 9; matrix products, arithmetic and copies ran while one was open for 0% -> 2% of each run, Pallas kernels for 31% -> 29%
where the time goes in v8:
time: 77.5 us; the launch traced here: 77.2 us
  Pallas kernels  26 us (34%)
  starting transfers between devices  23.7 us (31%)
  waiting for transfers between devices  17.8 us (23%)
  local copies, waits for them, and re-layouts  6.04 us (8%)
  other arithmetic  2.73 us (4%)
  between operations  0.97 us (1%)
    ppermute x18, starting transfers between devices, swap(): return lax.ppermute(value, ('tp', 'dp'), pairs)  23.7 us
    ppermute x18, waiting for transfers between devices, swap(): return lax.ppermute(value, ('tp', 'dp'), pairs)  17.8 us
    pallas_call x4, Pallas kernels, outer(): pl.pallas_call(kernel, in_specs=[VMEM, VMEM] + [HBM] * (len(args) - 2), o...  15.8 us
    unnamed x15, local copies, waits for them, and re-layouts  5.69 us
    pallas_call x2, Pallas kernels, load(): pl.pallas_call(functools.partial(load_kernel, begin=part * depth), in_spe...  3.12 us
    pallas_call x2, Pallas kernels, back(): pl.pallas_call(functools.partial(back_kernel, parts=len(weights)), in_spe...  2.77 us
    pallas_call x1, Pallas kernels, gather_ahead(): pl.pallas_call(kernel, in_specs=[VMEM] * (len(args) - 1) + [HBM], out_spe...  2.51 us
  transfers between devices with their start and end apart: 18, of which 9 were waited for; matrix products, arithmetic and copies ran while one was open for 2% of the time, Pallas kernels for 29%

profile of v8, /device:TPU:0, one launch (start us, length us, event | category | flops | bytes accessed | tf_op | source)
XLA Modules:
  0.0 77.2 jit_solution(17396754662256617479)
XLA Ops:
  0.6 3.6 %collective-permute-start.1 = (bf16[1,2,4096]{2,1,0:T(2,128)(2,1)}, bf16[1,2,4096]{2,1,0:T(2,128)(2,1)S(1)}, u32[]{:S(2)}, u32[]{:S(2)}) collective-permute-start(bf16[1,2,4096]{2,1,0:T(2,128)(2,1)} %in_ref.1), channel_id=1, source_target_pairs={{0,17},{1,16},{2,19},{3,18},{4,21},{5,20},{6,23},{7,22},{8,25},{9,... | collective-permute-start | bytes 49160 | tf_op jit(solution)/shard_map/ppermute | solution.py:23
  5.0 0.9 %collective-permute-done.1 = bf16[1,2,4096]{2,1,0:T(2,128)(2,1)S(1)} collective-permute-done((bf16[1,2,4096]{2,1,0:T(2,128)(2,1)}, bf16[1,2,4096]{2,1,0:T(2,128)(2,1)S(1)}, u32[]{:S(2)}, u32[]{:S(2)}) %collective-permute-start.1) | collective-permute-done | bytes 16416 | tf_op jit(solution)/shard_map/ppermute | solution.py:23
  5.9 2.0 %collective-permute-start.2 = (bf16[2,2,4096]{2,1,0:T(2,128)(2,1)S(1)}, bf16[2,2,4096]{2,1,0:T(2,128)(2,1)S(1)}, u32[]{:S(2)}, u32[]{:S(2)}) collective-permute-start(bf16[2,2,4096]{2,1,0:T(2,128)(2,1)S(1)} %get-tuple-element.32), channel_id=1, source_target_pairs={{0,9},{1,8},{2,11},{3,10},{4,13},{5,12},{6,15},{7,14},{8,1},{9,0},... | collective-permute-start | bytes 98312 | tf_op jit(solution)/shard_map/ppermute | solution.py:23
  7.9 1.6 %collective-permute-done.2 = bf16[2,2,4096]{2,1,0:T(2,128)(2,1)S(1)} collective-permute-done((bf16[2,2,4096]{2,1,0:T(2,128)(2,1)S(1)}, bf16[2,2,4096]{2,1,0:T(2,128)(2,1)S(1)}, u32[]{:S(2)}, u32[]{:S(2)}) %collective-permute-start.2) | collective-permute-done | bytes 32800 | tf_op jit(solution)/shard_map/ppermute | solution.py:23
  9.6 1.8 %collective-permute-start.3 = (bf16[4,2,4096]{2,1,0:T(2,128)(2,1)S(1)}, bf16[4,2,4096]{2,1,0:T(2,128)(2,1)S(1)}, u32[]{:S(2)}, u32[]{:S(2)}) collective-permute-start(bf16[4,2,4096]{2,1,0:T(2,128)(2,1)S(1)} %bitcast.78), channel_id=1, source_target_pairs={{0,5},{1,4},{2,7},{3,6},{4,1},{5,0},{6,3},{7,2},{8,13},{9,12},{10,... | collective-permute-start | bytes 196616 | tf_op jit(solution)/shard_map/ppermute | solution.py:23
  11.4 2.2 %collective-permute-done.3 = bf16[4,2,4096]{2,1,0:T(2,128)(2,1)S(1)} collective-permute-done((bf16[4,2,4096]{2,1,0:T(2,128)(2,1)S(1)}, bf16[4,2,4096]{2,1,0:T(2,128)(2,1)S(1)}, u32[]{:S(2)}, u32[]{:S(2)}) %collective-permute-start.3) | collective-permute-done | bytes 65568 | tf_op jit(solution)/shard_map/ppermute | solution.py:23
  13.9 1.9 %collective-permute-start.4 = (bf16[8,2,4096]{2,1,0:T(2,128)(2,1)S(1)}, bf16[8,2,4096]{2,1,0:T(2,128)(2,1)S(1)}, u32[]{:S(2)}, u32[]{:S(2)}) collective-permute-start(bf16[8,2,4096]{2,1,0:T(2,128)(2,1)S(1)} %bitcast.76), channel_id=1, source_target_pairs={{0,3},{1,2},{2,1},{3,0},{4,7},{5,6},{6,5},{7,4},{8,11},{9,10},{10,... | collective-permute-start | bytes 393224 | tf_op jit(solution)/shard_map/ppermute | solution.py:23
  15.9 3.6 %collective-permute-done.4 = bf16[8,2,4096]{2,1,0:T(2,128)(2,1)S(1)} collective-permute-done((bf16[8,2,4096]{2,1,0:T(2,128)(2,1)S(1)}, bf16[8,2,4096]{2,1,0:T(2,128)(2,1)S(1)}, u32[]{:S(2)}, u32[]{:S(2)}) %collective-permute-start.4) | collective-permute-done | bytes 131104 | tf_op jit(solution)/shard_map/ppermute | solution.py:23
  20.2 1.2 %collective-permute-done.5.far_ref = bf16[2,8,2,4096]{3,2,1,0:T(2,128)(2,1)S(1)} collective-permute-done((bf16[2,8,2,4096]{3,2,1,0:T(2,128)(2,1)S(1)}, bf16[2,8,2,4096]{3,2,1,0:T(2,128)(2,1)S(1)}, u32[]{:S(2)}, u32[]{:S(2)}) %collective-permute-start.5) | collective-permute-done | bytes 262176 | tf_op jit(solution)/shard_map/ppermute | solution.py:23
  21.4 2.5 %shard_map.77 = (bf16[1024,2048]{1,0:T(8,128)(2,1)S(1)}, f32[32,2048]{1,0:T(8,128)S(1)}, f32[32,2048]{1,0:T(8,128)S(1)}, bf16[64,4096]{1,0:T(8,128)(2,1)S(1)}) custom-call(bf16[2,8,2,4096]{3,2,1,0:T(2,128)(2,1)S(1)} %pad_maximum_fusion.part_ref, bf16[2,8,2,4096]{3,2,1,0:T(2,128)(2,1)S(1)} %collective-permute-done.5.far_ref, bf16[1024,2048]{1,0:T(8,128)(2,1)} %weight_ref.3), custom_call_target="tpu_custom_call" | custom-call | flops 268435456 | bytes 4194304 | tf_op jit(solution)/shard_map/pallas_call | solution.py:163
  23.9 2.0 %copy-done.3 = bf16[1024,2048]{1,0:T(8,128)(2,1)} copy-done((bf16[1024,2048]{1,0:T(8,128)(2,1)}, bf16[1024,2048]{1,0:T(8,128)(2,1)S(1)}, u32[]{:S(2)}) %copy-start.3) | copy-done | bytes 4194328
  26.4 2.1 %collective-permute-start = (bf16[16,2048]{1,0:T(8,128)(2,1)S(1)}, bf16[16,2048]{1,0:T(8,128)(2,1)S(1)}, u32[]{:S(2)}, u32[]{:S(2)}) collective-permute-start(bf16[16,2048]{1,0:T(8,128)(2,1)S(1)} %shard_map.75), channel_id=1, source_target_pairs={{0,3},{1,2},{2,1},{3,0},{4,7},{5,6},{6,5},{7,4},{8,11},{9,10},{10,... | collective-permute-start | bytes 196616 | tf_op jit(solution)/shard_map/ppermute | solution.py:23
  28.4 1.6 %shard_map.79.refs_1_.refs_2_ = bf16[512,2048]{1,0:T(8,128)(2,1)S(1)} custom-call(bf16[1024,2048]{1,0:T(8,128)(2,1)} %weight_ref.5), custom_call_target="tpu_custom_call" | custom-call | bytes 2097152 | tf_op jit(solution)/shard_map/pallas_call | solution.py:92
  30.0 1.6 %shard_map.78.refs_0_.refs_1_ = bf16[512,2048]{1,0:T(8,128)(2,1)S(1)} custom-call(bf16[1024,2048]{1,0:T(8,128)(2,1)} %weight_ref.5), custom_call_target="tpu_custom_call" | custom-call | bytes 2097152 | tf_op jit(solution)/shard_map/pallas_call | solution.py:92
  31.6 1.3 %copy-done = bf16[512,2048]{1,0:T(8,128)(2,1)} copy-done((bf16[512,2048]{1,0:T(8,128)(2,1)}, bf16[512,2048]{1,0:T(8,128)(2,1)S(1)}, u32[]{:S(2)}) %copy-start) | copy-done | bytes 2097176
  32.9 1.6 %copy-done.1 = bf16[512,2048]{1,0:T(8,128)(2,1)S(1)} copy-done((bf16[512,2048]{1,0:T(8,128)(2,1)S(1)}, bf16[512,2048]{1,0:T(8,128)(2,1)}, u32[]{:S(2)}) %copy-start.1) | copy-done | bytes 2097176
  35.5 1.0 %add_convert_fusion.1 = bf16[32,2048]{1,0:T(8,128)(2,1)S(1)} fusion(f32[32,2048]{1,0:T(8,128)S(1)} %get-tuple-element.13, f32[32,2048]{1,0:T(8,128)} %collective-permute-done.6), kind=kLoop, calls=%fused_computation.13 | loop fusion | flops 131072 | bytes 655360 | tf_op jit(solution)/shard_map/convert_element_type | solution.py:291
  37.0 1.5 %collective-permute-start.9 = (bf16[32,2048]{1,0:T(8,128)(2,1)S(1)}, bf16[32,2048]{1,0:T(8,128)(2,1)S(1)}, u32[]{:S(2)}, u32[]{:S(2)}) collective-permute-start(bf16[32,2048]{1,0:T(8,128)(2,1)S(1)} %add_convert_fusion), channel_id=1, source_target_pairs={{0,3},{1,2},{2,1},{3,0},{4,7},{5,6},{6,5},{7,4},{8,11},{9,10},{10,... | collective-permute-start | bytes 393224 | tf_op jit(solution)/shard_map/ppermute | solution.py:23
  38.5 3.4 %collective-permute-done.7 = bf16[32,2048]{1,0:T(8,128)(2,1)S(1)} collective-permute-done((bf16[32,2048]{1,0:T(8,128)(2,1)S(1)}, bf16[32,2048]{1,0:T(8,128)(2,1)S(1)}, u32[]{:S(2)}, u32[]{:S(2)}) %collective-permute-start.7) | collective-permute-done | bytes 131104 | tf_op jit(solution)/shard_map/ppermute | solution.py:23
  42.0 1.3 %collective-permute-start.11 = (bf16[32,2048]{1,0:T(8,128)(2,1)S(1)}, bf16[32,2048]{1,0:T(8,128)(2,1)S(1)}, u32[]{:S(2)}, u32[]{:S(2)}) collective-permute-start(bf16[32,2048]{1,0:T(8,128)(2,1)S(1)} %get-tuple-element.21), channel_id=1, source_target_pairs={{0,1},{1,0},{2,3},{3,2},{4,5},{5,4},{6,7},{7,6},{8,9},{9,8},{10,11... | collective-permute-start | bytes 393224 | tf_op jit(solution)/shard_map/ppermute | solution.py:23
  43.3 1.4 %collective-permute-done.9 = bf16[32,2048]{1,0:T(8,128)(2,1)S(1)} collective-permute-done((bf16[32,2048]{1,0:T(8,128)(2,1)S(1)}, bf16[32,2048]{1,0:T(8,128)(2,1)S(1)}, u32[]{:S(2)}, u32[]{:S(2)}) %collective-permute-start.9) | collective-permute-done | bytes 131104 | tf_op jit(solution)/shard_map/ppermute | solution.py:23
  45.2 1.4 %shard_map.82.refs_2_ = f32[64,1024]{1,0:T(8,128)S(1)} custom-call(bf16[64,2048]{1,0:T(8,128)(2,1)S(1)} %constant_dynamic-update-slice_fusion.refs_0_.grad_ref, bf16[512,2048]{1,0:T(8,128)(2,1)S(1)} %copy-done.2, bf16[512,2048]{1,0:T(8,128)(2,1)S(1)} %shard_map.79.refs_1_.refs_2_), custom_call_target="tpu_custom_call" | custom-call | flops 268435456 | bytes 1048576 | tf_op jit(solution)/shard_map/pallas_call | solution.py:213
  46.7 1.4 %shard_map.83 = f32[64,1024]{1,0:T(8,128)S(1)} custom-call(bf16[64,2048]{1,0:T(8,128)(2,1)S(1)} %pad_maximum_fusion.1.refs_0_.grad_ref, bf16[1024,2048]{1,0:T(8,128)(2,1)S(1)} %copy-done.4, f32[64,1024]{1,0:T(8,128)S(1)} %shard_map.82.refs_2_), custom_call_target="tpu_custom_call" | custom-call | flops 268435456 | bytes 1048576 | tf_op jit(solution)/shard_map/pallas_call | solution.py:213
  48.2 1.6 %collective-permute-start.12 = (f32[2,2,4,2,1024]{4,3,2,1,0:T(2,128)S(1)}, f32[2,2,4,2,1024]{4,3,2,1,0:T(2,128)S(1)}, u32[]{:S(2)}, u32[]{:S(2)}) collective-permute-start(f32[2,2,4,2,1024]{4,3,2,1,0:T(2,128)S(1)} %slice_bitcast_fusion), channel_id=1, source_target_pairs={{0,4},{1,5},{2,6},{3,7},{4,0},{5,1},{6,2},{7,3},{8,12},{9,13},{10,... | collective-permute-start | bytes 393224 | tf_op jit(solution)/shard_map/ppermute | solution.py:23
  50.6 3.2 %collective-permute-done.12 = f32[2,2,4,2,1024]{4,3,2,1,0:T(2,128)S(1)} collective-permute-done((f32[2,2,4,2,1024]{4,3,2,1,0:T(2,128)S(1)}, f32[2,2,4,2,1024]{4,3,2,1,0:T(2,128)S(1)}, u32[]{:S(2)}, u32[]{:S(2)}) %collective-permute-start.12) | collective-permute-done | bytes 131104 | tf_op jit(solution)/shard_map/ppermute | solution.py:23
  53.9 1.6 %collective-permute-start.13 = (f32[2,2,2,2,1024]{4,3,2,1,0:T(2,128)S(1)}, f32[2,2,2,2,1024]{4,3,2,1,0:T(2,128)S(1)}, u32[]{:S(2)}, u32[]{:S(2)}) collective-permute-start(f32[2,2,2,2,1024]{4,3,2,1,0:T(2,128)S(1)} %slice_bitcast_fusion.2), channel_id=1, source_target_pairs={{0,8},{1,9},{2,10},{3,11},{4,12},{5,13},{6,14},{7,15},{8,0},{9,1},... | collective-permute-start | bytes 196616 | tf_op jit(solution)/shard_map/ppermute | solution.py:23
  55.6 4.0 %shard_map.84.rest_0_ = bf16[4096,2048]{1,0:T(8,128)(2,1)} custom-call(bf16[64,4096]{1,0:T(8,128)(2,1)S(1)} %get-tuple-element.16.feats_ref.rows_ref, bf16[64,2048]{1,0:T(8,128)(2,1)S(1)} %pad_maximum_fusion.1.refs_0_.grad_ref), custom_call_target="tpu_custom_call" | custom-call | flops 536870912 | bytes 9175040 | tf_op jit(solution)/shard_map/pallas_call | solution.py:254
  59.5 4.0 %shard_map.86.rest_0_ = bf16[4096,2048]{1,0:T(8,128)(2,1)} custom-call(bf16[64,4096]{1,0:T(8,128)(2,1)S(1)} %get-tuple-element.16.feats_ref.rows_ref, bf16[64,2048]{1,0:T(8,128)(2,1)S(1)} %constant_dynamic-update-slice_fusion.refs_0_.grad_ref), custom_call_target="tpu_custom_call" | custom-call | flops 536870912 | bytes 9175040 | tf_op jit(solution)/shard_map/pallas_call | solution.py:254
  63.6 3.1 %collective-permute-start.14 = (f32[2,2,1,2,1024]{4,3,1,0,2:T(2,128)S(1)}, f32[2,2,1,2,1024]{4,3,1,0,2:T(2,128)S(1)}, u32[]{:S(2)}, u32[]{:S(2)}) collective-permute-start(f32[2,2,1,2,1024]{4,3,1,0,2:T(2,128)S(1)} %slice_bitcast_fusion.4), channel_id=1, source_target_pairs={{0,16},{1,17},{2,18},{3,19},{4,20},{5,21},{6,22},{7,23},{8,24},{9,... | collective-permute-start | bytes 98312 | tf_op jit(solution)/shard_map/ppermute | solution.py:23
  66.6 4.0 %shard_map.85 = bf16[4096,2048]{1,0:T(8,128)(2,1)} custom-call(bf16[64,4096]{1,0:T(8,128)(2,1)S(1)} %get-tuple-element.16.feats_ref.rows_ref, bf16[64,2048]{1,0:T(8,128)(2,1)S(1)} %pad_maximum_fusion.1.refs_0_.grad_ref, bf16[4096,2048]{1,0:T(8,128)(2,1)} %shard_map.84.rest_0_), custom_call_target="tpu_custom_call", output_to_operand_aliasing={{}: (2, {})} | custom-call | flops 536870912 | bytes 9175040 | tf_op jit(solution)/shard_map/pallas_call | solution.py:254
  71.3 1.3 %collective-permute-start.15 = (bf16[2,1024]{1,0:T(2,128)(2,1)S(1)}, bf16[2,1024]{1,0:T(2,128)(2,1)S(1)}, u32[]{:S(2)}, u32[]{:S(2)}) collective-permute-start(bf16[2,1024]{1,0:T(2,128)(2,1)S(1)} %get-tuple-element.39), channel_id=1, source_target_pairs={{0,3},{1,2},{2,1},{3,0},{4,7},{5,6},{6,5},{7,4},{8,11},{9,10},{10,... | collective-permute-start | bytes 12296 | tf_op jit(solution)/shard_map/ppermute | solution.py:23
  72.6 4.0 %shard_map.87 = bf16[4096,2048]{1,0:T(8,128)(2,1)} custom-call(bf16[64,4096]{1,0:T(8,128)(2,1)S(1)} %get-tuple-element.16.feats_ref.rows_ref, bf16[64,2048]{1,0:T(8,128)(2,1)S(1)} %constant_dynamic-update-slice_fusion.refs_0_.grad_ref, bf16[4096,2048]{1,0:T(8,128)(2,1)} %shard_map.86.rest_0_), custom_call_target="tpu_custom_call", output_to_operand_aliasing={{}: (2, {})} | custom-call | flops 536870912 | bytes 9175040 | tf_op jit(solution)/shard_map/pallas_call | solution.py:254
  (57 shorter events, 7.0 us)
Async XLA Ops:
  0.6 25.6 %copy-start.5 = (bf16[1,16,2048]{2,1,0:T(8,128)(2,1)S(1)}, bf16[1,16,2048]{2,1,0:T(8,128)(2,1)}, u32[]{:S(2)}) copy-start(bf16[1,16,2048]{2,1,0:T(8,128)(2,1)} %param.7) | copy-start | bytes 196612
  0.6 5.2 %collective-permute-start.1 = (bf16[1,2,4096]{2,1,0:T(2,128)(2,1)}, bf16[1,2,4096]{2,1,0:T(2,128)(2,1)S(1)}, u32[]{:S(2)}, u32[]{:S(2)}) collective-permute-start(bf16[1,2,4096]{2,1,0:T(2,128)(2,1)} %in_ref.1), channel_id=1, source_target_pairs={{0,17},{1,16},{2,19},{3,18},{4,21},{5,20},{6,23},{7,22},{8,25},{9,... | collective-permute-start | bytes 49160 | tf_op jit(solution)/shard_map/ppermute | solution.py:23
  4.2 0.8 copy-start.6
  5.9 3.6 %collective-permute-start.2 = (bf16[2,2,4096]{2,1,0:T(2,128)(2,1)S(1)}, bf16[2,2,4096]{2,1,0:T(2,128)(2,1)S(1)}, u32[]{:S(2)}, u32[]{:S(2)}) collective-permute-start(bf16[2,2,4096]{2,1,0:T(2,128)(2,1)S(1)} %get-tuple-element.32), channel_id=1, source_target_pairs={{0,9},{1,8},{2,11},{3,10},{4,13},{5,12},{6,15},{7,14},{8,1},{9,0},... | collective-permute-start | bytes 98312 | tf_op jit(solution)/shard_map/ppermute | solution.py:23
  9.6 4.0 %collective-permute-start.3 = (bf16[4,2,4096]{2,1,0:T(2,128)(2,1)S(1)}, bf16[4,2,4096]{2,1,0:T(2,128)(2,1)S(1)}, u32[]{:S(2)}, u32[]{:S(2)}) collective-permute-start(bf16[4,2,4096]{2,1,0:T(2,128)(2,1)S(1)} %bitcast.78), channel_id=1, source_target_pairs={{0,5},{1,4},{2,7},{3,6},{4,1},{5,0},{6,3},{7,2},{8,13},{9,12},{10,... | collective-permute-start | bytes 196616 | tf_op jit(solution)/shard_map/ppermute | solution.py:23
  13.9 5.5 %collective-permute-start.4 = (bf16[8,2,4096]{2,1,0:T(2,128)(2,1)S(1)}, bf16[8,2,4096]{2,1,0:T(2,128)(2,1)S(1)}, u32[]{:S(2)}, u32[]{:S(2)}) collective-permute-start(bf16[8,2,4096]{2,1,0:T(2,128)(2,1)S(1)} %bitcast.76), channel_id=1, source_target_pairs={{0,3},{1,2},{2,1},{3,0},{4,7},{5,6},{6,5},{7,4},{8,11},{9,10},{10,... | collective-permute-start | bytes 393224 | tf_op jit(solution)/shard_map/ppermute | solution.py:23
  19.8 1.6 %collective-permute-start.5 = (bf16[2,8,2,4096]{3,2,1,0:T(2,128)(2,1)S(1)}, bf16[2,8,2,4096]{3,2,1,0:T(2,128)(2,1)S(1)}, u32[]{:S(2)}, u32[]{:S(2)}) collective-permute-start(bf16[2,8,2,4096]{3,2,1,0:T(2,128)(2,1)S(1)} %pad_maximum_fusion.part_ref), channel_id=1, source_target_pairs={{0,1},{1,0},{2,3},{3,2},{4,5},{5,4},{6,7},{7,6},{8,9},{9,8},{10,11... | collective-permute-start | bytes 786440 | tf_op jit(solution)/shard_map/ppermute | solution.py:23
  23.9 2.0 %copy-start.3 = (bf16[1024,2048]{1,0:T(8,128)(2,1)}, bf16[1024,2048]{1,0:T(8,128)(2,1)S(1)}, u32[]{:S(2)}) copy-start(bf16[1024,2048]{1,0:T(8,128)(2,1)S(1)} %get-tuple-element.20.refs_1_) | copy-start | bytes 12582916
  25.9 9.6 %collective-permute-start.6 = (f32[32,2048]{1,0:T(8,128)S(1)}, f32[32,2048]{1,0:T(8,128)}, u32[]{:S(2)}, u32[]{:S(2)}) collective-permute-start(f32[32,2048]{1,0:T(8,128)S(1)} %get-tuple-element.14), channel_id=1, source_target_pairs={{0,1},{1,0},{2,3},{3,2},{4,5},{5,4},{6,7},{7,6},{8,9},{9,8},{10,11... | collective-permute-start | bytes 786440 | tf_op jit(solution)/shard_map/ppermute | solution.py:23
  26.4 15.5 %collective-permute-start = (bf16[16,2048]{1,0:T(8,128)(2,1)S(1)}, bf16[16,2048]{1,0:T(8,128)(2,1)S(1)}, u32[]{:S(2)}, u32[]{:S(2)}) collective-permute-start(bf16[16,2048]{1,0:T(8,128)(2,1)S(1)} %shard_map.75), channel_id=1, source_target_pairs={{0,3},{1,2},{2,1},{3,0},{4,7},{5,6},{6,5},{7,4},{8,11},{9,10},{10,... | collective-permute-start | bytes 196616 | tf_op jit(solution)/shard_map/ppermute | solution.py:23
  31.6 1.3 %copy-start = (bf16[512,2048]{1,0:T(8,128)(2,1)}, bf16[512,2048]{1,0:T(8,128)(2,1)S(1)}, u32[]{:S(2)}) copy-start(bf16[512,2048]{1,0:T(8,128)(2,1)S(1)} %shard_map.78.refs_0_.refs_1_) | copy-start | bytes 6291460
  32.9 1.6 %copy-start.1 = (bf16[512,2048]{1,0:T(8,128)(2,1)S(1)}, bf16[512,2048]{1,0:T(8,128)(2,1)}, u32[]{:S(2)}) copy-start(bf16[512,2048]{1,0:T(8,128)(2,1)} %copy-done) | copy-start | bytes 6291460
  34.5 10.7 %copy-start.2 = (bf16[512,2048]{1,0:T(8,128)(2,1)S(1)}, bf16[512,2048]{1,0:T(8,128)(2,1)}, u32[]{:S(2)}) copy-start(bf16[512,2048]{1,0:T(8,128)(2,1)} %copy-done) | copy-start | bytes 6291460
  35.3 1.6 %collective-permute-start.8 = (f32[32,2048]{1,0:T(8,128)S(1)}, f32[32,2048]{1,0:T(8,128)S(1)}, u32[]{:S(2)}, u32[]{:S(2)}) collective-permute-start(f32[32,2048]{1,0:T(8,128)S(1)} %get-tuple-element.18), channel_id=1, source_target_pairs={{0,1},{1,0},{2,3},{3,2},{4,5},{5,4},{6,7},{7,6},{8,9},{9,8},{10,11... | collective-permute-start | bytes 786440 | tf_op jit(solution)/shard_map/ppermute | solution.py:23
  36.5 5.3 %collective-permute-start.7 = (bf16[32,2048]{1,0:T(8,128)(2,1)S(1)}, bf16[32,2048]{1,0:T(8,128)(2,1)S(1)}, u32[]{:S(2)}, u32[]{:S(2)}) collective-permute-start(bf16[32,2048]{1,0:T(8,128)(2,1)S(1)} %add_convert_fusion.1), channel_id=1, source_target_pairs={{0,3},{1,2},{2,1},{3,0},{4,7},{5,6},{6,5},{7,4},{8,11},{9,10},{10,... | collective-permute-start | bytes 393224 | tf_op jit(solution)/shard_map/ppermute | solution.py:23
  37.0 9.7 %copy-start.4 = (bf16[1024,2048]{1,0:T(8,128)(2,1)S(1)}, bf16[1024,2048]{1,0:T(8,128)(2,1)}, u32[]{:S(2)}) copy-start(bf16[1024,2048]{1,0:T(8,128)(2,1)} %copy-done.3) | copy-start | bytes 12582916
  37.0 7.7 %collective-permute-start.9 = (bf16[32,2048]{1,0:T(8,128)(2,1)S(1)}, bf16[32,2048]{1,0:T(8,128)(2,1)S(1)}, u32[]{:S(2)}, u32[]{:S(2)}) collective-permute-start(bf16[32,2048]{1,0:T(8,128)(2,1)S(1)} %add_convert_fusion), channel_id=1, source_target_pairs={{0,3},{1,2},{2,1},{3,0},{4,7},{5,6},{6,5},{7,4},{8,11},{9,10},{10,... | collective-permute-start | bytes 393224 | tf_op jit(solution)/shard_map/ppermute | solution.py:23
  42.0 3.2 %collective-permute-start.11 = (bf16[32,2048]{1,0:T(8,128)(2,1)S(1)}, bf16[32,2048]{1,0:T(8,128)(2,1)S(1)}, u32[]{:S(2)}, u32[]{:S(2)}) collective-permute-start(bf16[32,2048]{1,0:T(8,128)(2,1)S(1)} %get-tuple-element.21), channel_id=1, source_target_pairs={{0,1},{1,0},{2,3},{3,2},{4,5},{5,4},{6,7},{7,6},{8,9},{9,8},{10,11... | collective-permute-start | bytes 393224 | tf_op jit(solution)/shard_map/ppermute | solution.py:23
  44.7 1.9 %collective-permute-start.10 = (bf16[32,2048]{1,0:T(8,128)(2,1)S(1)}, bf16[32,2048]{1,0:T(8,128)(2,1)S(1)}, u32[]{:S(2)}, u32[]{:S(2)}) collective-permute-start(bf16[32,2048]{1,0:T(8,128)(2,1)S(1)} %get-tuple-element.24), channel_id=1, source_target_pairs={{0,1},{1,0},{2,3},{3,2},{4,5},{5,4},{6,7},{7,6},{8,9},{9,8},{10,11... | collective-permute-start | bytes 393224 | tf_op jit(solution)/shard_map/ppermute | solution.py:23
  48.2 5.6 %collective-permute-start.12 = (f32[2,2,4,2,1024]{4,3,2,1,0:T(2,128)S(1)}, f32[2,2,4,2,1024]{4,3,2,1,0:T(2,128)S(1)}, u32[]{:S(2)}, u32[]{:S(2)}) collective-permute-start(f32[2,2,4,2,1024]{4,3,2,1,0:T(2,128)S(1)} %slice_bitcast_fusion), channel_id=1, source_target_pairs={{0,4},{1,5},{2,6},{3,7},{4,0},{5,1},{6,2},{7,3},{8,12},{9,13},{10,... | collective-permute-start | bytes 393224 | tf_op jit(solution)/shard_map/ppermute | solution.py:23
  53.9 9.6 %collective-permute-start.13 = (f32[2,2,2,2,1024]{4,3,2,1,0:T(2,128)S(1)}, f32[2,2,2,2,1024]{4,3,2,1,0:T(2,128)S(1)}, u32[]{:S(2)}, u32[]{:S(2)}) collective-permute-start(f32[2,2,2,2,1024]{4,3,2,1,0:T(2,128)S(1)} %slice_bitcast_fusion.2), channel_id=1, source_target_pairs={{0,8},{1,9},{2,10},{3,11},{4,12},{5,13},{6,14},{7,15},{8,0},{9,1},... | collective-permute-start | bytes 196616 | tf_op jit(solution)/shard_map/ppermute | solution.py:23
  63.6 7.0 %collective-permute-start.14 = (f32[2,2,1,2,1024]{4,3,1,0,2:T(2,128)S(1)}, f32[2,2,1,2,1024]{4,3,1,0,2:T(2,128)S(1)}, u32[]{:S(2)}, u32[]{:S(2)}) collective-permute-start(f32[2,2,1,2,1024]{4,3,1,0,2:T(2,128)S(1)} %slice_bitcast_fusion.4), channel_id=1, source_target_pairs={{0,16},{1,17},{2,18},{3,19},{4,20},{5,21},{6,22},{7,23},{8,24},{9,... | collective-permute-start | bytes 98312 | tf_op jit(solution)/shard_map/ppermute | solution.py:23
  70.7 5.9 %collective-permute-start.17 = (bf16[2,1024]{1,0:T(2,128)(2,1)S(1)}, bf16[2,1024]{1,0:T(2,128)(2,1)S(1)}, u32[]{:S(2)}, u32[]{:S(2)}) collective-permute-start(bf16[2,1024]{1,0:T(2,128)(2,1)S(1)} %get-tuple-element.37), channel_id=1, source_target_pairs={{0,1},{1,0},{2,3},{3,2},{4,5},{5,4},{6,7},{7,6},{8,9},{9,8},{10,11... | collective-permute-start | bytes 12296 | tf_op jit(solution)/shard_map/ppermute | solution.py:23
  70.7 5.8 %collective-permute-start.16 = (bf16[2,1024]{1,0:T(2,128)(2,1)S(1)}, bf16[2,1024]{1,0:T(2,128)(2,1)S(1)}, u32[]{:S(2)}, u32[]{:S(2)}) collective-permute-start(bf16[2,1024]{1,0:T(2,128)(2,1)S(1)} %get-tuple-element.38), channel_id=1, source_target_pairs={{0,2},{1,3},{2,0},{3,1},{4,6},{5,7},{6,4},{7,5},{8,10},{9,11},{10,... | collective-permute-start | bytes 12296 | tf_op jit(solution)/shard_map/ppermute | solution.py:23
  71.3 5.2 %collective-permute-start.15 = (bf16[2,1024]{1,0:T(2,128)(2,1)S(1)}, bf16[2,1024]{1,0:T(2,128)(2,1)S(1)}, u32[]{:S(2)}, u32[]{:S(2)}) collective-permute-start(bf16[2,1024]{1,0:T(2,128)(2,1)S(1)} %get-tuple-element.39), channel_id=1, source_target_pairs={{0,3},{1,2},{2,1},{3,0},{4,7},{5,6},{6,5},{7,4},{8,11},{9,10},{10,... | collective-permute-start | bytes 12296 | tf_op jit(solution)/shard_map/ppermute | solution.py:23

commit v9 on v8

--- a/solution.py
+++ b/solution.py
@@ -300,9 +300,8 @@
     gate_pre = summed(half_gate)
     up_pre = summed(half_up)
 
-    cot = reorder(cotangent[0], rt)
-    far = swap(cot, 0, 3)
-    cot = jnp.concatenate([cot, far])
+    cot = swap(cotangent[0], 0, 3)
+    cot = reorder(jnp.concatenate([cotangent[0], cot]), rt)
 
     grad_hidden = cot.astype(F32)
     act, slope = swish_parts(gate_pre)

time: 77.5 us -> 75.7 us (0.977)
  waiting for transfers between devices: 17.8 us -> 16.6 us
  other arithmetic: 2.73 us -> 1.79 us
    ppermute x18, waiting for transfers between devices: 17.8 us -> 16.6 us  [swap(): return lax.ppermute(value, ('tp', 'dp'), pairs)]
    convert_element_type x2, other arithmetic: 1.01 us -> 0.06 us  [partial(): return (keep + other).astype(BF16)]
  transfers between devices with their start and end apart: 18 -> 18, of which waited for: 9 -> 7; matrix products, arithmetic and copies ran while one was open for 2% -> 0% of each run, Pallas kernels for 29% -> 33%
where the time goes in v9:
time: 75.7 us; the launch traced here: 75.4 us
  Pallas kernels  26 us (34%)
  starting transfers between devices  24 us (32%)
  waiting for transfers between devices  16.6 us (22%)
  local copies, waits for them, and re-layouts  6.04 us (8%)
  other arithmetic  1.79 us (2%)
  between operations  0.98 us (1%)
    ppermute x18, starting transfers between devices, swap(): return lax.ppermute(value, ('tp', 'dp'), pairs)  24 us
    ppermute x18, waiting for transfers between devices, swap(): return lax.ppermute(value, ('tp', 'dp'), pairs)  16.6 us
    pallas_call x4, Pallas kernels, outer(): pl.pallas_call(kernel, in_specs=[VMEM, VMEM] + [HBM] * (len(args) - 2), o...  15.8 us
    unnamed x15, local copies, waits for them, and re-layouts  5.68 us
    pallas_call x2, Pallas kernels, load(): pl.pallas_call(functools.partial(load_kernel, begin=part * depth), in_spe...  3.15 us
    pallas_call x2, Pallas kernels, back(): pl.pallas_call(functools.partial(back_kernel, parts=len(weights)), in_spe...  2.77 us
    pallas_call x1, Pallas kernels, gather_ahead(): pl.pallas_call(kernel, in_specs=[VMEM] * (len(args) - 1) + [HBM], out_spe...  2.51 us
  transfers between devices with their start and end apart: 18, of which 7 were waited for; matrix products, arithmetic and copies ran while one was open for 0% of the time, Pallas kernels for 33%

profile of v9, /device:TPU:0, one launch (start us, length us, event | category | flops | bytes accessed | tf_op | source)
XLA Modules:
  0.0 75.4 jit_solution(8950335731160489565)
XLA Ops:
  0.6 3.6 %collective-permute-start.1 = (bf16[1,2,4096]{2,1,0:T(2,128)(2,1)}, bf16[1,2,4096]{2,1,0:T(2,128)(2,1)S(1)}, u32[]{:S(2)}, u32[]{:S(2)}) collective-permute-start(bf16[1,2,4096]{2,1,0:T(2,128)(2,1)} %in_ref.1), channel_id=1, source_target_pairs={{0,17},{1,16},{2,19},{3,18},{4,21},{5,20},{6,23},{7,22},{8,25},{9,... | collective-permute-start | bytes 49160 | tf_op jit(solution)/shard_map/ppermute | solution.py:23
  5.0 0.9 %collective-permute-done.1 = bf16[1,2,4096]{2,1,0:T(2,128)(2,1)S(1)} collective-permute-done((bf16[1,2,4096]{2,1,0:T(2,128)(2,1)}, bf16[1,2,4096]{2,1,0:T(2,128)(2,1)S(1)}, u32[]{:S(2)}, u32[]{:S(2)}) %collective-permute-start.1) | collective-permute-done | bytes 16416 | tf_op jit(solution)/shard_map/ppermute | solution.py:23
  5.9 2.0 %collective-permute-start.2 = (bf16[2,2,4096]{2,1,0:T(2,128)(2,1)S(1)}, bf16[2,2,4096]{2,1,0:T(2,128)(2,1)S(1)}, u32[]{:S(2)}, u32[]{:S(2)}) collective-permute-start(bf16[2,2,4096]{2,1,0:T(2,128)(2,1)S(1)} %get-tuple-element.32), channel_id=1, source_target_pairs={{0,9},{1,8},{2,11},{3,10},{4,13},{5,12},{6,15},{7,14},{8,1},{9,0},... | collective-permute-start | bytes 98312 | tf_op jit(solution)/shard_map/ppermute | solution.py:23
  7.9 1.6 %collective-permute-done.2 = bf16[2,2,4096]{2,1,0:T(2,128)(2,1)S(1)} collective-permute-done((bf16[2,2,4096]{2,1,0:T(2,128)(2,1)S(1)}, bf16[2,2,4096]{2,1,0:T(2,128)(2,1)S(1)}, u32[]{:S(2)}, u32[]{:S(2)}) %collective-permute-start.2) | collective-permute-done | bytes 32800 | tf_op jit(solution)/shard_map/ppermute | solution.py:23
  9.6 1.8 %collective-permute-start.3 = (bf16[4,2,4096]{2,1,0:T(2,128)(2,1)S(1)}, bf16[4,2,4096]{2,1,0:T(2,128)(2,1)S(1)}, u32[]{:S(2)}, u32[]{:S(2)}) collective-permute-start(bf16[4,2,4096]{2,1,0:T(2,128)(2,1)S(1)} %bitcast.77), channel_id=1, source_target_pairs={{0,5},{1,4},{2,7},{3,6},{4,1},{5,0},{6,3},{7,2},{8,13},{9,12},{10,... | collective-permute-start | bytes 196616 | tf_op jit(solution)/shard_map/ppermute | solution.py:23
  11.4 2.2 %collective-permute-done.3 = bf16[4,2,4096]{2,1,0:T(2,128)(2,1)S(1)} collective-permute-done((bf16[4,2,4096]{2,1,0:T(2,128)(2,1)S(1)}, bf16[4,2,4096]{2,1,0:T(2,128)(2,1)S(1)}, u32[]{:S(2)}, u32[]{:S(2)}) %collective-permute-start.3) | collective-permute-done | bytes 65568 | tf_op jit(solution)/shard_map/ppermute | solution.py:23
  13.9 1.9 %collective-permute-start.4 = (bf16[8,2,4096]{2,1,0:T(2,128)(2,1)S(1)}, bf16[8,2,4096]{2,1,0:T(2,128)(2,1)S(1)}, u32[]{:S(2)}, u32[]{:S(2)}) collective-permute-start(bf16[8,2,4096]{2,1,0:T(2,128)(2,1)S(1)} %bitcast.75), channel_id=1, source_target_pairs={{0,3},{1,2},{2,1},{3,0},{4,7},{5,6},{6,5},{7,4},{8,11},{9,10},{10,... | collective-permute-start | bytes 393224 | tf_op jit(solution)/shard_map/ppermute | solution.py:23
  15.8 3.6 %collective-permute-done.4 = bf16[8,2,4096]{2,1,0:T(2,128)(2,1)S(1)} collective-permute-done((bf16[8,2,4096]{2,1,0:T(2,128)(2,1)S(1)}, bf16[8,2,4096]{2,1,0:T(2,128)(2,1)S(1)}, u32[]{:S(2)}, u32[]{:S(2)}) %collective-permute-start.4) | collective-permute-done | bytes 131104 | tf_op jit(solution)/shard_map/ppermute | solution.py:23
  20.2 2.0 %collective-permute-start = (bf16[16,2048]{1,0:T(8,128)(2,1)}, bf16[16,2048]{1,0:T(8,128)(2,1)S(1)}, u32[]{:S(2)}, u32[]{:S(2)}) collective-permute-start(bf16[16,2048]{1,0:T(8,128)(2,1)} %bitcast.81), channel_id=1, source_target_pairs={{0,3},{1,2},{2,1},{3,0},{4,7},{5,6},{6,5},{7,4},{8,11},{9,10},{10,... | collective-permute-start | bytes 196616 | tf_op jit(solution)/shard_map/ppermute | solution.py:23
  22.2 2.5 %shard_map.77 = (bf16[1024,2048]{1,0:T(8,128)(2,1)S(1)}, f32[32,2048]{1,0:T(8,128)S(1)}, f32[32,2048]{1,0:T(8,128)S(1)}, bf16[64,4096]{1,0:T(8,128)(2,1)S(1)}) custom-call(bf16[2,8,2,4096]{3,2,1,0:T(2,128)(2,1)S(1)} %pad_maximum_fusion.part_ref, bf16[2,8,2,4096]{3,2,1,0:T(2,128)(2,1)S(1)} %collective-permute-done.5.far_ref, bf16[1024,2048]{1,0:T(8,128)(2,1)} %weight_ref.3), custom_call_target="tpu_custom_call" | custom-call | flops 268435456 | bytes 4194304 | tf_op jit(solution)/shard_map/pallas_call | solution.py:163
  24.7 2.0 %copy-done.3 = bf16[1024,2048]{1,0:T(8,128)(2,1)} copy-done((bf16[1024,2048]{1,0:T(8,128)(2,1)}, bf16[1024,2048]{1,0:T(8,128)(2,1)S(1)}, u32[]{:S(2)}) %copy-start.3) | copy-done | bytes 4194328
  26.8 1.6 %shard_map.79.refs_1_.refs_2_ = bf16[512,2048]{1,0:T(8,128)(2,1)S(1)} custom-call(bf16[1024,2048]{1,0:T(8,128)(2,1)} %weight_ref.5), custom_call_target="tpu_custom_call" | custom-call | bytes 2097152 | tf_op jit(solution)/shard_map/pallas_call | solution.py:92
  28.4 1.6 %shard_map.78.refs_0_.refs_1_ = bf16[512,2048]{1,0:T(8,128)(2,1)S(1)} custom-call(bf16[1024,2048]{1,0:T(8,128)(2,1)} %weight_ref.5), custom_call_target="tpu_custom_call" | custom-call | bytes 2097152 | tf_op jit(solution)/shard_map/pallas_call | solution.py:92
  30.0 1.3 %copy-done = bf16[512,2048]{1,0:T(8,128)(2,1)} copy-done((bf16[512,2048]{1,0:T(8,128)(2,1)}, bf16[512,2048]{1,0:T(8,128)(2,1)S(1)}, u32[]{:S(2)}) %copy-start) | copy-done | bytes 2097176
  31.5 1.6 %copy-done.1 = bf16[512,2048]{1,0:T(8,128)(2,1)S(1)} copy-done((bf16[512,2048]{1,0:T(8,128)(2,1)S(1)}, bf16[512,2048]{1,0:T(8,128)(2,1)}, u32[]{:S(2)}) %copy-start.1) | copy-done | bytes 2097176
  33.1 0.8 %shard_map.80 = (f32[32,2048]{1,0:T(8,128)S(1)}, f32[32,2048]{1,0:T(8,128)S(1)}) custom-call(bf16[64,4096]{1,0:T(8,128)(2,1)S(1)} %get-tuple-element.16.feats_ref.rows_ref, bf16[512,2048]{1,0:T(8,128)(2,1)S(1)} %copy-done.1, bf16[512,2048]{1,0:T(8,128)(2,1)S(1)} %shard_map.79.refs_1_.refs_2_), custom_call_target="tpu_custom_call" | custom-call | flops 268435456 | bytes 1048576 | tf_op jit(solution)/shard_map/pallas_call | solution.py:188
  34.4 1.2 %collective-permute-start.7 = (bf16[32,2048]{1,0:T(8,128)(2,1)S(1)}, bf16[32,2048]{1,0:T(8,128)(2,1)S(1)}, u32[]{:S(2)}, u32[]{:S(2)}) collective-permute-start(bf16[32,2048]{1,0:T(8,128)(2,1)S(1)} %add_convert_fusion.1), channel_id=1, source_target_pairs={{0,3},{1,2},{2,1},{3,0},{4,7},{5,6},{6,5},{7,4},{8,11},{9,10},{10,... | collective-permute-start | bytes 393224 | tf_op jit(solution)/shard_map/ppermute | solution.py:23
  35.7 1.4 %collective-permute-start.9 = (bf16[32,2048]{1,0:T(8,128)(2,1)S(1)}, bf16[32,2048]{1,0:T(8,128)(2,1)S(1)}, u32[]{:S(2)}, u32[]{:S(2)}) collective-permute-start(bf16[32,2048]{1,0:T(8,128)(2,1)S(1)} %add_convert_fusion), channel_id=1, source_target_pairs={{0,3},{1,2},{2,1},{3,0},{4,7},{5,6},{6,5},{7,4},{8,11},{9,10},{10,... | collective-permute-start | bytes 393224 | tf_op jit(solution)/shard_map/ppermute | solution.py:23
  37.1 2.9 %collective-permute-done.7 = bf16[32,2048]{1,0:T(8,128)(2,1)S(1)} collective-permute-done((bf16[32,2048]{1,0:T(8,128)(2,1)S(1)}, bf16[32,2048]{1,0:T(8,128)(2,1)S(1)}, u32[]{:S(2)}, u32[]{:S(2)}) %collective-permute-start.7) | collective-permute-done | bytes 131104 | tf_op jit(solution)/shard_map/ppermute | solution.py:23
  40.2 0.8 %collective-permute-start.11 = (bf16[32,2048]{1,0:T(8,128)(2,1)S(1)}, bf16[32,2048]{1,0:T(8,128)(2,1)S(1)}, u32[]{:S(2)}, u32[]{:S(2)}) collective-permute-start(bf16[32,2048]{1,0:T(8,128)(2,1)S(1)} %get-tuple-element.21), channel_id=1, source_target_pairs={{0,1},{1,0},{2,3},{3,2},{4,5},{5,4},{6,7},{7,6},{8,9},{9,8},{10,11... | collective-permute-start | bytes 393224 | tf_op jit(solution)/shard_map/ppermute | solution.py:23
  40.9 1.9 %collective-permute-done.9 = bf16[32,2048]{1,0:T(8,128)(2,1)S(1)} collective-permute-done((bf16[32,2048]{1,0:T(8,128)(2,1)S(1)}, bf16[32,2048]{1,0:T(8,128)(2,1)S(1)}, u32[]{:S(2)}, u32[]{:S(2)}) %collective-permute-start.9) | collective-permute-done | bytes 131104 | tf_op jit(solution)/shard_map/ppermute | solution.py:23
  43.1 1.4 %shard_map.82.refs_2_ = f32[64,1024]{1,0:T(8,128)S(1)} custom-call(bf16[64,2048]{1,0:T(8,128)(2,1)S(1)} %constant_dynamic-update-slice_fusion.refs_0_.grad_ref, bf16[512,2048]{1,0:T(8,128)(2,1)S(1)} %copy-done.2, bf16[512,2048]{1,0:T(8,128)(2,1)S(1)} %shard_map.79.refs_1_.refs_2_), custom_call_target="tpu_custom_call" | custom-call | flops 268435456 | bytes 1048576 | tf_op jit(solution)/shard_map/pallas_call | solution.py:213
  44.6 1.4 %shard_map.83 = f32[64,1024]{1,0:T(8,128)S(1)} custom-call(bf16[64,2048]{1,0:T(8,128)(2,1)S(1)} %pad_maximum_fusion.1.refs_0_.grad_ref, bf16[1024,2048]{1,0:T(8,128)(2,1)S(1)} %copy-done.4, f32[64,1024]{1,0:T(8,128)S(1)} %shard_map.82.refs_2_), custom_call_target="tpu_custom_call" | custom-call | flops 268435456 | bytes 1048576 | tf_op jit(solution)/shard_map/pallas_call | solution.py:213
  46.1 1.6 %collective-permute-start.12 = (f32[2,2,4,2,1024]{4,3,2,1,0:T(2,128)S(1)}, f32[2,2,4,2,1024]{4,3,2,1,0:T(2,128)S(1)}, u32[]{:S(2)}, u32[]{:S(2)}) collective-permute-start(f32[2,2,4,2,1024]{4,3,2,1,0:T(2,128)S(1)} %slice_bitcast_fusion), channel_id=1, source_target_pairs={{0,4},{1,5},{2,6},{3,7},{4,0},{5,1},{6,2},{7,3},{8,12},{9,13},{10,... | collective-permute-start | bytes 393224 | tf_op jit(solution)/shard_map/ppermute | solution.py:23
  48.5 3.5 %collective-permute-done.12 = f32[2,2,4,2,1024]{4,3,2,1,0:T(2,128)S(1)} collective-permute-done((f32[2,2,4,2,1024]{4,3,2,1,0:T(2,128)S(1)}, f32[2,2,4,2,1024]{4,3,2,1,0:T(2,128)S(1)}, u32[]{:S(2)}, u32[]{:S(2)}) %collective-permute-start.12) | collective-permute-done | bytes 131104 | tf_op jit(solution)/shard_map/ppermute | solution.py:23
  52.1 1.6 %collective-permute-start.13 = (f32[2,2,2,2,1024]{4,3,2,1,0:T(2,128)S(1)}, f32[2,2,2,2,1024]{4,3,2,1,0:T(2,128)S(1)}, u32[]{:S(2)}, u32[]{:S(2)}) collective-permute-start(f32[2,2,2,2,1024]{4,3,2,1,0:T(2,128)S(1)} %slice_bitcast_fusion.2), channel_id=1, source_target_pairs={{0,8},{1,9},{2,10},{3,11},{4,12},{5,13},{6,14},{7,15},{8,0},{9,1},... | collective-permute-start | bytes 196616 | tf_op jit(solution)/shard_map/ppermute | solution.py:23
  53.7 4.0 %shard_map.84.rest_0_ = bf16[4096,2048]{1,0:T(8,128)(2,1)} custom-call(bf16[64,4096]{1,0:T(8,128)(2,1)S(1)} %get-tuple-element.16.feats_ref.rows_ref, bf16[64,2048]{1,0:T(8,128)(2,1)S(1)} %pad_maximum_fusion.1.refs_0_.grad_ref), custom_call_target="tpu_custom_call" | custom-call | flops 536870912 | bytes 9175040 | tf_op jit(solution)/shard_map/pallas_call | solution.py:254
  57.7 4.0 %shard_map.86.rest_0_ = bf16[4096,2048]{1,0:T(8,128)(2,1)} custom-call(bf16[64,4096]{1,0:T(8,128)(2,1)S(1)} %get-tuple-element.16.feats_ref.rows_ref, bf16[64,2048]{1,0:T(8,128)(2,1)S(1)} %constant_dynamic-update-slice_fusion.refs_0_.grad_ref), custom_call_target="tpu_custom_call" | custom-call | flops 536870912 | bytes 9175040 | tf_op jit(solution)/shard_map/pallas_call | solution.py:254
  61.7 3.1 %collective-permute-start.14 = (f32[2,2,1,2,1024]{4,3,1,0,2:T(2,128)S(1)}, f32[2,2,1,2,1024]{4,3,1,0,2:T(2,128)S(1)}, u32[]{:S(2)}, u32[]{:S(2)}) collective-permute-start(f32[2,2,1,2,1024]{4,3,1,0,2:T(2,128)S(1)} %slice_bitcast_fusion.4), channel_id=1, source_target_pairs={{0,16},{1,17},{2,18},{3,19},{4,20},{5,21},{6,22},{7,23},{8,24},{9,... | collective-permute-start | bytes 98312 | tf_op jit(solution)/shard_map/ppermute | solution.py:23
  64.8 4.0 %shard_map.85 = bf16[4096,2048]{1,0:T(8,128)(2,1)} custom-call(bf16[64,4096]{1,0:T(8,128)(2,1)S(1)} %get-tuple-element.16.feats_ref.rows_ref, bf16[64,2048]{1,0:T(8,128)(2,1)S(1)} %pad_maximum_fusion.1.refs_0_.grad_ref, bf16[4096,2048]{1,0:T(8,128)(2,1)} %shard_map.84.rest_0_), custom_call_target="tpu_custom_call", output_to_operand_aliasing={{}: (2, {})} | custom-call | flops 536870912 | bytes 9175040 | tf_op jit(solution)/shard_map/pallas_call | solution.py:254
  68.9 1.5 %collective-permute-start.16 = (bf16[2,1024]{1,0:T(2,128)(2,1)S(1)}, bf16[2,1024]{1,0:T(2,128)(2,1)S(1)}, u32[]{:S(2)}, u32[]{:S(2)}) collective-permute-start(bf16[2,1024]{1,0:T(2,128)(2,1)S(1)} %get-tuple-element.38), channel_id=1, source_target_pairs={{0,2},{1,3},{2,0},{3,1},{4,6},{5,7},{6,4},{7,5},{8,10},{9,11},{10,... | collective-permute-start | bytes 12296 | tf_op jit(solution)/shard_map/ppermute | solution.py:23
  70.8 4.0 %shard_map.87 = bf16[4096,2048]{1,0:T(8,128)(2,1)} custom-call(bf16[64,4096]{1,0:T(8,128)(2,1)S(1)} %get-tuple-element.16.feats_ref.rows_ref, bf16[64,2048]{1,0:T(8,128)(2,1)S(1)} %constant_dynamic-update-slice_fusion.refs_0_.grad_ref, bf16[4096,2048]{1,0:T(8,128)(2,1)} %shard_map.86.rest_0_), custom_call_target="tpu_custom_call", output_to_operand_aliasing={{}: (2, {})} | custom-call | flops 536870912 | bytes 9175040 | tf_op jit(solution)/shard_map/pallas_call | solution.py:254
  (58 shorter events, 5.5 us)
Async XLA Ops:
  0.6 5.2 %collective-permute-start.1 = (bf16[1,2,4096]{2,1,0:T(2,128)(2,1)}, bf16[1,2,4096]{2,1,0:T(2,128)(2,1)S(1)}, u32[]{:S(2)}, u32[]{:S(2)}) collective-permute-start(bf16[1,2,4096]{2,1,0:T(2,128)(2,1)} %in_ref.1), channel_id=1, source_target_pairs={{0,17},{1,16},{2,19},{3,18},{4,21},{5,20},{6,23},{7,22},{8,25},{9,... | collective-permute-start | bytes 49160 | tf_op jit(solution)/shard_map/ppermute | solution.py:23
  4.2 0.8 copy-start.5
  5.9 3.6 %collective-permute-start.2 = (bf16[2,2,4096]{2,1,0:T(2,128)(2,1)S(1)}, bf16[2,2,4096]{2,1,0:T(2,128)(2,1)S(1)}, u32[]{:S(2)}, u32[]{:S(2)}) collective-permute-start(bf16[2,2,4096]{2,1,0:T(2,128)(2,1)S(1)} %get-tuple-element.32), channel_id=1, source_target_pairs={{0,9},{1,8},{2,11},{3,10},{4,13},{5,12},{6,15},{7,14},{8,1},{9,0},... | collective-permute-start | bytes 98312 | tf_op jit(solution)/shard_map/ppermute | solution.py:23
  9.6 4.0 %collective-permute-start.3 = (bf16[4,2,4096]{2,1,0:T(2,128)(2,1)S(1)}, bf16[4,2,4096]{2,1,0:T(2,128)(2,1)S(1)}, u32[]{:S(2)}, u32[]{:S(2)}) collective-permute-start(bf16[4,2,4096]{2,1,0:T(2,128)(2,1)S(1)} %bitcast.77), channel_id=1, source_target_pairs={{0,5},{1,4},{2,7},{3,6},{4,1},{5,0},{6,3},{7,2},{8,13},{9,12},{10,... | collective-permute-start | bytes 196616 | tf_op jit(solution)/shard_map/ppermute | solution.py:23
  13.9 5.5 %collective-permute-start.4 = (bf16[8,2,4096]{2,1,0:T(2,128)(2,1)S(1)}, bf16[8,2,4096]{2,1,0:T(2,128)(2,1)S(1)}, u32[]{:S(2)}, u32[]{:S(2)}) collective-permute-start(bf16[8,2,4096]{2,1,0:T(2,128)(2,1)S(1)} %bitcast.75), channel_id=1, source_target_pairs={{0,3},{1,2},{2,1},{3,0},{4,7},{5,6},{6,5},{7,4},{8,11},{9,10},{10,... | collective-permute-start | bytes 393224 | tf_op jit(solution)/shard_map/ppermute | solution.py:23
  19.8 2.4 %collective-permute-start.5 = (bf16[2,8,2,4096]{3,2,1,0:T(2,128)(2,1)S(1)}, bf16[2,8,2,4096]{3,2,1,0:T(2,128)(2,1)S(1)}, u32[]{:S(2)}, u32[]{:S(2)}) collective-permute-start(bf16[2,8,2,4096]{3,2,1,0:T(2,128)(2,1)S(1)} %pad_maximum_fusion.part_ref), channel_id=1, source_target_pairs={{0,1},{1,0},{2,3},{3,2},{4,5},{5,4},{6,7},{7,6},{8,9},{9,8},{10,11... | collective-permute-start | bytes 786440 | tf_op jit(solution)/shard_map/ppermute | solution.py:23
  20.2 11.2 %collective-permute-start = (bf16[16,2048]{1,0:T(8,128)(2,1)}, bf16[16,2048]{1,0:T(8,128)(2,1)S(1)}, u32[]{:S(2)}, u32[]{:S(2)}) collective-permute-start(bf16[16,2048]{1,0:T(8,128)(2,1)} %bitcast.81), channel_id=1, source_target_pairs={{0,3},{1,2},{2,1},{3,0},{4,7},{5,6},{6,5},{7,4},{8,11},{9,10},{10,... | collective-permute-start | bytes 196616 | tf_op jit(solution)/shard_map/ppermute | solution.py:23
  24.7 2.0 %copy-start.3 = (bf16[1024,2048]{1,0:T(8,128)(2,1)}, bf16[1024,2048]{1,0:T(8,128)(2,1)S(1)}, u32[]{:S(2)}) copy-start(bf16[1024,2048]{1,0:T(8,128)(2,1)S(1)} %get-tuple-element.20.refs_1_) | copy-start | bytes 12582916
  26.7 7.7 %collective-permute-start.6 = (f32[32,2048]{1,0:T(8,128)S(1)}, f32[32,2048]{1,0:T(8,128)S(1)}, u32[]{:S(2)}, u32[]{:S(2)}) collective-permute-start(f32[32,2048]{1,0:T(8,128)S(1)} %get-tuple-element.14), channel_id=1, source_target_pairs={{0,1},{1,0},{2,3},{3,2},{4,5},{5,4},{6,7},{7,6},{8,9},{9,8},{10,11... | collective-permute-start | bytes 786440 | tf_op jit(solution)/shard_map/ppermute | solution.py:23
  28.4 2.9 %copy-start.6 = (bf16[1,16,2048]{2,1,0:T(8,128)(2,1)S(1)}, bf16[1,16,2048]{2,1,0:T(8,128)(2,1)}, u32[]{:S(2)}) copy-start(bf16[1,16,2048]{2,1,0:T(8,128)(2,1)} %param.7) | copy-start | bytes 196612
  30.0 1.3 %copy-start = (bf16[512,2048]{1,0:T(8,128)(2,1)}, bf16[512,2048]{1,0:T(8,128)(2,1)S(1)}, u32[]{:S(2)}) copy-start(bf16[512,2048]{1,0:T(8,128)(2,1)S(1)} %shard_map.78.refs_0_.refs_1_) | copy-start | bytes 6291460
  31.5 1.6 %copy-start.1 = (bf16[512,2048]{1,0:T(8,128)(2,1)S(1)}, bf16[512,2048]{1,0:T(8,128)(2,1)}, u32[]{:S(2)}) copy-start(bf16[512,2048]{1,0:T(8,128)(2,1)} %copy-done) | copy-start | bytes 6291460
  33.1 10.0 %copy-start.2 = (bf16[512,2048]{1,0:T(8,128)(2,1)S(1)}, bf16[512,2048]{1,0:T(8,128)(2,1)}, u32[]{:S(2)}) copy-start(bf16[512,2048]{1,0:T(8,128)(2,1)} %copy-done) | copy-start | bytes 6291460
  33.9 1.7 %collective-permute-start.8 = (f32[32,2048]{1,0:T(8,128)S(1)}, f32[32,2048]{1,0:T(8,128)S(1)}, u32[]{:S(2)}, u32[]{:S(2)}) collective-permute-start(f32[32,2048]{1,0:T(8,128)S(1)} %get-tuple-element.18), channel_id=1, source_target_pairs={{0,1},{1,0},{2,3},{3,2},{4,5},{5,4},{6,7},{7,6},{8,9},{9,8},{10,11... | collective-permute-start | bytes 786440 | tf_op jit(solution)/shard_map/ppermute | solution.py:23
  34.4 5.6 %collective-permute-start.7 = (bf16[32,2048]{1,0:T(8,128)(2,1)S(1)}, bf16[32,2048]{1,0:T(8,128)(2,1)S(1)}, u32[]{:S(2)}, u32[]{:S(2)}) collective-permute-start(bf16[32,2048]{1,0:T(8,128)(2,1)S(1)} %add_convert_fusion.1), channel_id=1, source_target_pairs={{0,3},{1,2},{2,1},{3,0},{4,7},{5,6},{6,5},{7,4},{8,11},{9,10},{10,... | collective-permute-start | bytes 393224 | tf_op jit(solution)/shard_map/ppermute | solution.py:23
  35.7 8.9 %copy-start.4 = (bf16[1024,2048]{1,0:T(8,128)(2,1)S(1)}, bf16[1024,2048]{1,0:T(8,128)(2,1)}, u32[]{:S(2)}) copy-start(bf16[1024,2048]{1,0:T(8,128)(2,1)} %copy-done.3) | copy-start | bytes 12582916
  35.7 7.1 %collective-permute-start.9 = (bf16[32,2048]{1,0:T(8,128)(2,1)S(1)}, bf16[32,2048]{1,0:T(8,128)(2,1)S(1)}, u32[]{:S(2)}, u32[]{:S(2)}) collective-permute-start(bf16[32,2048]{1,0:T(8,128)(2,1)S(1)} %add_convert_fusion), channel_id=1, source_target_pairs={{0,3},{1,2},{2,1},{3,0},{4,7},{5,6},{6,5},{7,4},{8,11},{9,10},{10,... | collective-permute-start | bytes 393224 | tf_op jit(solution)/shard_map/ppermute | solution.py:23
  40.2 2.9 %collective-permute-start.11 = (bf16[32,2048]{1,0:T(8,128)(2,1)S(1)}, bf16[32,2048]{1,0:T(8,128)(2,1)S(1)}, u32[]{:S(2)}, u32[]{:S(2)}) collective-permute-start(bf16[32,2048]{1,0:T(8,128)(2,1)S(1)} %get-tuple-element.21), channel_id=1, source_target_pairs={{0,1},{1,0},{2,3},{3,2},{4,5},{5,4},{6,7},{7,6},{8,9},{9,8},{10,11... | collective-permute-start | bytes 393224 | tf_op jit(solution)/shard_map/ppermute | solution.py:23
  42.9 1.6 %collective-permute-start.10 = (bf16[32,2048]{1,0:T(8,128)(2,1)S(1)}, bf16[32,2048]{1,0:T(8,128)(2,1)S(1)}, u32[]{:S(2)}, u32[]{:S(2)}) collective-permute-start(bf16[32,2048]{1,0:T(8,128)(2,1)S(1)} %get-tuple-element.24), channel_id=1, source_target_pairs={{0,1},{1,0},{2,3},{3,2},{4,5},{5,4},{6,7},{7,6},{8,9},{9,8},{10,11... | collective-permute-start | bytes 393224 | tf_op jit(solution)/shard_map/ppermute | solution.py:23
  46.1 5.9 %collective-permute-start.12 = (f32[2,2,4,2,1024]{4,3,2,1,0:T(2,128)S(1)}, f32[2,2,4,2,1024]{4,3,2,1,0:T(2,128)S(1)}, u32[]{:S(2)}, u32[]{:S(2)}) collective-permute-start(f32[2,2,4,2,1024]{4,3,2,1,0:T(2,128)S(1)} %slice_bitcast_fusion), channel_id=1, source_target_pairs={{0,4},{1,5},{2,6},{3,7},{4,0},{5,1},{6,2},{7,3},{8,12},{9,13},{10,... | collective-permute-start | bytes 393224 | tf_op jit(solution)/shard_map/ppermute | solution.py:23
  52.1 9.6 %collective-permute-start.13 = (f32[2,2,2,2,1024]{4,3,2,1,0:T(2,128)S(1)}, f32[2,2,2,2,1024]{4,3,2,1,0:T(2,128)S(1)}, u32[]{:S(2)}, u32[]{:S(2)}) collective-permute-start(f32[2,2,2,2,1024]{4,3,2,1,0:T(2,128)S(1)} %slice_bitcast_fusion.2), channel_id=1, source_target_pairs={{0,8},{1,9},{2,10},{3,11},{4,12},{5,13},{6,14},{7,15},{8,0},{9,1},... | collective-permute-start | bytes 196616 | tf_op jit(solution)/shard_map/ppermute | solution.py:23
  61.7 7.0 %collective-permute-start.14 = (f32[2,2,1,2,1024]{4,3,1,0,2:T(2,128)S(1)}, f32[2,2,1,2,1024]{4,3,1,0,2:T(2,128)S(1)}, u32[]{:S(2)}, u32[]{:S(2)}) collective-permute-start(f32[2,2,1,2,1024]{4,3,1,0,2:T(2,128)S(1)} %slice_bitcast_fusion.4), channel_id=1, source_target_pairs={{0,16},{1,17},{2,18},{3,19},{4,20},{5,21},{6,22},{7,23},{8,24},{9,... | collective-permute-start | bytes 98312 | tf_op jit(solution)/shard_map/ppermute | solution.py:23
  68.8 5.9 %collective-permute-start.17 = (bf16[2,1024]{1,0:T(2,128)(2,1)S(1)}, bf16[2,1024]{1,0:T(2,128)(2,1)S(1)}, u32[]{:S(2)}, u32[]{:S(2)}) collective-permute-start(bf16[2,1024]{1,0:T(2,128)(2,1)S(1)} %get-tuple-element.37), channel_id=1, source_target_pairs={{0,1},{1,0},{2,3},{3,2},{4,5},{5,4},{6,7},{7,6},{8,9},{9,8},{10,11... | collective-permute-start | bytes 12296 | tf_op jit(solution)/shard_map/ppermute | solution.py:23
  68.9 5.8 %collective-permute-start.16 = (bf16[2,1024]{1,0:T(2,128)(2,1)S(1)}, bf16[2,1024]{1,0:T(2,128)(2,1)S(1)}, u32[]{:S(2)}, u32[]{:S(2)}) collective-permute-start(bf16[2,1024]{1,0:T(2,128)(2,1)S(1)} %get-tuple-element.38), channel_id=1, source_target_pairs={{0,2},{1,3},{2,0},{3,1},{4,6},{5,7},{6,4},{7,5},{8,10},{9,11},{10,... | collective-permute-start | bytes 12296 | tf_op jit(solution)/shard_map/ppermute | solution.py:23
  70.4 4.4 %collective-permute-start.15 = (bf16[2,1024]{1,0:T(2,128)(2,1)S(1)}, bf16[2,1024]{1,0:T(2,128)(2,1)S(1)}, u32[]{:S(2)}, u32[]{:S(2)}) collective-permute-start(bf16[2,1024]{1,0:T(2,128)(2,1)S(1)} %get-tuple-element.39), channel_id=1, source_target_pairs={{0,3},{1,2},{2,1},{3,0},{4,7},{5,6},{6,5},{7,4},{8,11},{9,10},{10,... | collective-permute-start | bytes 12296 | tf_op jit(solution)/shard_map/ppermute | solution.py:23
